TPU v7x, 32 devices: a whole 2x2x4 slice. The times are simulated.
32 devices in a mesh: rep: 2 (over core), shard: 16 (over z, y, x).
Axes of the slice: x: 2, y: 2, z: 4, core: 2. Of those that a mesh axis runs over, the one named last changes fastest.
Arguments:
- hidden_states: bfloat16 [4096, 768], P(('rep', 'shard')), may hold values from -40 to 40
- cotangent: bfloat16 [4096, 768], P(('rep', 'shard')), may hold values from -6 to 6
- lengths: int32 [32], P(('rep', 'shard')), may hold values from 32 to 128, as said below
- params: float32 [7087104], P('shard'), may hold values from -4 to 4
- first_moment: float32 [7087104], P('shard'), may hold values from -12 to 12
- second_moment: float32 [7087104], P('shard'), may hold values from 1 to 100
Outputs:
- block_output: bfloat16 [4096, 768], P(('rep', 'shard'))
- input_grad: bfloat16 [4096, 768], P(('rep', 'shard'))
- weight_grad: float32 [7087104], P('shard')
- new_params: float32 [7087104], P('shard')
- new_first: float32 [7087104], P('shard')
- new_second: float32 [7087104], P('shard')
Inputs may be any that keep to these rules, and one draw needn't show every extreme that they name: `lengths`: at least one sequence is entirely valid.
All inputs are finite; a program needn't handle non-finite values.
Results may differ from a plain program's by a relative error of at most 0.013.
The roundings to bfloat16 on the way count: a program that leaves them out, or rounds other values in their place, can miss the bound.
Values may be sent and summed in bfloat16 or wider, within the bound.
No kernel may reach another device: no remote copies, remote signals or barrier semaphores. Data moves between devices by JAX's collectives and lax.ppermute only.
A program may use at most 192 MiB of HBM per device.

v0:
```python
import math

import jax
import jax.numpy as jnp
from jax import lax
from jax.sharding import PartitionSpec as P

D = 768
HEADS = 12
HEAD = 64
FF = 3072
STEP = 3
HW = 768


norm_eps = 1e-05
adam_eps = 1e-06
beta_one = 0.9
beta_two = 0.98
learn_rate = 0.01
decay_rate = 0.01
masked_score = -1e30
inv_sqrt_two = 1.0 / math.sqrt(2.0)
inv_sqrt_tau = 1.0 / math.sqrt(2.0 * math.pi)


def layout():
    return [
        ("triple_weight", (D, 3 * HW)),
        ("output_weight", (HW, D)),
        ("expand_weight", (D, FF)),
        ("reduce_weight", (FF, D)),
        ("query_bias", (HW,)),
        ("value_bias", (HW,)),
        ("output_bias", (D,)),
        ("first_gain", (D,)),
        ("first_shift", (D,)),
        ("expand_bias", (FF,)),
        ("reduce_bias", (D,)),
        ("second_gain", (D,)),
        ("second_shift", (D,)),
    ]


def split_flat(flat_vector):
    pieces = {}
    offset = 0
    for entry_name, dims_of in layout():
        amount = math.prod(dims_of)
        pieces[entry_name] = flat_vector[offset : offset + amount].reshape(dims_of)
        offset = offset + amount
    return pieces


def inner_rows(left_side, right_side):
    return lax.dot_general(
        left_side, right_side, (((0,), (0,)), ((), ())), preferred_element_type=jnp.float32
    )


def by_transpose(left_side, right_side):
    return lax.dot_general(
        left_side, right_side, (((1,), (1,)), ((), ())), preferred_element_type=jnp.float32
    )


def heads_of(row_block):
    return row_block.reshape(row_block.shape[0], HEADS, HEAD)


def normalize(values_in):
    centered = values_in - jnp.mean(values_in, axis=-1, keepdims=True)
    inv_root = lax.rsqrt(jnp.mean(centered * centered, axis=-1, keepdims=True) + norm_eps)
    return (centered * inv_root, inv_root)


def norm_back(grad_in, normed, inv_root):
    return inv_root * (
        grad_in
        - jnp.mean(grad_in, axis=-1, keepdims=True)
        - normed * jnp.mean(grad_in * normed, axis=-1, keepdims=True)
    )


def gelu_slope(pre_act):
    return (
        0.5 * (1.0 + lax.erf(pre_act * inv_sqrt_two))
        + pre_act * jnp.exp(-0.5 * pre_act * pre_act) * inv_sqrt_tau
    )


def attention_scores(queries, key_rows, length):
    scores = jnp.einsum(
        "qhd,khd->hqk", heads_of(queries), heads_of(key_rows), preferred_element_type=jnp.float32
    ) * (1.0 / math.sqrt(HEAD))
    key_valid = jnp.arange(scores.shape[-1]) < length
    return jnp.where(key_valid, scores, masked_score)


def forward(tokens, length, prm):
    rows = tokens.shape[0]
    triple = jnp.dot(tokens, prm["triple_weight"], preferred_element_type=jnp.float32)
    queries = (triple[:, :HW] + prm["query_bias"].astype(jnp.float32)).astype(jnp.bfloat16)
    key_rows = triple[:, HW : 2 * HW].astype(jnp.bfloat16)
    value_rows = (triple[:, 2 * HW :] + prm["value_bias"].astype(jnp.float32)).astype(jnp.bfloat16)
    scores = attention_scores(queries, key_rows, length)
    top_score = jnp.max(scores, axis=-1, keepdims=True)
    log_total = top_score + jnp.log(jnp.sum(jnp.exp(scores - top_score), axis=-1, keepdims=True))
    soft_weights = jnp.exp(scores - log_total).astype(jnp.bfloat16)
    context = jnp.einsum(
        "hqk,khd->qhd", soft_weights, heads_of(value_rows), preferred_element_type=jnp.float32
    )
    context = context.reshape(rows, HW).astype(jnp.bfloat16)
    first_sum = (
        tokens.astype(jnp.float32)
        + jnp.dot(context, prm["output_weight"], preferred_element_type=jnp.float32)
        + prm["output_bias"].astype(jnp.float32)
    )
    normed_one, root_one = normalize(first_sum)
    middle = normed_one * prm["first_gain"].astype(jnp.float32) + prm["first_shift"].astype(
        jnp.float32
    )
    middle_b = middle.astype(jnp.bfloat16)
    pre_act = jnp.dot(middle_b, prm["expand_weight"], preferred_element_type=jnp.float32) + prm[
        "expand_bias"
    ].astype(jnp.float32)
    activated = (0.5 * pre_act * (1.0 + lax.erf(pre_act * inv_sqrt_two))).astype(jnp.bfloat16)
    second_sum = (
        middle
        + jnp.dot(activated, prm["reduce_weight"], preferred_element_type=jnp.float32)
        + prm["reduce_bias"].astype(jnp.float32)
    )
    normed_two, root_two = normalize(second_sum)
    block_out = (
        normed_two * prm["second_gain"].astype(jnp.float32)
        + prm["second_shift"].astype(jnp.float32)
    ).astype(jnp.bfloat16)
    kept = (
        queries,
        key_rows,
        value_rows,
        log_total,
        context,
        normed_one,
        root_one,
        middle_b,
        pre_act,
        activated,
        normed_two,
        root_two,
    )
    return (block_out, kept)


def backward(tokens, length, cotangent, kept, prm):
    (
        queries,
        key_rows,
        value_rows,
        log_total,
        context,
        normed_one,
        root_one,
        middle_b,
        pre_act,
        activated,
        normed_two,
        root_two,
    ) = kept
    rows = tokens.shape[0]
    grad_out = cotangent.astype(jnp.float32)
    d_second = norm_back(grad_out * prm["second_gain"].astype(jnp.float32), normed_two, root_two)
    d_second_b = d_second.astype(jnp.bfloat16)
    d_pre = by_transpose(d_second_b, prm["reduce_weight"]) * gelu_slope(pre_act)
    d_pre_b = d_pre.astype(jnp.bfloat16)
    d_middle = d_second + by_transpose(d_pre_b, prm["expand_weight"])
    d_first = norm_back(d_middle * prm["first_gain"].astype(jnp.float32), normed_one, root_one)
    d_first_b = d_first.astype(jnp.bfloat16)
    d_context = by_transpose(d_first_b, prm["output_weight"]).astype(jnp.bfloat16)
    scores = attention_scores(queries, key_rows, length)
    soft_float = jnp.exp(scores - log_total)
    soft_weights = soft_float.astype(jnp.bfloat16)
    d_soft = jnp.einsum(
        "qhd,khd->hqk",
        heads_of(d_context),
        heads_of(value_rows),
        preferred_element_type=jnp.float32,
    )
    delta = jnp.sum(d_soft * soft_float, axis=-1, keepdims=True)
    d_scores = (soft_float * (d_soft - delta) * (1.0 / math.sqrt(HEAD))).astype(jnp.bfloat16)
    d_query = jnp.einsum(
        "hqk,khd->qhd", d_scores, heads_of(key_rows), preferred_element_type=jnp.float32
    ).reshape(rows, HW)
    d_keys = jnp.einsum(
        "hqk,qhd->khd", d_scores, heads_of(queries), preferred_element_type=jnp.float32
    ).reshape(rows, HW)
    d_values = jnp.einsum(
        "hqk,qhd->khd", soft_weights, heads_of(d_context), preferred_element_type=jnp.float32
    ).reshape(rows, HW)
    d_triple = jnp.concatenate([d_query, d_keys, d_values], axis=1).astype(jnp.bfloat16)
    input_grad = (d_first + by_transpose(d_triple, prm["triple_weight"])).astype(jnp.bfloat16)
    grad_list = [
        inner_rows(tokens, d_triple),
        inner_rows(context, d_first_b),
        inner_rows(middle_b, d_pre_b),
        inner_rows(activated, d_second_b),
        jnp.sum(d_query, axis=0),
        jnp.sum(d_values, axis=0),
        jnp.sum(d_first, axis=0),
        jnp.sum(d_middle * normed_one, axis=0),
        jnp.sum(d_middle, axis=0),
        jnp.sum(d_pre, axis=0),
        jnp.sum(d_second, axis=0),
        jnp.sum(grad_out * normed_two, axis=0),
        jnp.sum(grad_out, axis=0),
    ]
    flat_grad = jnp.concatenate([piece_grad.reshape(-1) for piece_grad in grad_list])
    return (input_grad, flat_grad)


def adamw(param_now, first_now, second_now, grad_total):
    first_new = beta_one * first_now + (1.0 - beta_one) * grad_total
    second_new = beta_two * second_now + (1.0 - beta_two) * grad_total * grad_total
    fix_one = 1.0 - beta_one**STEP
    fix_two = 1.0 - beta_two**STEP
    param_new = param_now - learn_rate * (
        first_new / fix_one / (jnp.sqrt(second_new / fix_two) + adam_eps) + decay_rate * param_now
    )
    return (param_new, first_new, second_new)


def on_device(hidden_states, cotangent, lengths, params, first_moment, second_moment):
    length = lengths[0]
    shard_b = params.astype(jnp.bfloat16)
    gathered = lax.all_gather(shard_b, "shard", axis=0, tiled=True)
    prm = split_flat(gathered)
    block_out, kept = forward(hidden_states, length, prm)
    gathered_again = lax.all_gather(shard_b, "shard", axis=0, tiled=True)
    prm_back = split_flat(gathered_again)
    input_grad, flat_grad = backward(hidden_states, length, cotangent, kept, prm_back)
    owned = lax.psum_scatter(flat_grad, "shard", scatter_dimension=0, tiled=True)
    weight_grad = lax.psum(owned, "rep")
    new_params, new_first, new_second = adamw(params, first_moment, second_moment, weight_grad)
    return (block_out, input_grad, weight_grad, new_params, new_first, new_second)


def solution(mesh):
    placed = (
        P(("rep", "shard"), None),
        P(("rep", "shard"), None),
        P(("rep", "shard")),
        P("shard"),
        P("shard"),
        P("shard"),
    )
    return jax.shard_map(
        on_device,
        mesh=mesh,
        in_specs=placed,
        out_specs=(
            P(("rep", "shard"), None),
            P(("rep", "shard"), None),
            P("shard"),
            P("shard"),
            P("shard"),
            P("shard"),
        ),
        check_vma=False,
    )
```

profile of v0, /device:TPU:0, one launch (start us, length us, event | category | flops | bytes accessed | tf_op | source)
XLA Modules:
  0.0 1363.3 jit_solution(6395684006548909022)
XLA Ops:
  10.1 5.3 broadcast.99
  15.4 14.6 %dynamic-update-slice = bf16[7087104]{0:T(1024)(128)(2,1)} dynamic-update-slice(bf16[7087104]{0:T(1024)(128)(2,1)} %broadcast.99, bf16[442944]{0:T(1024)(128)(2,1)S(1)} %convert_element_type.87, u32[]{:T(128)} %bitcast) | dynamic-update-slice | bytes 1771780
  30.8 399.2 %all-reduce.8.cloned.1.call-done = bf16[7087104]{0:T(1024)(128)(2,1)} async-done(((bf16[7087104]{0:T(1024)(128)(2,1)}), bf16[7087104]{0:T(1024)(128)(2,1)}) %all-reduce.8.cloned.1.call-update) | async-done | bytes 14174224
  430.0 8.3 fusion.57
  438.3 9.2 slice.111
  447.5 8.2 slice.108
  455.7 3.4 slice.115
  459.1 6.3 slice.96
  479.2 3.5 fusion.63
  507.0 5.1 convolution_bitcast_fusion.2
  512.1 5.1 fusion.42
  517.2 4.0 convolution_bitcast_fusion
  521.3 8.0 copy.29
  529.3 7.9 reshape.164
  537.2 5.3 constant_dynamic-update-slice_fusion.12
  544.1 9.4 copy.34
  553.5 10.9 reshape.167
  566.1 9.6 constant_dynamic-update-slice_fusion.10
  575.8 4.0 constant_dynamic-update-slice_fusion.9
  592.1 733.6 %all-reduce.10.cloned.1.call-done = f32[7087104]{0:T(1024)} async-done(((f32[7087104]{0:T(1024)}), f32[7087104]{0:T(1024)}) %all-reduce.10.cloned.1.call-update) | async-done | bytes 28348432
  1325.7 3.4 dynamic-slice.2
  1329.1 3.2 fusion.13
  1332.3 16.7 %all-reduce.6.cloned.1.call-done = f32[442944]{0:T(1024)} async-done(((f32[442944]{0:T(1024)}), f32[442944]{0:T(1024)}) %all-reduce.6.cloned.1.call-update) | async-done | bytes 1771792 | tf_op jit(solution)/shard_map/psum | solution.py:242
  1349.1 6.4 multiply_subtract_fusion
  (141 shorter events, 56.5 us)
Async XLA Ops:
  7.2 422.8 %all-reduce.8.cloned.1.call-start = ((), (), s32[]{:S(2)}) async-start(), calls=%async_computation.1 | async-start | bytes 28348416
  30.1 1295.6 %all-reduce.10.cloned.1.call-start = ((), (), s32[]{:S(2)}) async-start(), calls=%async_computation.2 | async-start | bytes 56696832
  475.1 14.9 %copy-start.20 = (f32[128]{0:T(128)}, f32[128]{0:T(128)S(1)}, u32[]{:S(2)}) copy-start(f32[128]{0:T(128)S(1)} %broadcast_multiply_fusion.5) | copy-start | bytes 1540
  475.3 14.7 %copy-start.22 = (f32[128]{0:T(128)}, f32[128]{0:T(128)S(1)}, u32[]{:S(2)}) copy-start(f32[128]{0:T(128)S(1)} %add_rsqrt_fusion.1) | copy-start | bytes 1540
  479.2 6.0 slice-start.5
  479.2 6.0 slice-start.6
  490.7 13.5 copy-start.6
  512.1 5.1 copy-start.18
  537.2 5.3 copy-start.3
  553.5 10.9 copy-start.31
  553.5 10.9 copy-start.19
  553.5 11.0 copy-start.4
  564.5 11.2 slice-start.2
  566.1 9.6 slice-start.3
  566.1 9.6 slice-start.4
  575.7 6.6 copy-start.27
  575.7 7.9 copy-start.29
  575.7 9.2 copy-start.28
  575.7 10.5 copy-start.30
  575.7 11.8 copy-start.26
  575.7 13.1 copy-start.25
  575.7 14.3 %copy-start.24 = (f32[768]{0:T(1024)S(1)}, f32[768]{0:T(1024)}, u32[]{:S(2)}) copy-start(f32[768]{0:T(1024)} %get-tuple-element.13) | copy-start | bytes 9220
  591.4 757.7 %all-reduce.6.cloned.1.call-start = ((), (), s32[]{:S(2)}) async-start(), calls=%async_computation | async-start | bytes 3547136 | tf_op jit(solution)/shard_map/psum | solution.py:242
  1349.1 6.4 copy-start.5
  (20 other events, 59.6 us)
Sparse Core Ops, SparseCore 0:
  30.2 399.7 all-reduce.7
  591.5 734.1 all-reduce.9
  1329.2 19.8 all-reduce.5
where the time goes:
time: 1370 us; the launch traced here: 1360 us
  waiting for transfers between devices  1150 us (84%)
  local copies, waits for them, and re-layouts  136 us (10%)
  matrix products  48 us (4%)
  between operations  16.1 us (1%)
    unnamed x5, waiting for transfers between devices  1130 us
    unnamed x98, local copies, waits for them, and re-layouts  66.2 us
    slice x8, local copies, waits for them, and re-layouts, split_flat(): pieces[entry_name] = flat_vector[offset:offset + amount].reshape(dims_of)  38.5 us
  transfers between devices with their start and end apart: 3, of which 3 were waited for; matrix products, arithmetic and copies ran while one was open for 0% of the time, Pallas kernels for 0%

commit v1 on v0

--- a/solution.py
+++ b/solution.py
@@ -3,6 +3,8 @@
 import jax
 import jax.numpy as jnp
 from jax import lax
+from jax.experimental import pallas as pl
+from jax.experimental.pallas import tpu as pltpu
 from jax.sharding import PartitionSpec as P
 
 D = 768
@@ -228,16 +230,441 @@
     )
     return (param_new, first_new, second_new)
 
-
-def on_device(hidden_states, cotangent, lengths, params, first_moment, second_moment):
+ROW = 768
+STEP_ROWS = 576
+FRAME = 592
+HALF = ROW // 2
+LINES = FRAME * 6
+LOCAL = 442944
+LOCAL_LINES = 3464
+ROWS = 16 * STEP_ROWS + 16
+OUT_ROW = 2304
+EXP_ROW = 3072
+RED_ROW = 6144
+BIAS_ROW = 9216
+VMEM_CAP = 64 * 1024 * 1000
+
+f32 = jnp.float32
+bf16 = jnp.bfloat16
+
+
+def swap_half(block):
+    return pltpu.roll(block, 64, 1)
+
+
+def frame_kernel(meta, flat_ref, out_ref, lines, framed):
+    shift, odd, first_col = meta[0], meta[1], meta[2]
+    lines[0:8, :] = jnp.zeros((8, 128), f32)
+    lines[8 : 8 + LOCAL_LINES, :] = flat_ref[...]
+    framed[0:96, :] = jnp.zeros((96, 128), f32)
+    framed[LINES - 96 : LINES, :] = jnp.zeros((96, 128), f32)
+    low = lax.broadcasted_iota(jnp.int32, (LOCAL_LINES, 128), 1) < 64
+    here = lines[8 : 8 + LOCAL_LINES, :]
+    before = lines[7 : 7 + LOCAL_LINES, :]
+    moved = jnp.where(low, swap_half(before), swap_half(here))
+    framed[pl.ds(shift, LOCAL_LINES), :] = jnp.where(odd == 1, moved, here)
+    for j in range(3):
+        column = framed[pl.ds(first_col + j, FRAME, stride=6), :]
+        out_ref[:, 128 * j : 128 * (j + 1)] = column.astype(bf16)
+
+
+def make_frame(params, meta):
+    flat = jnp.pad(params, (0, LOCAL_LINES * 128 - LOCAL)).reshape(LOCAL_LINES, 128)
+    return pl.pallas_call(
+        frame_kernel,
+        out_shape=jax.ShapeDtypeStruct((FRAME, HALF), bf16),
+        in_specs=[
+            pl.BlockSpec(memory_space=pltpu.SMEM),
+            pl.BlockSpec(memory_space=pltpu.VMEM),
+        ],
+        out_specs=pl.BlockSpec(memory_space=pltpu.VMEM),
+        scratch_shapes=[
+            pltpu.VMEM((LOCAL_LINES + 16, 128), f32),
+            pltpu.VMEM((LINES, 128), f32),
+        ],
+    )(meta, flat)
+
+
+def unframe_kernel(meta, mine_ref, other_ref, out_ref, framed):
+    shift, odd, first_col, other_col = meta[0], meta[1], meta[2], meta[3]
+    for j in range(3):
+        framed[pl.ds(first_col + j, FRAME, stride=6), :] = mine_ref[:, 128 * j : 128 * (j + 1)]
+        framed[pl.ds(other_col + j, FRAME, stride=6), :] = other_ref[:, 128 * j : 128 * (j + 1)]
+    low = lax.broadcasted_iota(jnp.int32, (LOCAL_LINES, 128), 1) < 64
+    here = framed[pl.ds(shift, LOCAL_LINES), :]
+    after = framed[pl.ds(shift + 1, LOCAL_LINES), :]
+    moved = jnp.where(low, swap_half(here), swap_half(after))
+    out_ref[...] = jnp.where(odd == 1, moved, here)
+
+
+def take_frame(mine, other, meta):
+    lines = pl.pallas_call(
+        unframe_kernel,
+        out_shape=jax.ShapeDtypeStruct((LOCAL_LINES, 128), f32),
+        in_specs=[
+            pl.BlockSpec(memory_space=pltpu.SMEM),
+            pl.BlockSpec(memory_space=pltpu.VMEM),
+            pl.BlockSpec(memory_space=pltpu.VMEM),
+        ],
+        out_specs=pl.BlockSpec(memory_space=pltpu.VMEM),
+        scratch_shapes=[pltpu.VMEM((LINES + 8, 128), f32)],
+    )(meta, mine, other)
+    return lines.reshape(LOCAL_LINES * 128)[:LOCAL]
+
+
+def dot_nn(left_side, right_side):
+    return jnp.dot(left_side, right_side, preferred_element_type=f32)
+
+
+def row_mean(block):
+    return jnp.mean(block, axis=-1, keepdims=True)
+
+
+def layer_kernel(meta, tokens_ref, cot_ref, *refs):
+    frames = refs[:32]
+    block_ref, input_ref = refs[32:34]
+    keeps = refs[34:38]
+    sends = refs[38:42]
+    (
+        weights,
+        grads,
+        triple_w,
+        expand_w,
+        tails,
+        stage,
+        triple_b,
+        soft_all,
+        context_b,
+        act_b,
+        slope_all,
+        pre_b,
+        d_triple_b,
+        bias_grads,
+        sem_main,
+        sem_tail,
+        sem_out,
+    ) = refs[42:]
+    length = meta[0]
+    cols = (pl.multiple_of(meta[1], 128), pl.multiple_of(meta[2], 128))
+
+    arrivals = []
+    for side in range(2):
+        for k in range(16):
+            frame = frames[16 * side + k]
+            shard = meta[3 + 16 * side + k]
+            row = pl.multiple_of(shard * STEP_ROWS, 16)
+            main_copy = pltpu.make_async_copy(
+                frame.at[pl.ds(0, STEP_ROWS), :],
+                weights.at[pl.ds(row, STEP_ROWS), pl.ds(cols[side], HALF)],
+                sem_main.at[side, k],
+            )
+            tail_copy = pltpu.make_async_copy(
+                frame.at[pl.ds(STEP_ROWS, 16), :],
+                tails.at[shard, :, pl.ds(cols[side], HALF)],
+                sem_tail.at[side, k],
+            )
+            main_copy.start()
+            tail_copy.start()
+            arrivals.append(main_copy)
+            arrivals.append(tail_copy)
+    for copy in arrivals:
+        copy.wait()
+    for s in range(15):
+        at = STEP_ROWS * (s + 1)
+        joined = weights[at : at + 16, :].astype(f32) + tails[s].astype(f32)
+        weights[at : at + 16, :] = joined.astype(bf16)
+    weights[BIAS_ROW : BIAS_ROW + 16, :] = tails[15]
+
+    def spread_triple(i, carry):
+        for j in range(6):
+            at = slice(128 * j, 128 * (j + 1))
+            stage[j, 0:384, :] = weights[pl.ds(pl.multiple_of(384 * i, 16), 384), at].astype(f32)
+            for part in range(3):
+                rows = stage[j, pl.ds(part, 128, stride=3), :]
+                triple_w[part, pl.ds(pl.multiple_of(128 * i, 16), 128), at] = rows.astype(bf16)
+        return carry
+
+    lax.fori_loop(0, 6, spread_triple, 0)
+
+    def spread_expand(i, carry):
+        row = pl.multiple_of(EXP_ROW + 512 * i, 16)
+        for j in range(6):
+            at = slice(128 * j, 128 * (j + 1))
+            stage[j, :, :] = weights[pl.ds(row, 512), at].astype(f32)
+            for part in range(4):
+                rows = stage[j, pl.ds(part, 128, stride=4), :]
+                expand_w[part, pl.ds(pl.multiple_of(128 * i, 16), 128), at] = rows.astype(bf16)
+        return carry
+
+    lax.fori_loop(0, 6, spread_expand, 0)
+
+    biases = weights[BIAS_ROW : BIAS_ROW + 16, :].astype(f32)
+
+    def bias(index):
+        return biases[index : index + 1, :]
+
+    bias_grads[...] = jnp.zeros((16, ROW), f32)
+
+    def keep_bias(index, block):
+        bias_grads[index : index + 1, :] = jnp.sum(block, axis=0, keepdims=True)
+
+    tokens = tokens_ref[...]
+    triple_b[0] = (dot_nn(tokens, triple_w[0]) + bias(0)).astype(bf16)
+    triple_b[1] = dot_nn(tokens, triple_w[1]).astype(bf16)
+    triple_b[2] = (dot_nn(tokens, triple_w[2]) + bias(1)).astype(bf16)
+
+    lane = lax.broadcasted_iota(jnp.int32, (1, 128), 1)
+    head_masks = ((lane < 64).astype(f32).astype(bf16), (lane >= 64).astype(f32).astype(bf16))
+    key_valid = lax.broadcasted_iota(jnp.int32, (128, 128), 1) < length
+    scale = 1.0 / math.sqrt(HEAD)
+    for pair in range(6):
+        at = slice(128 * pair, 128 * (pair + 1))
+        queries, key_rows, value_rows = triple_b[0, :, at], triple_b[1, :, at], triple_b[2, :, at]
+        context = jnp.zeros((128, 128), f32)
+        for side in range(2):
+            scores = by_transpose(queries * head_masks[side], key_rows) * scale
+            scores = jnp.where(key_valid, scores, masked_score)
+            top_score = jnp.max(scores, axis=-1, keepdims=True)
+            log_total = top_score + jnp.log(
+                jnp.sum(jnp.exp(scores - top_score), axis=-1, keepdims=True)
+            )
+            soft_float = jnp.exp(scores - log_total)
+            soft_all[2 * pair + side] = soft_float
+            context = context + dot_nn(soft_float.astype(bf16), value_rows * head_masks[side])
+        context_b[:, at] = context.astype(bf16)
+
+    first_sum = tokens.astype(f32) + dot_nn(context_b[...], weights[OUT_ROW : OUT_ROW + 768, :]) + bias(2)
+    normed_one, root_one = normalize(first_sum)
+    middle = normed_one * bias(3) + bias(4)
+    middle_b = middle.astype(bf16)
+    second_sum = middle + bias(9)
+    for part in range(4):
+        at = slice(768 * part, 768 * (part + 1))
+        pre_act = dot_nn(middle_b, expand_w[part]) + bias(5 + part)
+        erf_term = 1.0 + lax.erf(pre_act * inv_sqrt_two)
+        activated = (0.5 * pre_act * erf_term).astype(bf16)
+        act_b[:, at] = activated
+        slope_all[:, at] = 0.5 * erf_term + pre_act * jnp.exp(-0.5 * pre_act * pre_act) * inv_sqrt_tau
+        red_at = RED_ROW + 768 * part
+        second_sum = second_sum + dot_nn(activated, weights[red_at : red_at + 768, :])
+    normed_two, root_two = normalize(second_sum)
+    block_ref[...] = (normed_two * bias(10) + bias(11)).astype(bf16)
+
+    grad_out = cot_ref[...].astype(f32)
+    keep_bias(10, grad_out * normed_two)
+    keep_bias(11, grad_out)
+    d_second = norm_back(grad_out * bias(10), normed_two, root_two)
+    keep_bias(9, d_second)
+    d_second_b = d_second.astype(bf16)
+    d_middle = d_second
+    for part in range(4):
+        at = slice(768 * part, 768 * (part + 1))
+        red_at = RED_ROW + 768 * part
+        d_pre = by_transpose(d_second_b, weights[red_at : red_at + 768, :]) * slope_all[:, at]
+        keep_bias(5 + part, d_pre)
+        d_pre_b = d_pre.astype(bf16)
+        pre_b[:, at] = d_pre_b
+        d_middle = d_middle + by_transpose(d_pre_b, expand_w[part])
+
+    def reduce_grad(i, carry):
+        at = pl.multiple_of(256 * i, 256)
+        block = inner_rows(act_b[:, pl.ds(at, 256)], d_second_b)
+        grads[pl.ds(pl.multiple_of(RED_ROW + at, 16), 256), :] = block.astype(bf16)
+        return carry
+
+    lax.fori_loop(0, 12, reduce_grad, 0)
+
+    act_b[:, 0:768] = middle_b
+
+    def expand_grad(i, carry):
+        left = act_b[:, pl.ds(pl.multiple_of(128 * i, 128), 128)]
+        for part in range(4):
+            block = inner_rows(left, pre_b[:, 768 * part : 768 * (part + 1)])
+            for j in range(6):
+                stage[j, pl.ds(part, 128, stride=4), :] = block[:, 128 * j : 128 * (j + 1)]
+        row = pl.multiple_of(EXP_ROW + 512 * i, 16)
+        for j in range(6):
+            grads[pl.ds(row, 512), 128 * j : 128 * (j + 1)] = stage[j].astype(bf16)
+        return carry
+
+    lax.fori_loop(0, 6, expand_grad, 0)
+
+    keep_bias(3, d_middle * normed_one)
+    keep_bias(4, d_middle)
+    d_first = norm_back(d_middle * bias(3), normed_one, root_one)
+    keep_bias(2, d_first)
+    d_first_b = d_first.astype(bf16)
+    d_context_b = by_transpose(d_first_b, weights[OUT_ROW : OUT_ROW + 768, :]).astype(bf16)
+
+    def output_grad(i, carry):
+        at = pl.multiple_of(256 * i, 256)
+        block = inner_rows(context_b[:, pl.ds(at, 256)], d_first_b)
+        grads[pl.ds(pl.multiple_of(OUT_ROW + at, 16), 256), :] = block.astype(bf16)
+        return carry
+
+    lax.fori_loop(0, 3, output_grad, 0)
+
+    for pair in range(6):
+        at = slice(128 * pair, 128 * (pair + 1))
+        queries, key_rows, value_rows = triple_b[0, :, at], triple_b[1, :, at], triple_b[2, :, at]
+        d_context = d_context_b[:, at]
+        d_query = jnp.zeros((128, 128), f32)
+        d_keys = jnp.zeros((128, 128), f32)
+        d_values = jnp.zeros((128, 128), f32)
+        for side in range(2):
+            soft_float = soft_all[2 * pair + side]
+            d_part = d_context * head_masks[side]
+            d_soft = by_transpose(d_part, value_rows)
+            delta = jnp.sum(d_soft * soft_float, axis=-1, keepdims=True)
+            d_scores = (soft_float * (d_soft - delta) * scale).astype(bf16)
+            d_query = d_query + dot_nn(d_scores, key_rows * head_masks[side])
+            d_keys = d_keys + inner_rows(d_scores, queries * head_masks[side])
+            d_values = d_values + inner_rows(soft_float.astype(bf16), d_part)
+        bias_grads[0:1, at] = jnp.sum(d_query, axis=0, keepdims=True)
+        bias_grads[1:2, at] = jnp.sum(d_values, axis=0, keepdims=True)
+        d_triple_b[0, :, at] = d_query.astype(bf16)
+        d_triple_b[1, :, at] = d_keys.astype(bf16)
+        d_triple_b[2, :, at] = d_values.astype(bf16)
+
+    input_grad = d_first
+    for part in range(3):
+        input_grad = input_grad + by_transpose(d_triple_b[part], triple_w[part])
+    input_ref[...] = input_grad.astype(bf16)
+
+    def triple_grad(i, carry):
+        left = tokens_ref[:, pl.ds(pl.multiple_of(128 * i, 128), 128)]
+        for part in range(3):
+            block = inner_rows(left, d_triple_b[part])
+            for j in range(6):
+                stage[j, pl.ds(part, 128, stride=3), :] = block[:, 128 * j : 128 * (j + 1)]
+        row = pl.multiple_of(384 * i, 16)
+        for j in range(6):
+            grads[pl.ds(row, 384), 128 * j : 128 * (j + 1)] = stage[j, 0:384, :].astype(bf16)
+        return carry
+
+    lax.fori_loop(0, 6, triple_grad, 0)
+    grads[BIAS_ROW : BIAS_ROW + 16, :] = bias_grads[...].astype(bf16)
+
+    departures = []
+    for side in range(2):
+        for k in range(16):
+            shard = meta[3 + 16 * side + k]
+            row = pl.multiple_of(shard * STEP_ROWS, 16)
+            target = (keeps if side == 0 else sends)[k // 4]
+            copy = pltpu.make_async_copy(
+                grads.at[pl.ds(row, FRAME), pl.ds(cols[side], HALF)],
+                target.at[k % 4],
+                sem_out.at[side, k],
+            )
+            copy.start()
+            departures.append(copy)
+    for copy in departures:
+        copy.wait()
+
+
+def run_layer(meta, tokens, cotangent, frames):
+    any_spec = pl.BlockSpec(memory_space=pl.ANY)
+    vmem_spec = pl.BlockSpec(memory_space=pltpu.VMEM)
+    rows = tokens.shape[0]
+    out = pl.pallas_call(
+        layer_kernel,
+        out_shape=[jax.ShapeDtypeStruct((rows, D), bf16)] * 2
+        + [jax.ShapeDtypeStruct((4, FRAME, HALF), bf16)] * 8,
+        in_specs=[pl.BlockSpec(memory_space=pltpu.SMEM), vmem_spec, vmem_spec] + [any_spec] * 32,
+        out_specs=[vmem_spec] * 2 + [any_spec] * 8,
+        scratch_shapes=[
+            pltpu.VMEM((ROWS, ROW), bf16),
+            pltpu.VMEM((ROWS, ROW), bf16),
+            pltpu.VMEM((3, D, HW), bf16),
+            pltpu.VMEM((4, D, ROW), bf16),
+            pltpu.VMEM((16, 16, ROW), bf16),
+            pltpu.VMEM((6, 512, 128), f32),
+            pltpu.VMEM((3, rows, HW), bf16),
+            pltpu.VMEM((HEADS, rows, rows), f32),
+            pltpu.VMEM((rows, HW), bf16),
+            pltpu.VMEM((rows, FF), bf16),
+            pltpu.VMEM((rows, FF), f32),
+            pltpu.VMEM((rows, FF), bf16),
+            pltpu.VMEM((3, rows, HW), bf16),
+            pltpu.VMEM((16, ROW), f32),
+            pltpu.SemaphoreType.DMA((2, 16)),
+            pltpu.SemaphoreType.DMA((2, 16)),
+            pltpu.SemaphoreType.DMA((2, 16)),
+        ],
+        compiler_params=pltpu.CompilerParams(vmem_limit_bytes=VMEM_CAP),
+    )(meta, tokens, cotangent, *frames)
+    return out[0], out[1], out[2:6], out[6:10]
+
+
+def plane_moves(n):
+    near, far = [], []
+    for s in range(n):
+        near += [(s, s ^ 1), (n + s, n + (s ^ 2))]
+        far += [(s, s ^ 2), (n + s, n + (s ^ 1))]
+    return near, far
+
+
+def on_device_planes(hidden_states, cotangent, lengths, params, first_moment, second_moment):
+    n = 16
+    both = ("rep", "shard")
+    near, far = plane_moves(n)
+    swap = [(0, 1), (1, 0)]
+    core = lax.axis_index("rep")
+    here = lax.axis_index("shard")
+    plane, spot = here // 4, here % 4
+    shift, odd = (9 * here) // 2, here % 2
+    shape_meta = jnp.stack([shift, odd, 3 * core, 3 - 3 * core]).astype(jnp.int32)
+    spots = jnp.array([[0, 1, 2, 3], [0, 2, 1, 3]], jnp.int32)
+    slots = jnp.arange(4, dtype=jnp.int32)
+    base = ((plane - slots) % 4)[:, None] * 4
+    mine_at = base + (spot ^ spots[core])[None, :]
+    other_at = base + (spot ^ spots[1 - core])[None, :]
+    layer_meta = jnp.concatenate(
+        [
+            jnp.stack([lengths[0], HALF * core, HALF - HALF * core]).astype(jnp.int32),
+            mine_at.reshape(-1),
+            other_at.reshape(-1),
+        ]
+    ).astype(jnp.int32)
+
+    own = make_frame(params, shape_meta)
+    mine, other = [], []
+    for t in range(4):
+        zero = own if t == 0 else lax.ppermute(own, "shard", [(s, (s + 4 * t) % n) for s in range(n)])
+        one = lax.ppermute(zero, both, near)
+        two = lax.ppermute(zero, both, far)
+        three = lax.ppermute(one, both, far)
+        group = [zero, one, two, three]
+        mine += group
+        other += [lax.ppermute(piece, "rep", swap) for piece in group]
+
+    block_out, input_grad, keeps, sends = run_layer(layer_meta, hidden_states, cotangent, mine + other)
+
+    total = None
+    for t in range(4):
+        keep = keeps[t].astype(f32)
+        got = lax.ppermute(sends[t], "rep", swap).astype(f32)
+        away = (keep[2:4] + got[2:4]).astype(bf16)
+        from_far = lax.ppermute(away, both, far).astype(f32)
+        away = (keep[1] + got[1] + from_far[1]).astype(bf16)
+        from_near = lax.ppermute(away, both, near).astype(f32)
+        partial = keep[0] + got[0] + from_far[0] + from_near
+        if t > 0:
+            partial = lax.ppermute(
+                partial.astype(bf16), "shard", [(s, (s - 4 * t) % n) for s in range(n)]
+            ).astype(f32)
+        total = partial if total is None else total + partial
+    weight_grad = take_frame(total, lax.ppermute(total, "rep", swap), shape_meta)
+    new_params, new_first, new_second = adamw(params, first_moment, second_moment, weight_grad)
+    return (block_out, input_grad, weight_grad, new_params, new_first, new_second)
+
+
+def on_device_any(hidden_states, cotangent, lengths, params, first_moment, second_moment):
     length = lengths[0]
-    shard_b = params.astype(jnp.bfloat16)
-    gathered = lax.all_gather(shard_b, "shard", axis=0, tiled=True)
+    gathered = lax.all_gather(params.astype(jnp.bfloat16), "shard", axis=0, tiled=True)
     prm = split_flat(gathered)
     block_out, kept = forward(hidden_states, length, prm)
-    gathered_again = lax.all_gather(shard_b, "shard", axis=0, tiled=True)
-    prm_back = split_flat(gathered_again)
-    input_grad, flat_grad = backward(hidden_states, length, cotangent, kept, prm_back)
+    input_grad, flat_grad = backward(hidden_states, length, cotangent, kept, prm)
     owned = lax.psum_scatter(flat_grad, "shard", scatter_dimension=0, tiled=True)
     weight_grad = lax.psum(owned, "rep")
     new_params, new_first, new_second = adamw(params, first_moment, second_moment, weight_grad)
@@ -253,8 +680,9 @@
         P("shard"),
         P("shard"),
     )
+    sixteen = mesh.shape["shard"] == 16 and mesh.shape["rep"] == 2
     return jax.shard_map(
-        on_device,
+        on_device_planes if sixteen else on_device_any,
         mesh=mesh,
         in_specs=placed,
         out_specs=(

time: 1370 us -> 270 us (0.20)
  waiting for transfers between devices: 1150 us -> 146 us
  local copies, waits for them, and re-layouts: 136 us -> 7.24 us
  starting transfers between devices: 0.12 us -> 56.7 us
  matrix products: 48 us -> 0 us
  Pallas kernels: 0 us -> 45 us
  between operations: 16.1 us -> 1.64 us
    unnamed x5 -> x0, waiting for transfers between devices: 1130 us -> none
    ppermute x0 -> x47, waiting for transfers between devices: none -> 146 us  [the longest x4 44.7 us: on_device_planes(): from_far = lax.ppermute(away, both, far).astype(f32)]
    unnamed x98 -> x56, local copies, waits for them, and re-layouts: 66.2 us -> 3.63 us
    ppermute x0 -> x47, starting transfers between devices: none -> 56.7 us  [the longest x3 15.1 us: on_device_planes(): lax.ppermute(partial.astype(bf16), 'shard', [(s, (s - 4 * t) % n) for s i...]
    dot_general x18 -> x0, matrix products: 48 us -> none  [the longest x4 17 us: inner_rows(): lax.dot_general(left_side, right_side, (((0,), (0,)), ((), ())), preferre...]
    pallas_call x0 -> x3, Pallas kernels: none -> 45 us  [the longest x1 37.9 us: run_layer(): pl.pallas_call(layer_kernel, out_shape=[jax.ShapeDtypeStruct((rows, D), b...]
    slice x9 -> x0, local copies, waits for them, and re-layouts: 38.5 us -> none  [the longest x8 38.5 us: split_flat(): pieces[entry_name] = flat_vector[offset:offset + amount].reshape(dims_of)]
    reshape x3 -> x1, local copies, waits for them, and re-layouts: 20.3 us -> 2.8 us  [make_frame(): jnp.pad(params, (0, LOCAL_LINES * 128 - LOCAL)).reshape(LOCAL_LINES, 128)]
  transfers between devices with their start and end apart: 3 -> 47, of which waited for: 3 -> 21; matrix products, arithmetic and copies ran while one was open for 0% -> 3% of each run, Pallas kernels for 0% -> 0%
where the time goes in v1:
time: 270 us; the launch traced here: 269 us
  waiting for transfers between devices  146 us (54%)
  starting transfers between devices  56.7 us (21%)
  Pallas kernels  45 us (17%)
  other arithmetic  13.1 us (5%)
  local copies, waits for them, and re-layouts  7.24 us (3%)
    ppermute x4, waiting for transfers between devices, on_device_planes(): from_far = lax.ppermute(away, both, far).astype(f32)  44.7 us
    pallas_call x1, Pallas kernels, run_layer(): pl.pallas_call(layer_kernel, out_shape=[jax.ShapeDtypeStruct((rows, D), b...  37.9 us
    ppermute x3, waiting for transfers between devices, on_device_planes(): lax.ppermute(partial.astype(bf16), 'shard', [(s, (s - 4 * t) % n) for s i...  33 us
    ppermute x3, waiting for transfers between devices, on_device_planes(): lax.ppermute(own, 'shard', [(s, (s + 4 * t) % n) for s in range(n)])  25.3 us
    ppermute x4, waiting for transfers between devices, on_device_planes(): one = lax.ppermute(zero, both, near)  20.2 us
    ppermute x3, starting transfers between devices, on_device_planes(): lax.ppermute(partial.astype(bf16), 'shard', [(s, (s - 4 * t) % n) for s i...  15.1 us
    ppermute x4, waiting for transfers between devices, on_device_planes(): three = lax.ppermute(one, both, far)  14.1 us
    ppermute x4, starting transfers between devices, on_device_planes(): two = lax.ppermute(zero, both, far)  7.31 us
  transfers between devices with their start and end apart: 47, of which 21 were waited for; matrix products, arithmetic and copies ran while one was open for 3% of the time, Pallas kernels for 0%

profile of v1, /device:TPU:0, one launch (start us, length us, event | category | flops | bytes accessed | tf_op | source)
XLA Modules:
  0.0 269.3 jit_solution(10062791597932590761)
XLA Ops:
  0.6 2.8 %pad_bitcast_fusion.flat_ref = f32[3464,128]{1,0:T(8,128)} fusion(f32[442944]{0:T(1024)} %param.10), kind=kLoop, calls=%fused_computation.12 | loop fusion | bytes 3545344 | tf_op jit(solution)/shard_map/reshape | solution.py:272
  4.1 3.3 %shard_map.118.refs_0_ = bf16[592,384]{1,0:T(8,128)(2,1)} custom-call(s32[4]{0:T(128)} %pad_add_fusion.meta, f32[3464,128]{1,0:T(8,128)} %pad_bitcast_fusion.flat_ref), custom_call_target="tpu_custom_call" | custom-call | tf_op jit(solution)/shard_map/pallas_call | solution.py:273
  7.4 3.0 %collective-permute-start.3 = (bf16[592,384]{1,0:T(8,128)(2,1)}, bf16[592,384]{1,0:T(8,128)(2,1)S(1)}, u32[]{:S(2)}, u32[]{:S(2)}) collective-permute-start(bf16[592,384]{1,0:T(8,128)(2,1)} %shard_map.118.refs_0_), channel_id=1, source_target_pairs={{0,4},{1,5},{2,6},{3,7},{4,8},{5,9},{6,10},{7,11},{8,12},{9,13},{1... | collective-permute-start | bytes 1363976 | tf_op jit(solution)/shard_map/ppermute | solution.py:633
  17.4 6.7 %collective-permute-done.3.refs_4_ = bf16[592,384]{1,0:T(8,128)(2,1)S(1)} collective-permute-done((bf16[592,384]{1,0:T(8,128)(2,1)}, bf16[592,384]{1,0:T(8,128)(2,1)S(1)}, u32[]{:S(2)}, u32[]{:S(2)}) %collective-permute-start.3) | collective-permute-done | bytes 454688 | tf_op jit(solution)/shard_map/ppermute | solution.py:633
  24.1 18.6 %collective-permute-done.7.refs_8_ = bf16[592,384]{1,0:T(8,128)(2,1)S(1)} collective-permute-done((bf16[592,384]{1,0:T(8,128)(2,1)}, bf16[592,384]{1,0:T(8,128)(2,1)S(1)}, u32[]{:S(2)}, u32[]{:S(2)}) %collective-permute-start.7) | collective-permute-done | bytes 454688 | tf_op jit(solution)/shard_map/ppermute | solution.py:633
  48.3 6.0 %collective-permute-done.4.refs_5_ = bf16[592,384]{1,0:T(8,128)(2,1)S(1)} collective-permute-done((bf16[592,384]{1,0:T(8,128)(2,1)S(1)}, bf16[592,384]{1,0:T(8,128)(2,1)S(1)}, u32[]{:S(2)}, u32[]{:S(2)}) %collective-permute-start.4) | collective-permute-done | bytes 454688 | tf_op jit(solution)/shard_map/ppermute | solution.py:634
  54.3 2.6 collective-permute-start.9
  56.9 7.1 %collective-permute-done.8.refs_9_ = bf16[592,384]{1,0:T(8,128)(2,1)S(1)} collective-permute-done((bf16[592,384]{1,0:T(8,128)(2,1)S(1)}, bf16[592,384]{1,0:T(8,128)(2,1)S(1)}, u32[]{:S(2)}, u32[]{:S(2)}) %collective-permute-start.8) | collective-permute-done | bytes 454688 | tf_op jit(solution)/shard_map/ppermute | solution.py:634
  66.7 7.1 %collective-permute-done.12.refs_13_ = bf16[592,384]{1,0:T(8,128)(2,1)S(1)} collective-permute-done((bf16[592,384]{1,0:T(8,128)(2,1)S(1)}, bf16[592,384]{1,0:T(8,128)(2,1)S(1)}, u32[]{:S(2)}, u32[]{:S(2)}) %collective-permute-start.12) | collective-permute-done | bytes 454688 | tf_op jit(solution)/shard_map/ppermute | solution.py:634
  75.7 3.7 %collective-permute-done.13.refs_14_ = bf16[592,384]{1,0:T(8,128)(2,1)} collective-permute-done((bf16[592,384]{1,0:T(8,128)(2,1)S(1)}, bf16[592,384]{1,0:T(8,128)(2,1)}, u32[]{:S(2)}, u32[]{:S(2)}) %collective-permute-start.13) | collective-permute-done | bytes 454688 | tf_op jit(solution)/shard_map/ppermute | solution.py:635
  84.5 4.4 %collective-permute-done.6.refs_7_ = bf16[592,384]{1,0:T(8,128)(2,1)} collective-permute-done((bf16[592,384]{1,0:T(8,128)(2,1)S(1)}, bf16[592,384]{1,0:T(8,128)(2,1)}, u32[]{:S(2)}, u32[]{:S(2)}) %collective-permute-start.6) | collective-permute-done | bytes 454688 | tf_op jit(solution)/shard_map/ppermute | solution.py:636
  88.9 4.9 %collective-permute-done.10.refs_11_ = bf16[592,384]{1,0:T(8,128)(2,1)} collective-permute-done((bf16[592,384]{1,0:T(8,128)(2,1)S(1)}, bf16[592,384]{1,0:T(8,128)(2,1)}, u32[]{:S(2)}, u32[]{:S(2)}) %collective-permute-start.10) | collective-permute-done | bytes 454688 | tf_op jit(solution)/shard_map/ppermute | solution.py:636
  93.7 4.9 %collective-permute-done.14.refs_15_ = bf16[592,384]{1,0:T(8,128)(2,1)} collective-permute-done((bf16[592,384]{1,0:T(8,128)(2,1)S(1)}, bf16[592,384]{1,0:T(8,128)(2,1)}, u32[]{:S(2)}, u32[]{:S(2)}) %collective-permute-start.14) | collective-permute-done | bytes 454688 | tf_op jit(solution)/shard_map/ppermute | solution.py:636
  104.0 37.9 %shard_map.119 = (bf16[128,768]{1,0:T(8,128)(2,1)}, bf16[128,768]{1,0:T(8,128)(2,1)}, bf16[4,592,384]{2,1,0:T(8,128)(2,1)}, bf16[4,592,384]{2,1,0:T(8,128)(2,1)}...) custom-call(s32[35]{0:T(128)} %concatenate.3.meta, ...), custom_call_target="tpu_custom_call" | custom-call | tf_op jit(solution)/shard_map/pallas_call | solution.py:569
  155.8 6.3 %collective-permute-done.32 = bf16[2,592,384]{2,1,0:T(8,128)(2,1)S(1)} collective-permute-done((bf16[2,592,384]{2,1,0:T(8,128)(2,1)S(1)}, bf16[2,592,384]{2,1,0:T(8,128)(2,1)S(1)}, u32[]{:S(2)}, u32[]{:S(2)}) %collective-permute-start.32) | collective-permute-done | bytes 909344 | tf_op jit(solution)/shard_map/ppermute | solution.py:648
  163.9 12.8 %collective-permute-done.35 = bf16[2,592,384]{2,1,0:T(8,128)(2,1)S(1)} collective-permute-done((bf16[2,592,384]{2,1,0:T(8,128)(2,1)S(1)}, bf16[2,592,384]{2,1,0:T(8,128)(2,1)S(1)}, u32[]{:S(2)}, u32[]{:S(2)}) %collective-permute-start.35) | collective-permute-done | bytes 909344 | tf_op jit(solution)/shard_map/ppermute | solution.py:648
  178.6 12.8 %collective-permute-done.39 = bf16[2,592,384]{2,1,0:T(8,128)(2,1)S(1)} collective-permute-done((bf16[2,592,384]{2,1,0:T(8,128)(2,1)S(1)}, bf16[2,592,384]{2,1,0:T(8,128)(2,1)S(1)}, u32[]{:S(2)}, u32[]{:S(2)}) %collective-permute-start.39) | collective-permute-done | bytes 909344 | tf_op jit(solution)/shard_map/ppermute | solution.py:648
  193.2 12.8 %collective-permute-done.43 = bf16[2,592,384]{2,1,0:T(8,128)(2,1)S(1)} collective-permute-done((bf16[2,592,384]{2,1,0:T(8,128)(2,1)S(1)}, bf16[2,592,384]{2,1,0:T(8,128)(2,1)S(1)}, u32[]{:S(2)}, u32[]{:S(2)}) %collective-permute-start.43) | collective-permute-done | bytes 909344 | tf_op jit(solution)/shard_map/ppermute | solution.py:648
  208.0 11.3 %collective-permute-start.37 = (bf16[592,384]{1,0:T(8,128)(2,1)S(1)}, bf16[592,384]{1,0:T(8,128)(2,1)S(1)}, u32[]{:S(2)}, u32[]{:S(2)}) collective-permute-start(bf16[592,384]{1,0:T(8,128)(2,1)S(1)} %fusion.16), channel_id=1, source_target_pairs={{0,12},{1,13},{2,14},{3,15},{4,0},{5,1},{6,2},{7,3},{8,4},{9,5},{1... | collective-permute-start | bytes 1363976 | tf_op jit(solution)/shard_map/ppermute | solution.py:653
  219.8 3.7 %collective-permute-start.45 = (bf16[592,384]{1,0:T(8,128)(2,1)S(1)}, bf16[592,384]{1,0:T(8,128)(2,1)S(1)}, u32[]{:S(2)}, u32[]{:S(2)}) collective-permute-start(bf16[592,384]{1,0:T(8,128)(2,1)S(1)} %fusion.8), channel_id=1, source_target_pairs={{0,4},{1,5},{2,6},{3,7},{4,8},{5,9},{6,10},{7,11},{8,12},{9,13},{1... | collective-permute-start | bytes 1363976 | tf_op jit(solution)/shard_map/ppermute | solution.py:653
  223.5 6.7 %collective-permute-done.37 = bf16[592,384]{1,0:T(8,128)(2,1)S(1)} collective-permute-done((bf16[592,384]{1,0:T(8,128)(2,1)S(1)}, bf16[592,384]{1,0:T(8,128)(2,1)S(1)}, u32[]{:S(2)}, u32[]{:S(2)}) %collective-permute-start.37) | collective-permute-done | bytes 454688 | tf_op jit(solution)/shard_map/ppermute | solution.py:653
  230.2 26.3 %collective-permute-done.41 = bf16[592,384]{1,0:T(8,128)(2,1)S(1)} collective-permute-done((bf16[592,384]{1,0:T(8,128)(2,1)S(1)}, bf16[592,384]{1,0:T(8,128)(2,1)S(1)}, u32[]{:S(2)}, u32[]{:S(2)}) %collective-permute-start.41) | collective-permute-done | bytes 454688 | tf_op jit(solution)/shard_map/ppermute | solution.py:653
  259.6 3.8 %shard_map.120 = f32[3464,128]{1,0:T(8,128)} custom-call(s32[4]{0:T(128)} %pad_add_fusion.meta, f32[592,384]{1,0:T(8,128)} %copy-done.1, f32[592,384]{1,0:T(8,128)} %collective-permute-done.46.other_ref), custom_call_target="tpu_custom_call" | custom-call | tf_op jit(solution)/shard_map/pallas_call | solution.py:301
  263.5 5.9 %multiply_subtract_fusion = (f32[442944]{0:T(1024)}, f32[442944]{0:T(1024)}, f32[442944]{0:T(1024)}, f32[442944]{0:T(1024)}) fusion(f32[442944]{0:T(1024)S(1)} %copy-done, f32[442944]{0:T(1024)} %param.11, f32[442944]{0:T(1024)} %param.12, f32[443392]{0:T(1024)} %bitcast.49), kind=kLoop, calls=%fused_computation.10 | loop fusion | flops 6644160 | bytes 14174208 | tf_op jit(solution)/shard_map/sub | solution.py:228
  (162 shorter events, 52.3 us)
Async XLA Ops:
  7.4 16.7 %collective-permute-start.3 = (bf16[592,384]{1,0:T(8,128)(2,1)}, bf16[592,384]{1,0:T(8,128)(2,1)S(1)}, u32[]{:S(2)}, u32[]{:S(2)}) collective-permute-start(bf16[592,384]{1,0:T(8,128)(2,1)} %shard_map.118.refs_0_), channel_id=1, source_target_pairs={{0,4},{1,5},{2,6},{3,7},{4,8},{5,9},{6,10},{7,11},{8,12},{9,13},{1... | collective-permute-start | bytes 1363976 | tf_op jit(solution)/shard_map/ppermute | solution.py:633
  10.4 32.3 %collective-permute-start.7 = (bf16[592,384]{1,0:T(8,128)(2,1)}, bf16[592,384]{1,0:T(8,128)(2,1)S(1)}, u32[]{:S(2)}, u32[]{:S(2)}) collective-permute-start(bf16[592,384]{1,0:T(8,128)(2,1)} %shard_map.118.refs_0_), channel_id=1, source_target_pairs={{0,8},{1,9},{2,10},{3,11},{4,12},{5,13},{6,14},{7,15},{8,0},{9,1},... | collective-permute-start | bytes 1363976 | tf_op jit(solution)/shard_map/ppermute | solution.py:633
  13.0 31.2 %collective-permute-start.11 = (bf16[592,384]{1,0:T(8,128)(2,1)}, bf16[592,384]{1,0:T(8,128)(2,1)S(1)}, u32[]{:S(2)}, u32[]{:S(2)}) collective-permute-start(bf16[592,384]{1,0:T(8,128)(2,1)} %shard_map.118.refs_0_), channel_id=1, source_target_pairs={{0,12},{1,13},{2,14},{3,15},{4,0},{5,1},{6,2},{7,3},{8,4},{9,5},{1... | collective-permute-start | bytes 1363976 | tf_op jit(solution)/shard_map/ppermute | solution.py:633
  14.4 30.4 %collective-permute-start = (bf16[592,384]{1,0:T(8,128)(2,1)}, bf16[592,384]{1,0:T(8,128)(2,1)S(1)}, u32[]{:S(2)}, u32[]{:S(2)}) collective-permute-start(bf16[592,384]{1,0:T(8,128)(2,1)} %shard_map.118.refs_0_), channel_id=1, source_target_pairs={{0,1},{16,18},{1,0},{17,19},{2,3},{18,16},{3,2},{19,17},{4,5},{20,... | collective-permute-start | bytes 1363976 | tf_op jit(solution)/shard_map/ppermute | solution.py:634
  15.8 30.4 %collective-permute-start.1 = (bf16[592,384]{1,0:T(8,128)(2,1)}, bf16[592,384]{1,0:T(8,128)(2,1)S(1)}, u32[]{:S(2)}, u32[]{:S(2)}) collective-permute-start(bf16[592,384]{1,0:T(8,128)(2,1)} %shard_map.118.refs_0_), channel_id=1, source_target_pairs={{0,2},{16,17},{1,3},{17,16},{2,0},{18,19},{3,1},{19,18},{4,6},{20,... | collective-permute-start | bytes 1363976 | tf_op jit(solution)/shard_map/ppermute | solution.py:635
  24.1 23.7 %collective-permute-start.15 = (bf16[592,384]{1,0:T(8,128)(2,1)}, bf16[592,384]{1,0:T(8,128)(2,1)S(1)}, u32[]{:S(2)}, u32[]{:S(2)}) collective-permute-start(bf16[592,384]{1,0:T(8,128)(2,1)} %shard_map.118.refs_0_), channel_id=1, source_target_pairs={{0,16},{16,0},{1,17},{17,1},{2,18},{18,2},{3,19},{19,3},{4,20},{20... | collective-permute-start | bytes 1363976 | tf_op jit(solution)/shard_map/ppermute | solution.py:639
  44.2 19.8 %collective-permute-start.8 = (bf16[592,384]{1,0:T(8,128)(2,1)S(1)}, bf16[592,384]{1,0:T(8,128)(2,1)S(1)}, u32[]{:S(2)}, u32[]{:S(2)}) collective-permute-start(bf16[592,384]{1,0:T(8,128)(2,1)S(1)} %collective-permute-done.7.refs_8_), channel_id=1, source_target_pairs={{0,1},{16,18},{1,0},{17,19},{2,3},{18,16},{3,2},{19,17},{4,5},{20,... | collective-permute-start | bytes 1363976 | tf_op jit(solution)/shard_map/ppermute | solution.py:634
  44.7 29.0 %collective-permute-start.12 = (bf16[592,384]{1,0:T(8,128)(2,1)S(1)}, bf16[592,384]{1,0:T(8,128)(2,1)S(1)}, u32[]{:S(2)}, u32[]{:S(2)}) collective-permute-start(bf16[592,384]{1,0:T(8,128)(2,1)S(1)} %collective-permute-done.11.refs_12_), channel_id=1, source_target_pairs={{0,1},{16,18},{1,0},{17,19},{2,3},{18,16},{3,2},{19,17},{4,5},{20,... | collective-permute-start | bytes 1363976 | tf_op jit(solution)/shard_map/ppermute | solution.py:634
  46.2 27.5 %collective-permute-start.2 = (bf16[592,384]{1,0:T(8,128)(2,1)S(1)}, bf16[592,384]{1,0:T(8,128)(2,1)S(1)}, u32[]{:S(2)}, u32[]{:S(2)}) collective-permute-start(bf16[592,384]{1,0:T(8,128)(2,1)S(1)} %collective-permute-done.refs_1_), channel_id=1, source_target_pairs={{0,2},{16,17},{1,3},{17,16},{2,0},{18,19},{3,1},{19,18},{4,6},{20,... | collective-permute-start | bytes 1363976 | tf_op jit(solution)/shard_map/ppermute | solution.py:636
  47.8 26.5 %collective-permute-start.5 = (bf16[592,384]{1,0:T(8,128)(2,1)S(1)}, bf16[592,384]{1,0:T(8,128)(2,1)S(1)}, u32[]{:S(2)}, u32[]{:S(2)}) collective-permute-start(bf16[592,384]{1,0:T(8,128)(2,1)S(1)} %collective-permute-done.3.refs_4_), channel_id=1, source_target_pairs={{0,2},{16,17},{1,3},{17,16},{2,0},{18,19},{3,1},{19,18},{4,6},{20,... | collective-permute-start | bytes 1363976 | tf_op jit(solution)/shard_map/ppermute | solution.py:635
  54.3 20.2 %collective-permute-start.9 = (bf16[592,384]{1,0:T(8,128)(2,1)S(1)}, bf16[592,384]{1,0:T(8,128)(2,1)S(1)}, u32[]{:S(2)}, u32[]{:S(2)}) collective-permute-start(bf16[592,384]{1,0:T(8,128)(2,1)S(1)} %collective-permute-done.7.refs_8_), channel_id=1, source_target_pairs={{0,2},{16,17},{1,3},{17,16},{2,0},{18,19},{3,1},{19,18},{4,6},{20,... | collective-permute-start | bytes 1363976 | tf_op jit(solution)/shard_map/ppermute | solution.py:635
  64.0 15.4 %collective-permute-start.13 = (bf16[592,384]{1,0:T(8,128)(2,1)S(1)}, bf16[592,384]{1,0:T(8,128)(2,1)}, u32[]{:S(2)}, u32[]{:S(2)}) collective-permute-start(bf16[592,384]{1,0:T(8,128)(2,1)S(1)} %collective-permute-done.11.refs_12_), channel_id=1, source_target_pairs={{0,2},{16,17},{1,3},{17,16},{2,0},{18,19},{3,1},{19,18},{4,6},{20,... | collective-permute-start | bytes 1363976 | tf_op jit(solution)/shard_map/ppermute | solution.py:635
  82.3 16.2 %collective-permute-start.14 = (bf16[592,384]{1,0:T(8,128)(2,1)S(1)}, bf16[592,384]{1,0:T(8,128)(2,1)}, u32[]{:S(2)}, u32[]{:S(2)}) collective-permute-start(bf16[592,384]{1,0:T(8,128)(2,1)S(1)} %collective-permute-done.12.refs_13_), channel_id=1, source_target_pairs={{0,2},{16,17},{1,3},{17,16},{2,0},{18,19},{3,1},{19,18},{4,6},{20,... | collective-permute-start | bytes 1363976 | tf_op jit(solution)/shard_map/ppermute | solution.py:636
  83.9 14.7 %collective-permute-start.18 = (bf16[592,384]{1,0:T(8,128)(2,1)S(1)}, bf16[592,384]{1,0:T(8,128)(2,1)S(1)}, u32[]{:S(2)}, u32[]{:S(2)}) collective-permute-start(bf16[592,384]{1,0:T(8,128)(2,1)S(1)} %collective-permute-done.2.refs_3_), channel_id=1, source_target_pairs={{0,16},{16,0},{1,17},{17,1},{2,18},{18,2},{3,19},{19,3},{4,20},{20... | collective-permute-start | bytes 1363976 | tf_op jit(solution)/shard_map/ppermute | solution.py:639
  83.9 15.2 %collective-permute-start.20 = (bf16[592,384]{1,0:T(8,128)(2,1)S(1)}, bf16[592,384]{1,0:T(8,128)(2,1)S(1)}, u32[]{:S(2)}, u32[]{:S(2)}) collective-permute-start(bf16[592,384]{1,0:T(8,128)(2,1)S(1)} %collective-permute-done.4.refs_5_), channel_id=1, source_target_pairs={{0,16},{16,0},{1,17},{17,1},{2,18},{18,2},{3,19},{19,3},{4,20},{20... | collective-permute-start | bytes 1363976 | tf_op jit(solution)/shard_map/ppermute | solution.py:639
  150.8 25.9 %collective-permute-start.35 = (bf16[2,592,384]{2,1,0:T(8,128)(2,1)S(1)}, bf16[2,592,384]{2,1,0:T(8,128)(2,1)S(1)}, u32[]{:S(2)}, u32[]{:S(2)}) collective-permute-start(bf16[2,592,384]{2,1,0:T(8,128)(2,1)S(1)} %fusion.2), channel_id=1, source_target_pairs={{0,2},{16,17},{1,3},{17,16},{2,0},{18,19},{3,1},{19,18},{4,6},{20,... | collective-permute-start | bytes 2727944 | tf_op jit(solution)/shard_map/ppermute | solution.py:648
  151.9 39.5 %collective-permute-start.39 = (bf16[2,592,384]{2,1,0:T(8,128)(2,1)S(1)}, bf16[2,592,384]{2,1,0:T(8,128)(2,1)S(1)}, u32[]{:S(2)}, u32[]{:S(2)}) collective-permute-start(bf16[2,592,384]{2,1,0:T(8,128)(2,1)S(1)} %fusion.1), channel_id=1, source_target_pairs={{0,2},{16,17},{1,3},{17,16},{2,0},{18,19},{3,1},{19,18},{4,6},{20,... | collective-permute-start | bytes 2727944 | tf_op jit(solution)/shard_map/ppermute | solution.py:648
  154.2 51.7 %collective-permute-start.43 = (bf16[2,592,384]{2,1,0:T(8,128)(2,1)S(1)}, bf16[2,592,384]{2,1,0:T(8,128)(2,1)S(1)}, u32[]{:S(2)}, u32[]{:S(2)}) collective-permute-start(bf16[2,592,384]{2,1,0:T(8,128)(2,1)S(1)} %fusion), channel_id=1, source_target_pairs={{0,2},{16,17},{1,3},{17,16},{2,0},{18,19},{3,1},{19,18},{4,6},{20,... | collective-permute-start | bytes 2727944 | tf_op jit(solution)/shard_map/ppermute | solution.py:648
  162.4 61.1 %collective-permute-start.33 = (bf16[592,384]{1,0:T(8,128)(2,1)S(1)}, bf16[592,384]{1,0:T(8,128)(2,1)S(1)}, u32[]{:S(2)}, u32[]{:S(2)}) collective-permute-start(bf16[592,384]{1,0:T(8,128)(2,1)S(1)} %fusion.23), channel_id=1, source_target_pairs={{0,1},{16,18},{1,0},{17,19},{2,3},{18,16},{3,2},{19,17},{4,5},{20,... | collective-permute-start | bytes 1363976 | tf_op jit(solution)/shard_map/ppermute | solution.py:650
  177.0 30.8 %collective-permute-start.36 = (bf16[592,384]{1,0:T(8,128)(2,1)S(1)}, bf16[592,384]{1,0:T(8,128)(2,1)S(1)}, u32[]{:S(2)}, u32[]{:S(2)}) collective-permute-start(bf16[592,384]{1,0:T(8,128)(2,1)S(1)} %fusion.24), channel_id=1, source_target_pairs={{0,1},{16,18},{1,0},{17,19},{2,3},{18,16},{3,2},{19,17},{4,5},{20,... | collective-permute-start | bytes 1363976 | tf_op jit(solution)/shard_map/ppermute | solution.py:650
  191.6 27.7 %collective-permute-start.40 = (bf16[592,384]{1,0:T(8,128)(2,1)S(1)}, bf16[592,384]{1,0:T(8,128)(2,1)S(1)}, u32[]{:S(2)}, u32[]{:S(2)}) collective-permute-start(bf16[592,384]{1,0:T(8,128)(2,1)S(1)} %fusion.25), channel_id=1, source_target_pairs={{0,1},{16,18},{1,0},{17,19},{2,3},{18,16},{3,2},{19,17},{4,5},{20,... | collective-permute-start | bytes 1363976 | tf_op jit(solution)/shard_map/ppermute | solution.py:650
  208.0 22.2 %collective-permute-start.37 = (bf16[592,384]{1,0:T(8,128)(2,1)S(1)}, bf16[592,384]{1,0:T(8,128)(2,1)S(1)}, u32[]{:S(2)}, u32[]{:S(2)}) collective-permute-start(bf16[592,384]{1,0:T(8,128)(2,1)S(1)} %fusion.16), channel_id=1, source_target_pairs={{0,12},{1,13},{2,14},{3,15},{4,0},{5,1},{6,2},{7,3},{8,4},{9,5},{1... | collective-permute-start | bytes 1363976 | tf_op jit(solution)/shard_map/ppermute | solution.py:653
  219.5 37.1 %collective-permute-start.41 = (bf16[592,384]{1,0:T(8,128)(2,1)S(1)}, bf16[592,384]{1,0:T(8,128)(2,1)S(1)}, u32[]{:S(2)}, u32[]{:S(2)}) collective-permute-start(bf16[592,384]{1,0:T(8,128)(2,1)S(1)} %fusion.12), channel_id=1, source_target_pairs={{0,8},{1,9},{2,10},{3,11},{4,12},{5,13},{6,14},{7,15},{8,0},{9,1},... | collective-permute-start | bytes 1363976 | tf_op jit(solution)/shard_map/ppermute | solution.py:653
  219.8 36.8 %collective-permute-start.45 = (bf16[592,384]{1,0:T(8,128)(2,1)S(1)}, bf16[592,384]{1,0:T(8,128)(2,1)S(1)}, u32[]{:S(2)}, u32[]{:S(2)}) collective-permute-start(bf16[592,384]{1,0:T(8,128)(2,1)S(1)} %fusion.8), channel_id=1, source_target_pairs={{0,4},{1,5},{2,6},{3,7},{4,8},{5,9},{6,10},{7,11},{8,12},{9,13},{1... | collective-permute-start | bytes 1363976 | tf_op jit(solution)/shard_map/ppermute | solution.py:653
  (51 other events, 878.9 us)

commit v2 on v1

--- a/solution.py
+++ b/solution.py
@@ -629,8 +629,11 @@
 
     own = make_frame(params, shape_meta)
     mine, other = [], []
+    up = [(s, (s + 4) % n) for s in range(n)]
+    down = [(s, (s - 4) % n) for s in range(n)]
+    zero = None
     for t in range(4):
-        zero = own if t == 0 else lax.ppermute(own, "shard", [(s, (s + 4 * t) % n) for s in range(n)])
+        zero = own if t == 0 else lax.ppermute(zero, "shard", up)
         one = lax.ppermute(zero, both, near)
         two = lax.ppermute(zero, both, far)
         three = lax.ppermute(one, both, far)
@@ -640,20 +643,24 @@
 
     block_out, input_grad, keeps, sends = run_layer(layer_meta, hidden_states, cotangent, mine + other)
 
-    total = None
-    for t in range(4):
+    far_done = {}
+    passed = None
+    for t in (3, 2, 1, 0):
         keep = keeps[t].astype(f32)
-        got = lax.ppermute(sends[t], "rep", swap).astype(f32)
+        send = sends[t]
+        if t < 2:
+            send, _ = lax.optimization_barrier((send, far_done[t + 2]))
+        got = lax.ppermute(send, "rep", swap).astype(f32)
         away = (keep[2:4] + got[2:4]).astype(bf16)
-        from_far = lax.ppermute(away, both, far).astype(f32)
+        far_done[t] = lax.ppermute(away, both, far)
+        from_far = far_done[t].astype(f32)
         away = (keep[1] + got[1] + from_far[1]).astype(bf16)
         from_near = lax.ppermute(away, both, near).astype(f32)
-        partial = keep[0] + got[0] + from_far[0] + from_near
+        total = keep[0] + got[0] + from_far[0] + from_near
+        if passed is not None:
+            total = total + passed
         if t > 0:
-            partial = lax.ppermute(
-                partial.astype(bf16), "shard", [(s, (s - 4 * t) % n) for s in range(n)]
-            ).astype(f32)
-        total = partial if total is None else total + partial
+            passed = lax.ppermute(total.astype(bf16), "shard", down).astype(f32)
     weight_grad = take_frame(total, lax.ppermute(total, "rep", swap), shape_meta)
     new_params, new_first, new_second = adamw(params, first_moment, second_moment, weight_grad)
     return (block_out, input_grad, weight_grad, new_params, new_first, new_second)

time: 270 us -> 215 us (0.80)
  waiting for transfers between devices: 146 us -> 117 us
  starting transfers between devices: 56.7 us -> 32.3 us
    ppermute x14, waiting for transfers between devices: 103 us -> 63.9 us  [the longest x4 30.6 us: on_device_planes(): far_done[t] = lax.ppermute(away, both, far)]
    ppermute x4, waiting for transfers between devices: 0.01 us -> 22.6 us  [on_device_planes(): from_near = lax.ppermute(away, both, near).astype(f32)]
    ppermute x14, starting transfers between devices: 28.4 us -> 9.1 us  [the longest x3 3.27 us: on_device_planes(): zero = own if t == 0 else lax.ppermute(zero, 'shard', up)]
    ppermute x4, waiting for transfers between devices: 20.2 us -> 3.8 us  [on_device_planes(): one = lax.ppermute(zero, both, near)]
    ppermute x4, waiting for transfers between devices: 14.1 us -> 22 us  [on_device_planes(): three = lax.ppermute(one, both, far)]
  transfers between devices with their start and end apart: 47 -> 47, of which waited for: 21 -> 22; matrix products, arithmetic and copies ran while one was open for 3% -> 3% of each run, Pallas kernels for 0% -> 0%
where the time goes in v2:
time: 215 us
  waiting for transfers between devices  117 us (54%)
  Pallas kernels  44.8 us (21%)
  starting transfers between devices  32.3 us (15%)
  other arithmetic  12.9 us (6%)
  local copies, waits for them, and re-layouts  5.45 us (3%)
    pallas_call x1, Pallas kernels, run_layer(): pl.pallas_call(layer_kernel, out_shape=[jax.ShapeDtypeStruct((rows, D), b...  37.7 us
    ppermute x4, waiting for transfers between devices, on_device_planes(): far_done[t] = lax.ppermute(away, both, far)  30.6 us
    ppermute x3, waiting for transfers between devices, on_device_planes(): zero = own if t == 0 else lax.ppermute(zero, 'shard', up)  25.3 us
    ppermute x4, waiting for transfers between devices, on_device_planes(): from_near = lax.ppermute(away, both, near).astype(f32)  22.6 us
    ppermute x4, waiting for transfers between devices, on_device_planes(): three = lax.ppermute(one, both, far)  22 us
    ppermute x4, starting transfers between devices, on_device_planes(): one = lax.ppermute(zero, both, near)  5.86 us
    sub x1, other arithmetic, adamw(): param_now - learn_rate * (first_new / fix_one / (jnp.sqrt(second_new / fi...  5.85 us
    ppermute x3, waiting for transfers between devices, on_device_planes(): passed = lax.ppermute(total.astype(bf16), 'shard', down).astype(f32)  5.61 us
  transfers between devices with their start and end apart: 47, of which 22 were waited for; matrix products, arithmetic and copies ran while one was open for 3% of the time, Pallas kernels for 0%

profile of v2, /device:TPU:0, one launch (start us, length us, event | category | flops | bytes accessed | tf_op | source)
XLA Modules:
  0.0 214.7 jit_solution(5103825783676272312)
XLA Ops:
  0.6 2.8 %pad_bitcast_fusion.flat_ref = f32[3464,128]{1,0:T(8,128)} fusion(f32[442944]{0:T(1024)} %param.10), kind=kLoop, calls=%fused_computation.12 | loop fusion | bytes 3545344 | tf_op jit(solution)/shard_map/reshape | solution.py:272
  4.1 3.3 %shard_map.118.refs_0_ = bf16[592,384]{1,0:T(8,128)(2,1)} custom-call(s32[4]{0:T(128)} %pad_add_fusion.meta, f32[3464,128]{1,0:T(8,128)} %pad_bitcast_fusion.flat_ref), custom_call_target="tpu_custom_call" | custom-call | tf_op jit(solution)/shard_map/pallas_call | solution.py:273
  7.4 3.0 %collective-permute-start.3 = (bf16[592,384]{1,0:T(8,128)(2,1)}, bf16[592,384]{1,0:T(8,128)(2,1)S(1)}, u32[]{:S(2)}, u32[]{:S(2)}) collective-permute-start(bf16[592,384]{1,0:T(8,128)(2,1)} %shard_map.118.refs_0_), channel_id=1, source_target_pairs={{0,4},{1,5},{2,6},{3,7},{4,8},{5,9},{6,10},{7,11},{8,12},{9,13},{1... | collective-permute-start | bytes 1363976 | tf_op jit(solution)/shard_map/ppermute | solution.py:636
  13.4 9.6 %collective-permute-done.3.refs_4_ = bf16[592,384]{1,0:T(8,128)(2,1)S(1)} collective-permute-done((bf16[592,384]{1,0:T(8,128)(2,1)}, bf16[592,384]{1,0:T(8,128)(2,1)S(1)}, u32[]{:S(2)}, u32[]{:S(2)}) %collective-permute-start.3) | collective-permute-done | bytes 454688 | tf_op jit(solution)/shard_map/ppermute | solution.py:636
  26.7 11.0 %collective-permute-done.7.refs_8_ = bf16[592,384]{1,0:T(8,128)(2,1)S(1)} collective-permute-done((bf16[592,384]{1,0:T(8,128)(2,1)S(1)}, bf16[592,384]{1,0:T(8,128)(2,1)S(1)}, u32[]{:S(2)}, u32[]{:S(2)}) %collective-permute-start.7) | collective-permute-done | bytes 454688 | tf_op jit(solution)/shard_map/ppermute | solution.py:636
  41.6 7.0 %collective-permute-done.2.refs_3_ = bf16[592,384]{1,0:T(8,128)(2,1)S(1)} collective-permute-done((bf16[592,384]{1,0:T(8,128)(2,1)S(1)}, bf16[592,384]{1,0:T(8,128)(2,1)S(1)}, u32[]{:S(2)}, u32[]{:S(2)}) %collective-permute-start.2) | collective-permute-done | bytes 454688 | tf_op jit(solution)/shard_map/ppermute | solution.py:639
  49.2 4.7 %collective-permute-done.11.refs_12_ = bf16[592,384]{1,0:T(8,128)(2,1)S(1)} collective-permute-done((bf16[592,384]{1,0:T(8,128)(2,1)S(1)}, bf16[592,384]{1,0:T(8,128)(2,1)S(1)}, u32[]{:S(2)}, u32[]{:S(2)}) %collective-permute-start.11) | collective-permute-done | bytes 454688 | tf_op jit(solution)/shard_map/ppermute | solution.py:636
  59.6 5.9 %collective-permute-done.6.refs_7_ = bf16[592,384]{1,0:T(8,128)(2,1)S(1)} collective-permute-done((bf16[592,384]{1,0:T(8,128)(2,1)S(1)}, bf16[592,384]{1,0:T(8,128)(2,1)S(1)}, u32[]{:S(2)}, u32[]{:S(2)}) %collective-permute-start.6) | collective-permute-done | bytes 454688 | tf_op jit(solution)/shard_map/ppermute | solution.py:639
  66.1 3.8 %collective-permute-done.12.refs_13_ = bf16[592,384]{1,0:T(8,128)(2,1)S(1)} collective-permute-done((bf16[592,384]{1,0:T(8,128)(2,1)S(1)}, bf16[592,384]{1,0:T(8,128)(2,1)S(1)}, u32[]{:S(2)}, u32[]{:S(2)}) %collective-permute-start.12) | collective-permute-done | bytes 454688 | tf_op jit(solution)/shard_map/ppermute | solution.py:637
  72.8 4.3 %collective-permute-done.10.refs_11_ = bf16[592,384]{1,0:T(8,128)(2,1)} collective-permute-done((bf16[592,384]{1,0:T(8,128)(2,1)S(1)}, bf16[592,384]{1,0:T(8,128)(2,1)}, u32[]{:S(2)}, u32[]{:S(2)}) %collective-permute-start.10) | collective-permute-done | bytes 454688 | tf_op jit(solution)/shard_map/ppermute | solution.py:639
  77.1 4.9 %collective-permute-done.14.refs_15_ = bf16[592,384]{1,0:T(8,128)(2,1)} collective-permute-done((bf16[592,384]{1,0:T(8,128)(2,1)S(1)}, bf16[592,384]{1,0:T(8,128)(2,1)}, u32[]{:S(2)}, u32[]{:S(2)}) %collective-permute-start.14) | collective-permute-done | bytes 454688 | tf_op jit(solution)/shard_map/ppermute | solution.py:639
  84.2 37.7 %shard_map.119 = (bf16[128,768]{1,0:T(8,128)(2,1)}, bf16[128,768]{1,0:T(8,128)(2,1)}, bf16[4,592,384]{2,1,0:T(8,128)(2,1)}, bf16[4,592,384]{2,1,0:T(8,128)(2,1)}...) custom-call(s32[35]{0:T(128)} %concatenate.3.meta, ...), custom_call_target="tpu_custom_call" | custom-call | tf_op jit(solution)/shard_map/pallas_call | solution.py:569
  124.2 1.7 collective-permute-done.36
  129.8 10.0 %collective-permute-done.37 = bf16[2,592,384]{2,1,0:T(8,128)(2,1)S(1)} collective-permute-done((bf16[2,592,384]{2,1,0:T(8,128)(2,1)S(1)}, bf16[2,592,384]{2,1,0:T(8,128)(2,1)S(1)}, u32[]{:S(2)}, u32[]{:S(2)}) %collective-permute-start.37) | collective-permute-done | bytes 909344 | tf_op jit(solution)/shard_map/ppermute | solution.py:655
  139.8 9.7 %collective-permute-done.32 = bf16[2,592,384]{2,1,0:T(8,128)(2,1)S(1)} collective-permute-done((bf16[2,592,384]{2,1,0:T(8,128)(2,1)S(1)}, bf16[2,592,384]{2,1,0:T(8,128)(2,1)S(1)}, u32[]{:S(2)}, u32[]{:S(2)}) %collective-permute-start.32) | collective-permute-done | bytes 909344 | tf_op jit(solution)/shard_map/ppermute | solution.py:655
  155.2 7.7 %collective-permute-done.42 = bf16[592,384]{1,0:T(8,128)(2,1)S(1)} collective-permute-done((bf16[592,384]{1,0:T(8,128)(2,1)S(1)}, bf16[592,384]{1,0:T(8,128)(2,1)S(1)}, u32[]{:S(2)}, u32[]{:S(2)}) %collective-permute-start.42) | collective-permute-done | bytes 454688 | tf_op jit(solution)/shard_map/ppermute | solution.py:658
  164.5 8.2 %collective-permute-done.41 = bf16[592,384]{1,0:T(8,128)(2,1)S(1)} collective-permute-done((bf16[592,384]{1,0:T(8,128)(2,1)S(1)}, bf16[592,384]{1,0:T(8,128)(2,1)S(1)}, u32[]{:S(2)}, u32[]{:S(2)}) %collective-permute-start.41) | collective-permute-done | bytes 454688 | tf_op jit(solution)/shard_map/ppermute | solution.py:658
  174.0 2.1 collective-permute-start.44
  178.0 10.8 %collective-permute-done.34 = bf16[2,592,384]{2,1,0:T(8,128)(2,1)S(1)} collective-permute-done((bf16[2,592,384]{2,1,0:T(8,128)(2,1)S(1)}, bf16[2,592,384]{2,1,0:T(8,128)(2,1)S(1)}, u32[]{:S(2)}, u32[]{:S(2)}) %collective-permute-start.34) | collective-permute-done | bytes 909344 | tf_op jit(solution)/shard_map/ppermute | solution.py:655
  191.0 6.6 %collective-permute-done.35 = bf16[592,384]{1,0:T(8,128)(2,1)S(1)} collective-permute-done((bf16[592,384]{1,0:T(8,128)(2,1)S(1)}, bf16[592,384]{1,0:T(8,128)(2,1)S(1)}, u32[]{:S(2)}, u32[]{:S(2)}) %collective-permute-start.35) | collective-permute-done | bytes 454688 | tf_op jit(solution)/shard_map/ppermute | solution.py:658
  197.6 4.6 %collective-permute-done.45 = bf16[592,384]{1,0:T(8,128)(2,1)S(1)} collective-permute-done((bf16[592,384]{1,0:T(8,128)(2,1)S(1)}, bf16[592,384]{1,0:T(8,128)(2,1)S(1)}, u32[]{:S(2)}, u32[]{:S(2)}) %collective-permute-start.45) | collective-permute-done | bytes 454688 | tf_op jit(solution)/shard_map/ppermute | solution.py:663
  202.5 2.6 %collective-permute-done.46.other_ref = f32[592,384]{1,0:T(8,128)} collective-permute-done((f32[592,384]{1,0:T(8,128)S(1)}, f32[592,384]{1,0:T(8,128)}, u32[]{:S(2)}, u32[]{:S(2)}) %collective-permute-start.46) | collective-permute-done | bytes 909344 | tf_op jit(solution)/shard_map/ppermute | solution.py:664
  205.1 3.8 %shard_map.120 = f32[3464,128]{1,0:T(8,128)} custom-call(s32[4]{0:T(128)} %pad_add_fusion.meta, f32[592,384]{1,0:T(8,128)} %copy-done.1, f32[592,384]{1,0:T(8,128)} %collective-permute-done.46.other_ref), custom_call_target="tpu_custom_call" | custom-call | tf_op jit(solution)/shard_map/pallas_call | solution.py:301
  208.9 5.9 %multiply_subtract_fusion = (f32[442944]{0:T(1024)}, f32[442944]{0:T(1024)}, f32[442944]{0:T(1024)}, f32[442944]{0:T(1024)}) fusion(f32[442944]{0:T(1024)S(1)} %copy-done, f32[442944]{0:T(1024)} %param.11, f32[442944]{0:T(1024)} %param.12, f32[443392]{0:T(1024)} %bitcast.49), kind=kLoop, calls=%fused_computation.10 | loop fusion | flops 6644160 | bytes 14174208 | tf_op jit(solution)/shard_map/sub | solution.py:228
  (170 shorter events, 41.0 us)
Async XLA Ops:
  7.4 15.7 %collective-permute-start.3 = (bf16[592,384]{1,0:T(8,128)(2,1)}, bf16[592,384]{1,0:T(8,128)(2,1)S(1)}, u32[]{:S(2)}, u32[]{:S(2)}) collective-permute-start(bf16[592,384]{1,0:T(8,128)(2,1)} %shard_map.118.refs_0_), channel_id=1, source_target_pairs={{0,4},{1,5},{2,6},{3,7},{4,8},{5,9},{6,10},{7,11},{8,12},{9,13},{1... | collective-permute-start | bytes 1363976 | tf_op jit(solution)/shard_map/ppermute | solution.py:636
  10.4 12.7 %collective-permute-start.15 = (bf16[592,384]{1,0:T(8,128)(2,1)}, bf16[592,384]{1,0:T(8,128)(2,1)S(1)}, u32[]{:S(2)}, u32[]{:S(2)}) collective-permute-start(bf16[592,384]{1,0:T(8,128)(2,1)} %shard_map.118.refs_0_), channel_id=1, source_target_pairs={{0,16},{16,0},{1,17},{17,1},{2,18},{18,2},{3,19},{19,3},{4,20},{20... | collective-permute-start | bytes 1363976 | tf_op jit(solution)/shard_map/ppermute | solution.py:642
  10.4 14.3 %collective-permute-start.1 = (bf16[592,384]{1,0:T(8,128)(2,1)}, bf16[592,384]{1,0:T(8,128)(2,1)S(1)}, u32[]{:S(2)}, u32[]{:S(2)}) collective-permute-start(bf16[592,384]{1,0:T(8,128)(2,1)} %shard_map.118.refs_0_), channel_id=1, source_target_pairs={{0,2},{16,17},{1,3},{17,16},{2,0},{18,19},{3,1},{19,18},{4,6},{20,... | collective-permute-start | bytes 1363976 | tf_op jit(solution)/shard_map/ppermute | solution.py:638
  11.9 14.3 %collective-permute-start = (bf16[592,384]{1,0:T(8,128)(2,1)}, bf16[592,384]{1,0:T(8,128)(2,1)S(1)}, u32[]{:S(2)}, u32[]{:S(2)}) collective-permute-start(bf16[592,384]{1,0:T(8,128)(2,1)} %shard_map.118.refs_0_), channel_id=1, source_target_pairs={{0,1},{16,18},{1,0},{17,19},{2,3},{18,16},{3,2},{19,17},{4,5},{20,... | collective-permute-start | bytes 1363976 | tf_op jit(solution)/shard_map/ppermute | solution.py:637
  23.1 14.6 %collective-permute-start.7 = (bf16[592,384]{1,0:T(8,128)(2,1)S(1)}, bf16[592,384]{1,0:T(8,128)(2,1)S(1)}, u32[]{:S(2)}, u32[]{:S(2)}) collective-permute-start(bf16[592,384]{1,0:T(8,128)(2,1)S(1)} %collective-permute-done.3.refs_4_), channel_id=1, source_target_pairs={{0,4},{1,5},{2,6},{3,7},{4,8},{5,9},{6,10},{7,11},{8,12},{9,13},{1... | collective-permute-start | bytes 1363976 | tf_op jit(solution)/shard_map/ppermute | solution.py:636
  23.1 16.1 %collective-permute-start.5 = (bf16[592,384]{1,0:T(8,128)(2,1)S(1)}, bf16[592,384]{1,0:T(8,128)(2,1)S(1)}, u32[]{:S(2)}, u32[]{:S(2)}) collective-permute-start(bf16[592,384]{1,0:T(8,128)(2,1)S(1)} %collective-permute-done.3.refs_4_), channel_id=1, source_target_pairs={{0,2},{16,17},{1,3},{17,16},{2,0},{18,19},{3,1},{19,18},{4,6},{20,... | collective-permute-start | bytes 1363976 | tf_op jit(solution)/shard_map/ppermute | solution.py:638
  24.7 14.6 %collective-permute-start.4 = (bf16[592,384]{1,0:T(8,128)(2,1)S(1)}, bf16[592,384]{1,0:T(8,128)(2,1)S(1)}, u32[]{:S(2)}, u32[]{:S(2)}) collective-permute-start(bf16[592,384]{1,0:T(8,128)(2,1)S(1)} %collective-permute-done.3.refs_4_), channel_id=1, source_target_pairs={{0,1},{16,18},{1,0},{17,19},{2,3},{18,16},{3,2},{19,17},{4,5},{20,... | collective-permute-start | bytes 1363976 | tf_op jit(solution)/shard_map/ppermute | solution.py:637
  26.2 13.3 %collective-permute-start.17 = (bf16[592,384]{1,0:T(8,128)(2,1)S(1)}, bf16[592,384]{1,0:T(8,128)(2,1)S(1)}, u32[]{:S(2)}, u32[]{:S(2)}) collective-permute-start(bf16[592,384]{1,0:T(8,128)(2,1)S(1)} %collective-permute-done.1.refs_2_), channel_id=1, source_target_pairs={{0,16},{16,0},{1,17},{17,1},{2,18},{18,2},{3,19},{19,3},{4,20},{20... | collective-permute-start | bytes 1363976 | tf_op jit(solution)/shard_map/ppermute | solution.py:642
  26.2 14.1 %collective-permute-start.16 = (bf16[592,384]{1,0:T(8,128)(2,1)S(1)}, bf16[592,384]{1,0:T(8,128)(2,1)S(1)}, u32[]{:S(2)}, u32[]{:S(2)}) collective-permute-start(bf16[592,384]{1,0:T(8,128)(2,1)S(1)} %collective-permute-done.refs_1_), channel_id=1, source_target_pairs={{0,16},{16,0},{1,17},{17,1},{2,18},{18,2},{3,19},{19,3},{4,20},{20... | collective-permute-start | bytes 1363976 | tf_op jit(solution)/shard_map/ppermute | solution.py:642
  39.3 14.6 %collective-permute-start.11 = (bf16[592,384]{1,0:T(8,128)(2,1)S(1)}, bf16[592,384]{1,0:T(8,128)(2,1)S(1)}, u32[]{:S(2)}, u32[]{:S(2)}) collective-permute-start(bf16[592,384]{1,0:T(8,128)(2,1)S(1)} %collective-permute-done.7.refs_8_), channel_id=1, source_target_pairs={{0,4},{1,5},{2,6},{3,7},{4,8},{5,9},{6,10},{7,11},{8,12},{9,13},{1... | collective-permute-start | bytes 1363976 | tf_op jit(solution)/shard_map/ppermute | solution.py:636
  39.6 16.3 %collective-permute-start.9 = (bf16[592,384]{1,0:T(8,128)(2,1)S(1)}, bf16[592,384]{1,0:T(8,128)(2,1)S(1)}, u32[]{:S(2)}, u32[]{:S(2)}) collective-permute-start(bf16[592,384]{1,0:T(8,128)(2,1)S(1)} %collective-permute-done.7.refs_8_), channel_id=1, source_target_pairs={{0,2},{16,17},{1,3},{17,16},{2,0},{18,19},{3,1},{19,18},{4,6},{20,... | collective-permute-start | bytes 1363976 | tf_op jit(solution)/shard_map/ppermute | solution.py:638
  40.3 15.6 %collective-permute-start.8 = (bf16[592,384]{1,0:T(8,128)(2,1)S(1)}, bf16[592,384]{1,0:T(8,128)(2,1)S(1)}, u32[]{:S(2)}, u32[]{:S(2)}) collective-permute-start(bf16[592,384]{1,0:T(8,128)(2,1)S(1)} %collective-permute-done.7.refs_8_), channel_id=1, source_target_pairs={{0,1},{16,18},{1,0},{17,19},{2,3},{18,16},{3,2},{19,17},{4,5},{20,... | collective-permute-start | bytes 1363976 | tf_op jit(solution)/shard_map/ppermute | solution.py:637
  56.5 13.4 %collective-permute-start.12 = (bf16[592,384]{1,0:T(8,128)(2,1)S(1)}, bf16[592,384]{1,0:T(8,128)(2,1)S(1)}, u32[]{:S(2)}, u32[]{:S(2)}) collective-permute-start(bf16[592,384]{1,0:T(8,128)(2,1)S(1)} %collective-permute-done.11.refs_12_), channel_id=1, source_target_pairs={{0,1},{16,18},{1,0},{17,19},{2,3},{18,16},{3,2},{19,17},{4,5},{20,... | collective-permute-start | bytes 1363976 | tf_op jit(solution)/shard_map/ppermute | solution.py:637
  58.1 14.0 %collective-permute-start.13 = (bf16[592,384]{1,0:T(8,128)(2,1)S(1)}, bf16[592,384]{1,0:T(8,128)(2,1)S(1)}, u32[]{:S(2)}, u32[]{:S(2)}) collective-permute-start(bf16[592,384]{1,0:T(8,128)(2,1)S(1)} %collective-permute-done.11.refs_12_), channel_id=1, source_target_pairs={{0,2},{16,17},{1,3},{17,16},{2,0},{18,19},{3,1},{19,18},{4,6},{20,... | collective-permute-start | bytes 1363976 | tf_op jit(solution)/shard_map/ppermute | solution.py:638
  69.9 12.0 %collective-permute-start.14 = (bf16[592,384]{1,0:T(8,128)(2,1)S(1)}, bf16[592,384]{1,0:T(8,128)(2,1)}, u32[]{:S(2)}, u32[]{:S(2)}) collective-permute-start(bf16[592,384]{1,0:T(8,128)(2,1)S(1)} %collective-permute-done.12.refs_13_), channel_id=1, source_target_pairs={{0,2},{16,17},{1,3},{17,16},{2,0},{18,19},{3,1},{19,18},{4,6},{20,... | collective-permute-start | bytes 1363976 | tf_op jit(solution)/shard_map/ppermute | solution.py:639
  126.4 13.4 %collective-permute-start.37 = (bf16[2,592,384]{2,1,0:T(8,128)(2,1)S(1)}, bf16[2,592,384]{2,1,0:T(8,128)(2,1)S(1)}, u32[]{:S(2)}, u32[]{:S(2)}) collective-permute-start(bf16[2,592,384]{2,1,0:T(8,128)(2,1)S(1)} %fusion.1), channel_id=1, source_target_pairs={{0,2},{16,17},{1,3},{17,16},{2,0},{18,19},{3,1},{19,18},{4,6},{20,... | collective-permute-start | bytes 2727944 | tf_op jit(solution)/shard_map/ppermute | solution.py:655
  129.0 20.5 %collective-permute-start.32 = (bf16[2,592,384]{2,1,0:T(8,128)(2,1)S(1)}, bf16[2,592,384]{2,1,0:T(8,128)(2,1)S(1)}, u32[]{:S(2)}, u32[]{:S(2)}) collective-permute-start(bf16[2,592,384]{2,1,0:T(8,128)(2,1)S(1)} %fusion.3), channel_id=1, source_target_pairs={{0,2},{16,17},{1,3},{17,16},{2,0},{18,19},{3,1},{19,18},{4,6},{20,... | collective-permute-start | bytes 2727944 | tf_op jit(solution)/shard_map/ppermute | solution.py:655
  139.8 14.2 %collective-permute-start.38 = (bf16[4,592,384]{2,1,0:T(8,128)(2,1)S(1)}, bf16[4,592,384]{2,1,0:T(8,128)(2,1)S(1)}, u32[]{:S(2)}, u32[]{:S(2)}) collective-permute-start(bf16[4,592,384]{2,1,0:T(8,128)(2,1)S(1)} %copy-done.31), channel_id=1, source_target_pairs={{0,16},{16,0},{1,17},{17,1},{2,18},{18,2},{3,19},{19,3},{4,20},{20... | collective-permute-start | bytes 5455880 | tf_op jit(solution)/shard_map/ppermute | solution.py:653
  149.5 13.7 %collective-permute-start.33 = (bf16[4,592,384]{2,1,0:T(8,128)(2,1)S(1)}, bf16[4,592,384]{2,1,0:T(8,128)(2,1)S(1)}, u32[]{:S(2)}, u32[]{:S(2)}) collective-permute-start(bf16[4,592,384]{2,1,0:T(8,128)(2,1)S(1)} %copy-done.30), channel_id=1, source_target_pairs={{0,16},{16,0},{1,17},{17,1},{2,18},{18,2},{3,19},{19,3},{4,20},{20... | collective-permute-start | bytes 5455880 | tf_op jit(solution)/shard_map/ppermute | solution.py:653
  153.4 19.3 %collective-permute-start.41 = (bf16[592,384]{1,0:T(8,128)(2,1)S(1)}, bf16[592,384]{1,0:T(8,128)(2,1)S(1)}, u32[]{:S(2)}, u32[]{:S(2)}) collective-permute-start(bf16[592,384]{1,0:T(8,128)(2,1)S(1)} %fusion.25), channel_id=1, source_target_pairs={{0,1},{16,18},{1,0},{17,19},{2,3},{18,16},{3,2},{19,17},{4,5},{20,... | collective-permute-start | bytes 1363976 | tf_op jit(solution)/shard_map/ppermute | solution.py:658
  154.5 21.7 %collective-permute-start.39 = (bf16[2,592,384]{2,1,0:T(8,128)(2,1)S(1)}, bf16[2,592,384]{2,1,0:T(8,128)(2,1)S(1)}, u32[]{:S(2)}, u32[]{:S(2)}) collective-permute-start(bf16[2,592,384]{2,1,0:T(8,128)(2,1)S(1)} %fusion), channel_id=1, source_target_pairs={{0,2},{16,17},{1,3},{17,16},{2,0},{18,19},{3,1},{19,18},{4,6},{20,... | collective-permute-start | bytes 2727944 | tf_op jit(solution)/shard_map/ppermute | solution.py:655
  163.8 25.1 %collective-permute-start.34 = (bf16[2,592,384]{2,1,0:T(8,128)(2,1)S(1)}, bf16[2,592,384]{2,1,0:T(8,128)(2,1)S(1)}, u32[]{:S(2)}, u32[]{:S(2)}) collective-permute-start(bf16[2,592,384]{2,1,0:T(8,128)(2,1)S(1)} %fusion.2), channel_id=1, source_target_pairs={{0,2},{16,17},{1,3},{17,16},{2,0},{18,19},{3,1},{19,18},{4,6},{20,... | collective-permute-start | bytes 2727944 | tf_op jit(solution)/shard_map/ppermute | solution.py:655
  174.0 16.7 %collective-permute-start.44 = (bf16[592,384]{1,0:T(8,128)(2,1)S(1)}, bf16[592,384]{1,0:T(8,128)(2,1)S(1)}, u32[]{:S(2)}, u32[]{:S(2)}) collective-permute-start(bf16[592,384]{1,0:T(8,128)(2,1)S(1)} %fusion.13), channel_id=1, source_target_pairs={{0,12},{1,13},{2,14},{3,15},{4,0},{5,1},{6,2},{7,3},{8,4},{9,5},{1... | collective-permute-start | bytes 1363976 | tf_op jit(solution)/shard_map/ppermute | solution.py:663
  176.4 14.2 %collective-permute-start.40 = (bf16[592,384]{1,0:T(8,128)(2,1)S(1)}, bf16[592,384]{1,0:T(8,128)(2,1)S(1)}, u32[]{:S(2)}, u32[]{:S(2)}) collective-permute-start(bf16[592,384]{1,0:T(8,128)(2,1)S(1)} %fusion.24), channel_id=1, source_target_pairs={{0,1},{16,18},{1,0},{17,19},{2,3},{18,16},{3,2},{19,17},{4,5},{20,... | collective-permute-start | bytes 1363976 | tf_op jit(solution)/shard_map/ppermute | solution.py:658
  (55 other events, 865.2 us)

commit v3 on v2

--- a/solution.py
+++ b/solution.py
@@ -1,7 +1,9 @@
+import functools
 import math
 
 import jax
 import jax.numpy as jnp
+import numpy as np
 from jax import lax
 from jax.experimental import pallas as pl
 from jax.experimental.pallas import tpu as pltpu
@@ -242,6 +244,8 @@
 EXP_ROW = 3072
 RED_ROW = 6144
 BIAS_ROW = 9216
+LEFT = 4608
+RIGHT = 9 * HALF
 VMEM_CAP = 64 * 1024 * 1000
 
 f32 = jnp.float32
@@ -320,60 +324,65 @@
     return jnp.mean(block, axis=-1, keepdims=True)
 
 
-def layer_kernel(meta, tokens_ref, cot_ref, *refs):
+def layer_kernel(meta, length_ref, tokens_ref, cot_ref, *refs):
     frames = refs[:32]
-    block_ref, input_ref = refs[32:34]
-    keeps = refs[34:38]
-    sends = refs[38:42]
+    block_ref, input_ref, left_ref, right_ref, sums_ref = refs[32:37]
     (
         weights,
-        grads,
         triple_w,
         expand_w,
         tails,
         stage,
         triple_b,
         soft_all,
-        context_b,
-        act_b,
         slope_all,
-        pre_b,
-        d_triple_b,
-        bias_grads,
+        rights,
         sem_main,
         sem_tail,
-        sem_out,
-    ) = refs[42:]
-    length = meta[0]
-    cols = (pl.multiple_of(meta[1], 128), pl.multiple_of(meta[2], 128))
-
-    arrivals = []
-    for side in range(2):
-        for k in range(16):
-            frame = frames[16 * side + k]
-            shard = meta[3 + 16 * side + k]
-            row = pl.multiple_of(shard * STEP_ROWS, 16)
-            main_copy = pltpu.make_async_copy(
-                frame.at[pl.ds(0, STEP_ROWS), :],
-                weights.at[pl.ds(row, STEP_ROWS), pl.ds(cols[side], HALF)],
-                sem_main.at[side, k],
-            )
-            tail_copy = pltpu.make_async_copy(
-                frame.at[pl.ds(STEP_ROWS, 16), :],
-                tails.at[shard, :, pl.ds(cols[side], HALF)],
-                sem_tail.at[side, k],
-            )
-            main_copy.start()
-            tail_copy.start()
-            arrivals.append(main_copy)
-            arrivals.append(tail_copy)
-    for copy in arrivals:
-        copy.wait()
-    for s in range(15):
-        at = STEP_ROWS * (s + 1)
-        joined = weights[at : at + 16, :].astype(f32) + tails[s].astype(f32)
-        weights[at : at + 16, :] = joined.astype(bf16)
-    weights[BIAS_ROW : BIAS_ROW + 16, :] = tails[15]
+    ) = refs[37:]
+    bias_grads = sums_ref
+    length = length_ref[0]
+    cols = (pl.multiple_of(meta[4], 128), pl.multiple_of(meta[5], 128))
+
+    def main_copy(frame, shard, side):
+        return pltpu.make_async_copy(
+            frame.at[pl.ds(0, STEP_ROWS), :],
+            weights.at[pl.ds(pl.multiple_of(shard * STEP_ROWS, 16), STEP_ROWS), pl.ds(cols[side], HALF)],
+            sem_main.at[side, shard],
+        )
+
+    def tail_copy(frame, shard, side):
+        return pltpu.make_async_copy(
+            frame.at[pl.ds(STEP_ROWS, 16), :],
+            tails.at[shard, :, pl.ds(cols[side], HALF)],
+            sem_tail.at[side, shard],
+        )
+
+    for quad in range(4):
+        for t in range(4):
+
+            @pl.when(meta[6 + quad] == t)
+            def _():
+                for side in range(2):
+                    for j in range(4):
+                        shard = 4 * quad + meta[10 + 4 * side + j]
+                        tail_copy(frames[16 * side + 4 * t + j], shard, side).start()
+                        main_copy(frames[16 * side + 4 * t + j], shard, side).start()
+
+    for shard in range(16):
+        for side in range(2):
+            tail_copy(frames[0], shard, side).wait()
+
+    def arrive(first, last):
+        for shard in range(first, last):
+            for side in range(2):
+                main_copy(frames[0], shard, side).wait()
+            if shard > 0:
+                at = STEP_ROWS * shard
+                joined = weights[at : at + 16, :].astype(f32) + tails[shard - 1].astype(f32)
+                weights[at : at + 16, :] = joined.astype(bf16)
+
+    arrive(0, 4)
 
     def spread_triple(i, carry):
         for j in range(6):
@@ -396,9 +405,7 @@
                 expand_w[part, pl.ds(pl.multiple_of(128 * i, 16), 128), at] = rows.astype(bf16)
         return carry
 
-    lax.fori_loop(0, 6, spread_expand, 0)
-
-    biases = weights[BIAS_ROW : BIAS_ROW + 16, :].astype(f32)
+    biases = tails[15].astype(f32)
 
     def bias(index):
         return biases[index : index + 1, :]
@@ -431,19 +438,24 @@
             soft_float = jnp.exp(scores - log_total)
             soft_all[2 * pair + side] = soft_float
             context = context + dot_nn(soft_float.astype(bf16), value_rows * head_masks[side])
-        context_b[:, at] = context.astype(bf16)
-
-    first_sum = tokens.astype(f32) + dot_nn(context_b[...], weights[OUT_ROW : OUT_ROW + 768, :]) + bias(2)
+        left_ref[:, at] = context.astype(bf16)
+
+    arrive(4, 6)
+    first_sum = tokens.astype(f32) + dot_nn(left_ref[:, 0:768], weights[OUT_ROW : OUT_ROW + 768, :]) + bias(2)
     normed_one, root_one = normalize(first_sum)
     middle = normed_one * bias(3) + bias(4)
     middle_b = middle.astype(bf16)
+    left_ref[:, 768:1536] = middle_b
     second_sum = middle + bias(9)
+    arrive(6, 11)
+    lax.fori_loop(0, 6, spread_expand, 0)
+    arrive(11, 16)
     for part in range(4):
         at = slice(768 * part, 768 * (part + 1))
         pre_act = dot_nn(middle_b, expand_w[part]) + bias(5 + part)
         erf_term = 1.0 + lax.erf(pre_act * inv_sqrt_two)
         activated = (0.5 * pre_act * erf_term).astype(bf16)
-        act_b[:, at] = activated
+        left_ref[:, 1536 + 768 * part : 1536 + 768 * (part + 1)] = activated
         slope_all[:, at] = 0.5 * erf_term + pre_act * jnp.exp(-0.5 * pre_act * pre_act) * inv_sqrt_tau
         red_at = RED_ROW + 768 * part
         second_sum = second_sum + dot_nn(activated, weights[red_at : red_at + 768, :])
@@ -463,32 +475,10 @@
         d_pre = by_transpose(d_second_b, weights[red_at : red_at + 768, :]) * slope_all[:, at]
         keep_bias(5 + part, d_pre)
         d_pre_b = d_pre.astype(bf16)
-        pre_b[:, at] = d_pre_b
+        rights[1 + part] = d_pre_b
         d_middle = d_middle + by_transpose(d_pre_b, expand_w[part])
 
-    def reduce_grad(i, carry):
-        at = pl.multiple_of(256 * i, 256)
-        block = inner_rows(act_b[:, pl.ds(at, 256)], d_second_b)
-        grads[pl.ds(pl.multiple_of(RED_ROW + at, 16), 256), :] = block.astype(bf16)
-        return carry
-
-    lax.fori_loop(0, 12, reduce_grad, 0)
-
-    act_b[:, 0:768] = middle_b
-
-    def expand_grad(i, carry):
-        left = act_b[:, pl.ds(pl.multiple_of(128 * i, 128), 128)]
-        for part in range(4):
-            block = inner_rows(left, pre_b[:, 768 * part : 768 * (part + 1)])
-            for j in range(6):
-                stage[j, pl.ds(part, 128, stride=4), :] = block[:, 128 * j : 128 * (j + 1)]
-        row = pl.multiple_of(EXP_ROW + 512 * i, 16)
-        for j in range(6):
-            grads[pl.ds(row, 512), 128 * j : 128 * (j + 1)] = stage[j].astype(bf16)
-        return carry
-
-    lax.fori_loop(0, 6, expand_grad, 0)
-
+    rights[5] = d_second_b
     keep_bias(3, d_middle * normed_one)
     keep_bias(4, d_middle)
     d_first = norm_back(d_middle * bias(3), normed_one, root_one)
@@ -496,14 +486,7 @@
     d_first_b = d_first.astype(bf16)
     d_context_b = by_transpose(d_first_b, weights[OUT_ROW : OUT_ROW + 768, :]).astype(bf16)
 
-    def output_grad(i, carry):
-        at = pl.multiple_of(256 * i, 256)
-        block = inner_rows(context_b[:, pl.ds(at, 256)], d_first_b)
-        grads[pl.ds(pl.multiple_of(OUT_ROW + at, 16), 256), :] = block.astype(bf16)
-        return carry
-
-    lax.fori_loop(0, 3, output_grad, 0)
-
+    rights[0] = d_first_b
     for pair in range(6):
         at = slice(128 * pair, 128 * (pair + 1))
         queries, key_rows, value_rows = triple_b[0, :, at], triple_b[1, :, at], triple_b[2, :, at]
@@ -522,58 +505,37 @@
             d_values = d_values + inner_rows(soft_float.astype(bf16), d_part)
         bias_grads[0:1, at] = jnp.sum(d_query, axis=0, keepdims=True)
         bias_grads[1:2, at] = jnp.sum(d_values, axis=0, keepdims=True)
-        d_triple_b[0, :, at] = d_query.astype(bf16)
-        d_triple_b[1, :, at] = d_keys.astype(bf16)
-        d_triple_b[2, :, at] = d_values.astype(bf16)
+        rights[6, :, at] = d_query.astype(bf16)
+        rights[7, :, at] = d_keys.astype(bf16)
+        rights[8, :, at] = d_values.astype(bf16)
 
     input_grad = d_first
     for part in range(3):
-        input_grad = input_grad + by_transpose(d_triple_b[part], triple_w[part])
+        input_grad = input_grad + by_transpose(rights[6 + part], triple_w[part])
     input_ref[...] = input_grad.astype(bf16)
 
-    def triple_grad(i, carry):
-        left = tokens_ref[:, pl.ds(pl.multiple_of(128 * i, 128), 128)]
-        for part in range(3):
-            block = inner_rows(left, d_triple_b[part])
-            for j in range(6):
-                stage[j, pl.ds(part, 128, stride=3), :] = block[:, 128 * j : 128 * (j + 1)]
-        row = pl.multiple_of(384 * i, 16)
-        for j in range(6):
-            grads[pl.ds(row, 384), 128 * j : 128 * (j + 1)] = stage[j, 0:384, :].astype(bf16)
-        return carry
-
-    lax.fori_loop(0, 6, triple_grad, 0)
-    grads[BIAS_ROW : BIAS_ROW + 16, :] = bias_grads[...].astype(bf16)
-
-    departures = []
-    for side in range(2):
-        for k in range(16):
-            shard = meta[3 + 16 * side + k]
-            row = pl.multiple_of(shard * STEP_ROWS, 16)
-            target = (keeps if side == 0 else sends)[k // 4]
-            copy = pltpu.make_async_copy(
-                grads.at[pl.ds(row, FRAME), pl.ds(cols[side], HALF)],
-                target.at[k % 4],
-                sem_out.at[side, k],
-            )
-            copy.start()
-            departures.append(copy)
-    for copy in departures:
-        copy.wait()
-
-
-def run_layer(meta, tokens, cotangent, frames):
+    for k in range(9):
+        right_ref[:, HALF * k : HALF * (k + 1)] = rights[k, :, pl.ds(cols[0], HALF)]
+        left_ref[:, 4608 + HALF * k : 4608 + HALF * (k + 1)] = rights[k, :, pl.ds(cols[1], HALF)]
+
+
+def run_layer(meta, lengths, tokens, cotangent, frames):
     any_spec = pl.BlockSpec(memory_space=pl.ANY)
     vmem_spec = pl.BlockSpec(memory_space=pltpu.VMEM)
     rows = tokens.shape[0]
+    thin = jax.ShapeDtypeStruct((rows, D), bf16)
     out = pl.pallas_call(
         layer_kernel,
-        out_shape=[jax.ShapeDtypeStruct((rows, D), bf16)] * 2
-        + [jax.ShapeDtypeStruct((4, FRAME, HALF), bf16)] * 8,
-        in_specs=[pl.BlockSpec(memory_space=pltpu.SMEM), vmem_spec, vmem_spec] + [any_spec] * 32,
-        out_specs=[vmem_spec] * 2 + [any_spec] * 8,
+        out_shape=[
+            thin,
+            thin,
+            jax.ShapeDtypeStruct((rows, LEFT + RIGHT), bf16),
+            jax.ShapeDtypeStruct((rows, RIGHT), bf16),
+            jax.ShapeDtypeStruct((16, ROW), f32),
+        ],
+        in_specs=[pl.BlockSpec(memory_space=pltpu.SMEM)] * 2 + [vmem_spec] * 2 + [any_spec] * 32,
+        out_specs=[vmem_spec] * 5,
         scratch_shapes=[
-            pltpu.VMEM((ROWS, ROW), bf16),
             pltpu.VMEM((ROWS, ROW), bf16),
             pltpu.VMEM((3, D, HW), bf16),
             pltpu.VMEM((4, D, ROW), bf16),
@@ -581,19 +543,151 @@
             pltpu.VMEM((6, 512, 128), f32),
             pltpu.VMEM((3, rows, HW), bf16),
             pltpu.VMEM((HEADS, rows, rows), f32),
-            pltpu.VMEM((rows, HW), bf16),
-            pltpu.VMEM((rows, FF), bf16),
             pltpu.VMEM((rows, FF), f32),
-            pltpu.VMEM((rows, FF), bf16),
-            pltpu.VMEM((3, rows, HW), bf16),
-            pltpu.VMEM((16, ROW), f32),
-            pltpu.SemaphoreType.DMA((2, 16)),
+            pltpu.VMEM((9, rows, HW), bf16),
             pltpu.SemaphoreType.DMA((2, 16)),
             pltpu.SemaphoreType.DMA((2, 16)),
         ],
         compiler_params=pltpu.CompilerParams(vmem_limit_bytes=VMEM_CAP),
-    )(meta, tokens, cotangent, *frames)
-    return out[0], out[1], out[2:6], out[6:10]
+    )(meta, lengths, tokens, cotangent, *frames)
+    return out
+
+
+def grad_kernel(
+    slot,
+    meta,
+    tokens_ref,
+    tokens_other,
+    left_ref,
+    left_other,
+    right_ref,
+    sums_ref,
+    sums_other,
+    low_ref,
+    high_ref,
+    left,
+    right,
+    grads,
+    stage,
+    sem_in,
+    sem_out,
+):
+    quad = meta[6 + slot]
+
+    def load(pieces):
+        copies = []
+        for k, (source, first, size, target, at, row) in enumerate(pieces):
+            copies.append(
+                pltpu.make_async_copy(
+                    source.at[:, pl.ds(first, size)],
+                    target.at[pl.ds(row, 128), pl.ds(at, size)],
+                    sem_in.at[k],
+                )
+            )
+        for copy in copies:
+            copy.start()
+        for copy in copies:
+            copy.wait()
+
+    def left_pieces(first, size, at):
+        return [(left_ref, first, size, left, at, 0), (left_other, first, size, left, at, 128)]
+
+    def right_pieces(first, size, at):
+        return [
+            (right_ref, first, size, right, at, 0),
+            (left_other, LEFT + first, size, right, at, 128),
+        ]
+
+    def mixed(first, right_first, parts, chunks, row, rows_used):
+        def step(i, carry):
+            rows = left[:, pl.ds(pl.multiple_of(first + 128 * i, 128), 128)]
+            for part in range(parts):
+                at = right_first + HALF * part
+                block = inner_rows(rows, right[:, at : at + HALF])
+                for j in range(3):
+                    stage[j, pl.ds(part, 128, stride=parts), :] = block[:, 128 * j : 128 * (j + 1)]
+            at = pl.multiple_of(row + 128 * parts * i, 16)
+            for j in range(3):
+                grads[pl.ds(at, rows_used), 128 * j : 128 * (j + 1)] = stage[j, 0:rows_used, :].astype(bf16)
+            return carry
+
+        lax.fori_loop(0, chunks, step, 0)
+
+    def plain(first, right_first, chunks, row):
+        def step(i, carry):
+            rows = left[:, pl.ds(pl.multiple_of(first + 256 * i, 128), 256)]
+            block = inner_rows(rows, right[:, right_first : right_first + HALF])
+            grads[pl.ds(pl.multiple_of(row + 256 * i, 16), 256), :] = block.astype(bf16)
+            return carry
+
+        lax.fori_loop(0, chunks, step, 0)
+
+    def last_rows(first, right_first):
+        block = inner_rows(left[:, first : first + 128], right[:, right_first : right_first + HALF])
+        grads[2304:2320, :] = block[0:16].astype(bf16)
+
+    @pl.when(quad == 0)
+    def _():
+        load(
+            [(tokens_ref, 0, 768, left, 0, 0), (tokens_other, 0, 768, left, 0, 128)]
+            + left_pieces(0, 128, 768)
+            + right_pieces(2304, 1152, 0)
+            + right_pieces(0, 384, 1152)
+        )
+        mixed(0, 0, 3, 6, 0, 384)
+        last_rows(768, 1152)
+
+    @pl.when(quad == 1)
+    def _():
+        load(left_pieces(0, 1280, 0) + right_pieces(0, 1920, 0))
+        plain(0, 0, 3, 0)
+        mixed(768, 384, 4, 3, 768, 512)
+        mixed(1152, 384, 4, 1, 2304, 16)
+
+    @pl.when(quad == 2)
+    def _():
+        load(left_pieces(1152, 1280, 0) + right_pieces(384, 1920, 0))
+        mixed(0, 0, 4, 3, 0, 512)
+        plain(384, 1536, 3, 1536)
+        last_rows(1152, 1536)
+
+    @pl.when(quad == 3)
+    def _():
+        load(left_pieces(2304, 2304, 0) + right_pieces(1920, 384, 0))
+        plain(0, 0, 9, 0)
+        own = pl.ds(pl.multiple_of(meta[4], 128), HALF)
+        grads[2304:2320, :] = (sums_ref[:, own] + sums_other[:, own]).astype(bf16)
+
+    departures = []
+    for j in (2, 3, 0, 1):
+        row = pl.multiple_of(meta[10 + j] * STEP_ROWS, 16)
+        target = (low_ref, high_ref)[j // 2].at[j % 2]
+        copy = pltpu.make_async_copy(grads.at[pl.ds(row, FRAME), :], target, sem_out.at[j])
+        copy.start()
+        departures.append(copy)
+    for copy in departures:
+        copy.wait()
+
+
+def quad_grads(slot, meta, operands):
+    any_spec = pl.BlockSpec(memory_space=pl.ANY)
+    vmem_spec = pl.BlockSpec(memory_space=pltpu.VMEM)
+    frames = jax.ShapeDtypeStruct((2, FRAME, HALF), bf16)
+    return pl.pallas_call(
+        functools.partial(grad_kernel, slot),
+        out_shape=[frames, frames],
+        in_specs=[pl.BlockSpec(memory_space=pltpu.SMEM)] + [any_spec] * 5 + [vmem_spec] * 2,
+        out_specs=[any_spec] * 2,
+        scratch_shapes=[
+            pltpu.VMEM((256, 2304), bf16),
+            pltpu.VMEM((256, 1920), bf16),
+            pltpu.VMEM((4 * STEP_ROWS + 16, HALF), bf16),
+            pltpu.VMEM((3, 512, 128), f32),
+            pltpu.SemaphoreType.DMA((8,)),
+            pltpu.SemaphoreType.DMA((4,)),
+        ],
+        cost_estimate=pl.CostEstimate(flops=1000, bytes_accessed=1000, transcendentals=0),
+    )(meta, *operands)
 
 
 def plane_moves(n):
@@ -604,30 +698,28 @@
     return near, far
 
 
+def device_table(n):
+    rows = []
+    for core in range(2):
+        for here in range(n):
+            plane, spot = divmod(here, 4)
+            spots = ((0, 1, 2, 3), (0, 2, 1, 3))
+            row = [(9 * here) // 2, here % 2, 3 * core, 3 - 3 * core, HALF * core, HALF - HALF * core]
+            row += [(plane - t) % 4 for t in range(4)]
+            row += [spot ^ k for k in spots[core]] + [spot ^ k for k in spots[1 - core]]
+            rows.append(row)
+    return np.array(rows, np.int32)
+
+
 def on_device_planes(hidden_states, cotangent, lengths, params, first_moment, second_moment):
     n = 16
     both = ("rep", "shard")
     near, far = plane_moves(n)
     swap = [(0, 1), (1, 0)]
-    core = lax.axis_index("rep")
-    here = lax.axis_index("shard")
-    plane, spot = here // 4, here % 4
-    shift, odd = (9 * here) // 2, here % 2
-    shape_meta = jnp.stack([shift, odd, 3 * core, 3 - 3 * core]).astype(jnp.int32)
-    spots = jnp.array([[0, 1, 2, 3], [0, 2, 1, 3]], jnp.int32)
-    slots = jnp.arange(4, dtype=jnp.int32)
-    base = ((plane - slots) % 4)[:, None] * 4
-    mine_at = base + (spot ^ spots[core])[None, :]
-    other_at = base + (spot ^ spots[1 - core])[None, :]
-    layer_meta = jnp.concatenate(
-        [
-            jnp.stack([lengths[0], HALF * core, HALF - HALF * core]).astype(jnp.int32),
-            mine_at.reshape(-1),
-            other_at.reshape(-1),
-        ]
-    ).astype(jnp.int32)
-
-    own = make_frame(params, shape_meta)
+    device = lax.axis_index("rep") * n + lax.axis_index("shard")
+    meta = lax.dynamic_slice(jnp.asarray(device_table(n)), (device, 0), (1, 18)).reshape(18)
+
+    own = make_frame(params, meta)
     mine, other = [], []
     up = [(s, (s + 4) % n) for s in range(n)]
     down = [(s, (s - 4) % n) for s in range(n)]
@@ -641,27 +733,29 @@
         mine += group
         other += [lax.ppermute(piece, "rep", swap) for piece in group]
 
-    block_out, input_grad, keeps, sends = run_layer(layer_meta, hidden_states, cotangent, mine + other)
-
-    far_done = {}
+    block_out, input_grad, left, right, sums = run_layer(meta, lengths, hidden_states, cotangent, mine + other)
+
+    operands = (
+        hidden_states,
+        lax.ppermute(hidden_states, "rep", swap),
+        left,
+        lax.ppermute(left, "rep", swap),
+        right,
+        sums,
+        lax.ppermute(sums, "rep", swap),
+    )
     passed = None
     for t in (3, 2, 1, 0):
-        keep = keeps[t].astype(f32)
-        send = sends[t]
-        if t < 2:
-            send, _ = lax.optimization_barrier((send, far_done[t + 2]))
-        got = lax.ppermute(send, "rep", swap).astype(f32)
-        away = (keep[2:4] + got[2:4]).astype(bf16)
-        far_done[t] = lax.ppermute(away, both, far)
-        from_far = far_done[t].astype(f32)
-        away = (keep[1] + got[1] + from_far[1]).astype(bf16)
-        from_near = lax.ppermute(away, both, near).astype(f32)
-        total = keep[0] + got[0] + from_far[0] + from_near
+        low, high = quad_grads(t, meta, operands)
+        from_far = lax.ppermute(high, both, far)
+        away = (low[1].astype(f32) + from_far[1].astype(f32)).astype(bf16)
+        from_near = lax.ppermute(away, both, near)
+        total = low[0].astype(f32) + from_far[0].astype(f32) + from_near.astype(f32)
         if passed is not None:
-            total = total + passed
+            total = total + passed.astype(f32)
         if t > 0:
-            passed = lax.ppermute(total.astype(bf16), "shard", down).astype(f32)
-    weight_grad = take_frame(total, lax.ppermute(total, "rep", swap), shape_meta)
+            passed = lax.ppermute(total.astype(bf16), "shard", down)
+    weight_grad = take_frame(total, lax.ppermute(total, "rep", swap), meta)
     new_params, new_first, new_second = adamw(params, first_moment, second_moment, weight_grad)
     return (block_out, input_grad, weight_grad, new_params, new_first, new_second)
 

time: 215 us -> 198 us (0.921)
  waiting for transfers between devices: 117 us -> 78.2 us
  starting transfers between devices: 32.3 us -> 45.4 us
  Pallas kernels: 44.8 us -> 53.2 us
    ppermute x16 -> x15, waiting for transfers between devices: 63.7 us -> 34.4 us  [the longest x4 19.5 us: on_device_planes(): from_far = lax.ppermute(high, both, far)]
    ppermute x4, waiting for transfers between devices: 22 us -> 8.5 us  [on_device_planes(): three = lax.ppermute(one, both, far)]
    ppermute x16 -> x15, starting transfers between devices: 11.2 us -> 21.4 us  [the longest x3 10.6 us: on_device_planes(): passed = lax.ppermute(total.astype(bf16), 'shard', down)]
    pallas_call x1 -> x5, Pallas kernels: 37.7 us -> 46.1 us  [the longest x4 23.2 us: quad_grads(): pl.pallas_call(functools.partial(grad_kernel, slot), out_shape=[frames, f...]
    ppermute x3, waiting for transfers between devices: 25.3 us -> 28.4 us  [on_device_planes(): zero = own if t == 0 else lax.ppermute(zero, 'shard', up)]
    ppermute x16, starting transfers between devices: 2.88 us -> 5.03 us  [on_device_planes(): other += [lax.ppermute(piece, 'rep', swap) for piece in group]]
    convert_element_type x23 -> x7, other arithmetic: 6.13 us -> 5.34 us  [the longest x3 2.97 us: on_device_planes(): passed = lax.ppermute(total.astype(bf16), 'shard', down)]
  transfers between devices with their start and end apart: 47 -> 46, of which waited for: 22 -> 18; matrix products, arithmetic and copies ran while one was open for 3% -> 3% of each run, Pallas kernels for 0% -> 9%
where the time goes in v3:
time: 198 us; the launch traced here: 197 us
  waiting for transfers between devices  78.2 us (39%)
  Pallas kernels  53.2 us (27%)
  starting transfers between devices  45.4 us (23%)
  other arithmetic  11.4 us (6%)
  local copies, waits for them, and re-layouts  7.3 us (4%)
    ppermute x3, waiting for transfers between devices, on_device_planes(): zero = own if t == 0 else lax.ppermute(zero, 'shard', up)  28.4 us
    pallas_call x4, Pallas kernels, quad_grads(): pl.pallas_call(functools.partial(grad_kernel, slot), out_shape=[frames, f...  23.2 us
    pallas_call x1, Pallas kernels, run_layer(): pl.pallas_call(layer_kernel, out_shape=[thin, thin, jax.ShapeDtypeStruct(...  22.9 us
    ppermute x4, waiting for transfers between devices, on_device_planes(): from_far = lax.ppermute(high, both, far)  19.5 us
    ppermute x3, starting transfers between devices, on_device_planes(): passed = lax.ppermute(total.astype(bf16), 'shard', down)  10.6 us
    ppermute x4, waiting for transfers between devices, on_device_planes(): three = lax.ppermute(one, both, far)  8.5 us
    ppermute x4, starting transfers between devices, on_device_planes(): one = lax.ppermute(zero, both, near)  6.03 us
    ppermute x4, starting transfers between devices, on_device_planes(): two = lax.ppermute(zero, both, far)  5.88 us
  transfers between devices with their start and end apart: 46, of which 18 were waited for; matrix products, arithmetic and copies ran while one was open for 3% of the time, Pallas kernels for 9%

profile of v3, /device:TPU:0, one launch (start us, length us, event | category | flops | bytes accessed | tf_op | source)
XLA Modules:
  0.0 197.2 jit_solution(13149766078318785981)
XLA Ops:
  4.7 3.3 %shard_map.118.refs_0_ = bf16[592,384]{1,0:T(8,128)(2,1)} custom-call(s32[18]{0:T(128)} %dynamic-slice_bitcast_fusion.meta, f32[3464,128]{1,0:T(8,128)} %pad_bitcast_fusion.flat_ref), custom_call_target="tpu_custom_call" | custom-call | tf_op jit(solution)/shard_map/pallas_call | solution.py:277
  8.0 3.0 %collective-permute-start.3 = (bf16[592,384]{1,0:T(8,128)(2,1)}, bf16[592,384]{1,0:T(8,128)(2,1)S(1)}, u32[]{:S(2)}, u32[]{:S(2)}) collective-permute-start(bf16[592,384]{1,0:T(8,128)(2,1)} %shard_map.118.refs_0_), channel_id=1, source_target_pairs={{0,4},{1,5},{2,6},{3,7},{4,8},{5,9},{6,10},{7,11},{8,12},{9,13},{1... | collective-permute-start | bytes 1363976 | tf_op jit(solution)/shard_map/ppermute | solution.py:728
  14.1 9.6 %collective-permute-done.3.refs_4_ = bf16[592,384]{1,0:T(8,128)(2,1)S(1)} collective-permute-done((bf16[592,384]{1,0:T(8,128)(2,1)}, bf16[592,384]{1,0:T(8,128)(2,1)S(1)}, u32[]{:S(2)}, u32[]{:S(2)}) %collective-permute-start.3) | collective-permute-done | bytes 454688 | tf_op jit(solution)/shard_map/ppermute | solution.py:728
  27.3 9.8 %collective-permute-done.7.refs_8_ = bf16[592,384]{1,0:T(8,128)(2,1)S(1)} collective-permute-done((bf16[592,384]{1,0:T(8,128)(2,1)S(1)}, bf16[592,384]{1,0:T(8,128)(2,1)S(1)}, u32[]{:S(2)}, u32[]{:S(2)}) %collective-permute-start.7) | collective-permute-done | bytes 454688 | tf_op jit(solution)/shard_map/ppermute | solution.py:728
  43.0 9.0 %collective-permute-done.11.refs_12_ = bf16[592,384]{1,0:T(8,128)(2,1)S(1)} collective-permute-done((bf16[592,384]{1,0:T(8,128)(2,1)S(1)}, bf16[592,384]{1,0:T(8,128)(2,1)S(1)}, u32[]{:S(2)}, u32[]{:S(2)}) %collective-permute-start.11) | collective-permute-done | bytes 454688 | tf_op jit(solution)/shard_map/ppermute | solution.py:728
  58.7 4.5 %collective-permute-done.12.refs_13_ = bf16[592,384]{1,0:T(8,128)(2,1)S(1)} collective-permute-done((bf16[592,384]{1,0:T(8,128)(2,1)S(1)}, bf16[592,384]{1,0:T(8,128)(2,1)S(1)}, u32[]{:S(2)}, u32[]{:S(2)}) %collective-permute-start.12) | collective-permute-done | bytes 454688 | tf_op jit(solution)/shard_map/ppermute | solution.py:729
  67.1 3.3 %collective-permute-done.10.refs_11_ = bf16[592,384]{1,0:T(8,128)(2,1)S(1)} collective-permute-done((bf16[592,384]{1,0:T(8,128)(2,1)S(1)}, bf16[592,384]{1,0:T(8,128)(2,1)S(1)}, u32[]{:S(2)}, u32[]{:S(2)}) %collective-permute-start.10) | collective-permute-done | bytes 454688 | tf_op jit(solution)/shard_map/ppermute | solution.py:731
  72.1 3.2 %collective-permute-done.14.refs_15_ = bf16[592,384]{1,0:T(8,128)(2,1)S(1)} collective-permute-done((bf16[592,384]{1,0:T(8,128)(2,1)S(1)}, bf16[592,384]{1,0:T(8,128)(2,1)S(1)}, u32[]{:S(2)}, u32[]{:S(2)}) %collective-permute-start.14) | collective-permute-done | bytes 454688 | tf_op jit(solution)/shard_map/ppermute | solution.py:731
  78.5 22.9 %shard_map.119 = (bf16[128,768]{1,0:T(8,128)(2,1)}, bf16[128,768]{1,0:T(8,128)(2,1)}, bf16[128,8064]{1,0:T(8,128)(2,1)}, bf16[128,3456]{1,0:T(8,128)(2,1)}, f32[16,768]{1,0:T(8,128)}) custom-call(s32[18]{0:T(128)} %dynamic-slice_bitcast_fusion.meta, s32[1]{0:T(128)S(6)} %copy.13.length_ref, bf16[128,768]{1,0:T(8,128)(2,1)} %tokens_ref.9, ...), custom_call_target="tpu_custom_call" | custom-call | tf_op jit(solution)/shard_map/pallas_call | solution.py:527
  102.1 3.6 %collective-permute-done.31.tokens_other = bf16[128,768]{1,0:T(8,128)(2,1)S(1)} collective-permute-done((bf16[128,768]{1,0:T(8,128)(2,1)S(1)}, bf16[128,768]{1,0:T(8,128)(2,1)S(1)}, u32[]{:S(2)}, u32[]{:S(2)}) %collective-permute-start.31) | collective-permute-done | bytes 196640 | tf_op jit(solution)/shard_map/ppermute | solution.py:740
  107.5 5.8 %shard_map.123 = (bf16[2,592,384]{2,1,0:T(8,128)(2,1)}, bf16[2,592,384]{2,1,0:T(8,128)(2,1)}) custom-call(s32[18]{0:T(128)} %dynamic-slice_bitcast_fusion.meta, bf16[128,768]{1,0:T(8,128)(2,1)} %tokens_ref.9, bf16[128,768]{1,0:T(8,128)(2,1)} %copy-done.4, bf16[128,8064]{1,0:T(8,128)(2,1)} %get-tuple-element.21.left_ref, bf16[128,8064]{1,0:T(8,128)(2,1)} %copy-done, ...), custom_call_target="tpu_custom_call" | custom-call | flops 1000 | bytes 1000 | tf_op jit(solution)/shard_map/pallas_call | solution.py:676
  115.0 5.9 %shard_map.122 = (bf16[2,592,384]{2,1,0:T(8,128)(2,1)}, bf16[2,592,384]{2,1,0:T(8,128)(2,1)}) custom-call(s32[18]{0:T(128)} %dynamic-slice_bitcast_fusion.meta, bf16[128,768]{1,0:T(8,128)(2,1)} %tokens_ref.9, bf16[128,768]{1,0:T(8,128)(2,1)} %copy-done.4, bf16[128,8064]{1,0:T(8,128)(2,1)} %get-tuple-element.21.left_ref, bf16[128,8064]{1,0:T(8,128)(2,1)} %copy-done, ...), custom_call_target="tpu_custom_call" | custom-call | flops 1000 | bytes 1000 | tf_op jit(solution)/shard_map/pallas_call | solution.py:676
  121.4 5.5 %collective-permute-done.40 = bf16[2,592,384]{2,1,0:T(8,128)(2,1)S(1)} collective-permute-done((bf16[2,592,384]{2,1,0:T(8,128)(2,1)}, bf16[2,592,384]{2,1,0:T(8,128)(2,1)S(1)}, u32[]{:S(2)}, u32[]{:S(2)}) %collective-permute-start.40) | collective-permute-done | bytes 909344 | tf_op jit(solution)/shard_map/ppermute | solution.py:750
  128.6 5.8 %shard_map.121 = (bf16[2,592,384]{2,1,0:T(8,128)(2,1)}, bf16[2,592,384]{2,1,0:T(8,128)(2,1)}) custom-call(s32[18]{0:T(128)} %dynamic-slice_bitcast_fusion.meta, bf16[128,768]{1,0:T(8,128)(2,1)} %tokens_ref.9, bf16[128,768]{1,0:T(8,128)(2,1)} %copy-done.4, bf16[128,8064]{1,0:T(8,128)(2,1)} %get-tuple-element.21.left_ref, bf16[128,8064]{1,0:T(8,128)(2,1)} %copy-done, ...), custom_call_target="tpu_custom_call" | custom-call | flops 1000 | bytes 1000 | tf_op jit(solution)/shard_map/pallas_call | solution.py:676
  136.0 5.6 %collective-permute-done.38 = bf16[2,592,384]{2,1,0:T(8,128)(2,1)} collective-permute-done((bf16[2,592,384]{2,1,0:T(8,128)(2,1)}, bf16[2,592,384]{2,1,0:T(8,128)(2,1)}, u32[]{:S(2)}, u32[]{:S(2)}) %collective-permute-start.38) | collective-permute-done | bytes 909344 | tf_op jit(solution)/shard_map/ppermute | solution.py:750
  146.4 2.9 %collective-permute-start.42 = (bf16[592,384]{1,0:T(8,128)(2,1)S(1)}, bf16[592,384]{1,0:T(8,128)(2,1)}, u32[]{:S(2)}, u32[]{:S(2)}) collective-permute-start(bf16[592,384]{1,0:T(8,128)(2,1)S(1)} %fusion.1), channel_id=1, source_target_pairs={{0,12},{1,13},{2,14},{3,15},{4,0},{5,1},{6,2},{7,3},{8,4},{9,5},{1... | collective-permute-start | bytes 1363976 | tf_op jit(solution)/shard_map/ppermute | solution.py:757
  149.2 5.8 %shard_map.120 = (bf16[2,592,384]{2,1,0:T(8,128)(2,1)}, bf16[2,592,384]{2,1,0:T(8,128)(2,1)}) custom-call(s32[18]{0:T(128)} %dynamic-slice_bitcast_fusion.meta, bf16[128,768]{1,0:T(8,128)(2,1)} %tokens_ref.9, bf16[128,768]{1,0:T(8,128)(2,1)} %copy-done.4, bf16[128,8064]{1,0:T(8,128)(2,1)} %get-tuple-element.21.left_ref, bf16[128,8064]{1,0:T(8,128)(2,1)} %copy-done, ...), custom_call_target="tpu_custom_call" | custom-call | flops 1000 | bytes 1000 | tf_op jit(solution)/shard_map/pallas_call | solution.py:676
  159.7 4.4 %collective-permute-start.43 = (bf16[592,384]{1,0:T(8,128)(2,1)S(1)}, bf16[592,384]{1,0:T(8,128)(2,1)S(1)}, u32[]{:S(2)}, u32[]{:S(2)}) collective-permute-start(bf16[592,384]{1,0:T(8,128)(2,1)S(1)} %fusion.3), channel_id=1, source_target_pairs={{0,12},{1,13},{2,14},{3,15},{4,0},{5,1},{6,2},{7,3},{8,4},{9,5},{1... | collective-permute-start | bytes 1363976 | tf_op jit(solution)/shard_map/ppermute | solution.py:757
  164.1 8.3 %collective-permute-done.34 = bf16[2,592,384]{2,1,0:T(8,128)(2,1)S(1)} collective-permute-done((bf16[2,592,384]{2,1,0:T(8,128)(2,1)}, bf16[2,592,384]{2,1,0:T(8,128)(2,1)S(1)}, u32[]{:S(2)}, u32[]{:S(2)}) %collective-permute-start.34) | collective-permute-done | bytes 909344 | tf_op jit(solution)/shard_map/ppermute | solution.py:750
  173.4 3.3 %collective-permute-start.44 = (bf16[592,384]{1,0:T(8,128)(2,1)S(1)}, bf16[592,384]{1,0:T(8,128)(2,1)S(1)}, u32[]{:S(2)}, u32[]{:S(2)}) collective-permute-start(bf16[592,384]{1,0:T(8,128)(2,1)S(1)} %fusion.5), channel_id=1, source_target_pairs={{0,12},{1,13},{2,14},{3,15},{4,0},{5,1},{6,2},{7,3},{8,4},{9,5},{1... | collective-permute-start | bytes 1363976 | tf_op jit(solution)/shard_map/ppermute | solution.py:757
  176.7 4.4 %collective-permute-done.35 = bf16[592,384]{1,0:T(8,128)(2,1)S(1)} collective-permute-done((bf16[592,384]{1,0:T(8,128)(2,1)S(1)}, bf16[592,384]{1,0:T(8,128)(2,1)S(1)}, u32[]{:S(2)}, u32[]{:S(2)}) %collective-permute-start.35) | collective-permute-done | bytes 454688 | tf_op jit(solution)/shard_map/ppermute | solution.py:752
  181.1 3.6 %collective-permute-done.44 = bf16[592,384]{1,0:T(8,128)(2,1)S(1)} collective-permute-done((bf16[592,384]{1,0:T(8,128)(2,1)S(1)}, bf16[592,384]{1,0:T(8,128)(2,1)S(1)}, u32[]{:S(2)}, u32[]{:S(2)}) %collective-permute-start.44) | collective-permute-done | bytes 454688 | tf_op jit(solution)/shard_map/ppermute | solution.py:757
  187.6 3.8 %shard_map.124 = f32[3464,128]{1,0:T(8,128)} custom-call(s32[18]{0:T(128)} %dynamic-slice_bitcast_fusion.meta, f32[592,384]{1,0:T(8,128)} %copy-done.3, f32[592,384]{1,0:T(8,128)} %collective-permute-done.45.other_ref), custom_call_target="tpu_custom_call" | custom-call | tf_op jit(solution)/shard_map/pallas_call | solution.py:305
  191.4 5.9 %multiply_subtract_fusion = (f32[442944]{0:T(1024)}, f32[442944]{0:T(1024)}, f32[442944]{0:T(1024)}, f32[442944]{0:T(1024)}) fusion(f32[442944]{0:T(1024)S(1)} %copy-done.1, f32[442944]{0:T(1024)} %param.11, f32[442944]{0:T(1024)} %param.12, f32[443392]{0:T(1024)} %bitcast.33), kind=kLoop, calls=%fused_computation.2 | loop fusion | flops 6644160 | bytes 14174208 | tf_op jit(solution)/shard_map/sub | solution.py:230
  (166 shorter events, 52.5 us)
Async XLA Ops:
  8.0 15.7 %collective-permute-start.3 = (bf16[592,384]{1,0:T(8,128)(2,1)}, bf16[592,384]{1,0:T(8,128)(2,1)S(1)}, u32[]{:S(2)}, u32[]{:S(2)}) collective-permute-start(bf16[592,384]{1,0:T(8,128)(2,1)} %shard_map.118.refs_0_), channel_id=1, source_target_pairs={{0,4},{1,5},{2,6},{3,7},{4,8},{5,9},{6,10},{7,11},{8,12},{9,13},{1... | collective-permute-start | bytes 1363976 | tf_op jit(solution)/shard_map/ppermute | solution.py:728
  11.1 14.2 %collective-permute-start = (bf16[592,384]{1,0:T(8,128)(2,1)}, bf16[592,384]{1,0:T(8,128)(2,1)S(1)}, u32[]{:S(2)}, u32[]{:S(2)}) collective-permute-start(bf16[592,384]{1,0:T(8,128)(2,1)} %shard_map.118.refs_0_), channel_id=1, source_target_pairs={{0,1},{16,18},{1,0},{17,19},{2,3},{18,16},{3,2},{19,17},{4,5},{20,... | collective-permute-start | bytes 1363976 | tf_op jit(solution)/shard_map/ppermute | solution.py:729
  12.5 14.2 %collective-permute-start.1 = (bf16[592,384]{1,0:T(8,128)(2,1)}, bf16[592,384]{1,0:T(8,128)(2,1)S(1)}, u32[]{:S(2)}, u32[]{:S(2)}) collective-permute-start(bf16[592,384]{1,0:T(8,128)(2,1)} %shard_map.118.refs_0_), channel_id=1, source_target_pairs={{0,2},{16,17},{1,3},{17,16},{2,0},{18,19},{3,1},{19,18},{4,6},{20,... | collective-permute-start | bytes 1363976 | tf_op jit(solution)/shard_map/ppermute | solution.py:730
  14.1 12.7 %collective-permute-start.15 = (bf16[592,384]{1,0:T(8,128)(2,1)}, bf16[592,384]{1,0:T(8,128)(2,1)S(1)}, u32[]{:S(2)}, u32[]{:S(2)}) collective-permute-start(bf16[592,384]{1,0:T(8,128)(2,1)} %shard_map.118.refs_0_), channel_id=1, source_target_pairs={{0,16},{16,0},{1,17},{17,1},{2,18},{18,2},{3,19},{19,3},{4,20},{20... | collective-permute-start | bytes 1363976 | tf_op jit(solution)/shard_map/ppermute | solution.py:734
  23.7 13.4 %collective-permute-start.7 = (bf16[592,384]{1,0:T(8,128)(2,1)S(1)}, bf16[592,384]{1,0:T(8,128)(2,1)S(1)}, u32[]{:S(2)}, u32[]{:S(2)}) collective-permute-start(bf16[592,384]{1,0:T(8,128)(2,1)S(1)} %collective-permute-done.3.refs_4_), channel_id=1, source_target_pairs={{0,4},{1,5},{2,6},{3,7},{4,8},{5,9},{6,10},{7,11},{8,12},{9,13},{1... | collective-permute-start | bytes 1363976 | tf_op jit(solution)/shard_map/ppermute | solution.py:728
  23.7 13.4 %collective-permute-start.4 = (bf16[592,384]{1,0:T(8,128)(2,1)S(1)}, bf16[592,384]{1,0:T(8,128)(2,1)S(1)}, u32[]{:S(2)}, u32[]{:S(2)}) collective-permute-start(bf16[592,384]{1,0:T(8,128)(2,1)S(1)} %collective-permute-done.3.refs_4_), channel_id=1, source_target_pairs={{0,1},{16,18},{1,0},{17,19},{2,3},{18,16},{3,2},{19,17},{4,5},{20,... | collective-permute-start | bytes 1363976 | tf_op jit(solution)/shard_map/ppermute | solution.py:729
  25.2 12.4 %collective-permute-start.5 = (bf16[592,384]{1,0:T(8,128)(2,1)S(1)}, bf16[592,384]{1,0:T(8,128)(2,1)S(1)}, u32[]{:S(2)}, u32[]{:S(2)}) collective-permute-start(bf16[592,384]{1,0:T(8,128)(2,1)S(1)} %collective-permute-done.3.refs_4_), channel_id=1, source_target_pairs={{0,2},{16,17},{1,3},{17,16},{2,0},{18,19},{3,1},{19,18},{4,6},{20,... | collective-permute-start | bytes 1363976 | tf_op jit(solution)/shard_map/ppermute | solution.py:730
  26.8 13.4 %collective-permute-start.2 = (bf16[592,384]{1,0:T(8,128)(2,1)S(1)}, bf16[592,384]{1,0:T(8,128)(2,1)S(1)}, u32[]{:S(2)}, u32[]{:S(2)}) collective-permute-start(bf16[592,384]{1,0:T(8,128)(2,1)S(1)} %collective-permute-done.refs_1_), channel_id=1, source_target_pairs={{0,2},{16,17},{1,3},{17,16},{2,0},{18,19},{3,1},{19,18},{4,6},{20,... | collective-permute-start | bytes 1363976 | tf_op jit(solution)/shard_map/ppermute | solution.py:731
  37.7 14.3 %collective-permute-start.11 = (bf16[592,384]{1,0:T(8,128)(2,1)S(1)}, bf16[592,384]{1,0:T(8,128)(2,1)S(1)}, u32[]{:S(2)}, u32[]{:S(2)}) collective-permute-start(bf16[592,384]{1,0:T(8,128)(2,1)S(1)} %collective-permute-done.7.refs_8_), channel_id=1, source_target_pairs={{0,4},{1,5},{2,6},{3,7},{4,8},{5,9},{6,10},{7,11},{8,12},{9,13},{1... | collective-permute-start | bytes 1363976 | tf_op jit(solution)/shard_map/ppermute | solution.py:728
  38.4 13.6 %collective-permute-start.8 = (bf16[592,384]{1,0:T(8,128)(2,1)S(1)}, bf16[592,384]{1,0:T(8,128)(2,1)S(1)}, u32[]{:S(2)}, u32[]{:S(2)}) collective-permute-start(bf16[592,384]{1,0:T(8,128)(2,1)S(1)} %collective-permute-done.7.refs_8_), channel_id=1, source_target_pairs={{0,1},{16,18},{1,0},{17,19},{2,3},{18,16},{3,2},{19,17},{4,5},{20,... | collective-permute-start | bytes 1363976 | tf_op jit(solution)/shard_map/ppermute | solution.py:729
  40.2 12.3 %collective-permute-start.9 = (bf16[592,384]{1,0:T(8,128)(2,1)S(1)}, bf16[592,384]{1,0:T(8,128)(2,1)S(1)}, u32[]{:S(2)}, u32[]{:S(2)}) collective-permute-start(bf16[592,384]{1,0:T(8,128)(2,1)S(1)} %collective-permute-done.7.refs_8_), channel_id=1, source_target_pairs={{0,2},{16,17},{1,3},{17,16},{2,0},{18,19},{3,1},{19,18},{4,6},{20,... | collective-permute-start | bytes 1363976 | tf_op jit(solution)/shard_map/ppermute | solution.py:730
  42.3 13.5 %collective-permute-start.6 = (bf16[592,384]{1,0:T(8,128)(2,1)S(1)}, bf16[592,384]{1,0:T(8,128)(2,1)S(1)}, u32[]{:S(2)}, u32[]{:S(2)}) collective-permute-start(bf16[592,384]{1,0:T(8,128)(2,1)S(1)} %collective-permute-done.4.refs_5_), channel_id=1, source_target_pairs={{0,2},{16,17},{1,3},{17,16},{2,0},{18,19},{3,1},{19,18},{4,6},{20,... | collective-permute-start | bytes 1363976 | tf_op jit(solution)/shard_map/ppermute | solution.py:731
  57.4 13.0 %collective-permute-start.10 = (bf16[592,384]{1,0:T(8,128)(2,1)S(1)}, bf16[592,384]{1,0:T(8,128)(2,1)S(1)}, u32[]{:S(2)}, u32[]{:S(2)}) collective-permute-start(bf16[592,384]{1,0:T(8,128)(2,1)S(1)} %collective-permute-done.8.refs_9_), channel_id=1, source_target_pairs={{0,2},{16,17},{1,3},{17,16},{2,0},{18,19},{3,1},{19,18},{4,6},{20,... | collective-permute-start | bytes 1363976 | tf_op jit(solution)/shard_map/ppermute | solution.py:731
  57.9 13.4 %collective-permute-start.27 = (bf16[592,384]{1,0:T(8,128)(2,1)S(1)}, bf16[592,384]{1,0:T(8,128)(2,1)S(1)}, u32[]{:S(2)}, u32[]{:S(2)}) collective-permute-start(bf16[592,384]{1,0:T(8,128)(2,1)S(1)} %collective-permute-done.11.refs_12_), channel_id=1, source_target_pairs={{0,16},{16,0},{1,17},{17,1},{2,18},{18,2},{3,19},{19,3},{4,20},{20... | collective-permute-start | bytes 1363976 | tf_op jit(solution)/shard_map/ppermute | solution.py:734
  58.6 12.8 %collective-permute-start.24 = (bf16[592,384]{1,0:T(8,128)(2,1)S(1)}, bf16[592,384]{1,0:T(8,128)(2,1)S(1)}, u32[]{:S(2)}, u32[]{:S(2)}) collective-permute-start(bf16[592,384]{1,0:T(8,128)(2,1)S(1)} %collective-permute-done.8.refs_9_), channel_id=1, source_target_pairs={{0,16},{16,0},{1,17},{17,1},{2,18},{18,2},{3,19},{19,3},{4,20},{20... | collective-permute-start | bytes 1363976 | tf_op jit(solution)/shard_map/ppermute | solution.py:734
  113.3 13.6 %collective-permute-start.40 = (bf16[2,592,384]{2,1,0:T(8,128)(2,1)}, bf16[2,592,384]{2,1,0:T(8,128)(2,1)S(1)}, u32[]{:S(2)}, u32[]{:S(2)}) collective-permute-start(bf16[2,592,384]{2,1,0:T(8,128)(2,1)} %get-tuple-element.31), channel_id=1, source_target_pairs={{0,2},{16,17},{1,3},{17,16},{2,0},{18,19},{3,1},{19,18},{4,6},{20,... | collective-permute-start | bytes 2727944 | tf_op jit(solution)/shard_map/ppermute | solution.py:750
  120.9 20.7 %collective-permute-start.38 = (bf16[2,592,384]{2,1,0:T(8,128)(2,1)}, bf16[2,592,384]{2,1,0:T(8,128)(2,1)}, u32[]{:S(2)}, u32[]{:S(2)}) collective-permute-start(bf16[2,592,384]{2,1,0:T(8,128)(2,1)} %get-tuple-element.29), channel_id=1, source_target_pairs={{0,2},{16,17},{1,3},{17,16},{2,0},{18,19},{3,1},{19,18},{4,6},{20,... | collective-permute-start | bytes 2727944 | tf_op jit(solution)/shard_map/ppermute | solution.py:750
  127.0 18.1 %collective-permute-start.41 = (bf16[592,384]{1,0:T(8,128)(2,1)S(1)}, bf16[592,384]{1,0:T(8,128)(2,1)}, u32[]{:S(2)}, u32[]{:S(2)}) collective-permute-start(bf16[592,384]{1,0:T(8,128)(2,1)S(1)} %fusion.10), channel_id=1, source_target_pairs={{0,1},{16,18},{1,0},{17,19},{2,3},{18,16},{3,2},{19,17},{4,5},{20,... | collective-permute-start | bytes 1363976 | tf_op jit(solution)/shard_map/ppermute | solution.py:752
  134.3 22.3 %collective-permute-start.36 = (bf16[2,592,384]{2,1,0:T(8,128)(2,1)}, bf16[2,592,384]{2,1,0:T(8,128)(2,1)S(1)}, u32[]{:S(2)}, u32[]{:S(2)}) collective-permute-start(bf16[2,592,384]{2,1,0:T(8,128)(2,1)} %get-tuple-element.27), channel_id=1, source_target_pairs={{0,2},{16,17},{1,3},{17,16},{2,0},{18,19},{3,1},{19,18},{4,6},{20,... | collective-permute-start | bytes 2727944 | tf_op jit(solution)/shard_map/ppermute | solution.py:750
  143.7 14.2 %collective-permute-start.39 = (bf16[592,384]{1,0:T(8,128)(2,1)}, bf16[592,384]{1,0:T(8,128)(2,1)}, u32[]{:S(2)}, u32[]{:S(2)}) collective-permute-start(bf16[592,384]{1,0:T(8,128)(2,1)} %fusion.9), channel_id=1, source_target_pairs={{0,1},{16,18},{1,0},{17,19},{2,3},{18,16},{3,2},{19,17},{4,5},{20,... | collective-permute-start | bytes 1363976 | tf_op jit(solution)/shard_map/ppermute | solution.py:752
  146.4 11.8 %collective-permute-start.42 = (bf16[592,384]{1,0:T(8,128)(2,1)S(1)}, bf16[592,384]{1,0:T(8,128)(2,1)}, u32[]{:S(2)}, u32[]{:S(2)}) collective-permute-start(bf16[592,384]{1,0:T(8,128)(2,1)S(1)} %fusion.1), channel_id=1, source_target_pairs={{0,12},{1,13},{2,14},{3,15},{4,0},{5,1},{6,2},{7,3},{8,4},{9,5},{1... | collective-permute-start | bytes 1363976 | tf_op jit(solution)/shard_map/ppermute | solution.py:757
  155.0 17.4 %collective-permute-start.34 = (bf16[2,592,384]{2,1,0:T(8,128)(2,1)}, bf16[2,592,384]{2,1,0:T(8,128)(2,1)S(1)}, u32[]{:S(2)}, u32[]{:S(2)}) collective-permute-start(bf16[2,592,384]{2,1,0:T(8,128)(2,1)} %get-tuple-element.25), channel_id=1, source_target_pairs={{0,2},{16,17},{1,3},{17,16},{2,0},{18,19},{3,1},{19,18},{4,6},{20,... | collective-permute-start | bytes 2727944 | tf_op jit(solution)/shard_map/ppermute | solution.py:750
  156.7 16.4 %collective-permute-start.37 = (bf16[592,384]{1,0:T(8,128)(2,1)S(1)}, bf16[592,384]{1,0:T(8,128)(2,1)S(1)}, u32[]{:S(2)}, u32[]{:S(2)}) collective-permute-start(bf16[592,384]{1,0:T(8,128)(2,1)S(1)} %fusion.8), channel_id=1, source_target_pairs={{0,1},{16,18},{1,0},{17,19},{2,3},{18,16},{3,2},{19,17},{4,5},{20,... | collective-permute-start | bytes 1363976 | tf_op jit(solution)/shard_map/ppermute | solution.py:752
  159.7 13.5 %collective-permute-start.43 = (bf16[592,384]{1,0:T(8,128)(2,1)S(1)}, bf16[592,384]{1,0:T(8,128)(2,1)S(1)}, u32[]{:S(2)}, u32[]{:S(2)}) collective-permute-start(bf16[592,384]{1,0:T(8,128)(2,1)S(1)} %fusion.3), channel_id=1, source_target_pairs={{0,12},{1,13},{2,14},{3,15},{4,0},{5,1},{6,2},{7,3},{8,4},{9,5},{1... | collective-permute-start | bytes 1363976 | tf_op jit(solution)/shard_map/ppermute | solution.py:757
  (62 other events, 672.9 us)

commit v4 on v3

--- a/solution.py
+++ b/solution.py
@@ -245,6 +245,7 @@
 RED_ROW = 6144
 BIAS_ROW = 9216
 LEFT = 4608
+BLOCK_LINES = 872
 RIGHT = 9 * HALF
 VMEM_CAP = 64 * 1024 * 1000
 
@@ -256,10 +257,14 @@
     return pltpu.roll(block, 64, 1)
 
 
-def frame_kernel(meta, flat_ref, out_ref, lines, framed):
-    shift, odd, first_col = meta[0], meta[1], meta[2]
+def frame_kernel(flat_ref, out_ref, lines, framed):
+    here_at, core = lax.axis_index("shard"), lax.axis_index("rep")
+    shift, odd, first_col = (9 * here_at) // 2, here_at % 2, 3 * core
     lines[0:8, :] = jnp.zeros((8, 128), f32)
-    lines[8 : 8 + LOCAL_LINES, :] = flat_ref[...]
+    lines[LOCAL_LINES : LOCAL_LINES + 16, :] = jnp.zeros((16, 128), f32)
+    lines[8:3464, :] = flat_ref[pl.ds(0, 442368)].reshape(3456, 128)
+    lines[3464:3468, :] = flat_ref[pl.ds(442368, 512)].reshape(4, 128)
+    lines[3468:3469, 0:64] = flat_ref[pl.ds(442880, 64)].reshape(1, 64)
     framed[0:96, :] = jnp.zeros((96, 128), f32)
     framed[LINES - 96 : LINES, :] = jnp.zeros((96, 128), f32)
     low = lax.broadcasted_iota(jnp.int32, (LOCAL_LINES, 128), 1) < 64
@@ -272,48 +277,56 @@
         out_ref[:, 128 * j : 128 * (j + 1)] = column.astype(bf16)
 
 
-def make_frame(params, meta):
-    flat = jnp.pad(params, (0, LOCAL_LINES * 128 - LOCAL)).reshape(LOCAL_LINES, 128)
+def make_frame(params):
     return pl.pallas_call(
         frame_kernel,
         out_shape=jax.ShapeDtypeStruct((FRAME, HALF), bf16),
-        in_specs=[
-            pl.BlockSpec(memory_space=pltpu.SMEM),
-            pl.BlockSpec(memory_space=pltpu.VMEM),
-        ],
+        in_specs=[pl.BlockSpec(memory_space=pltpu.VMEM)],
         out_specs=pl.BlockSpec(memory_space=pltpu.VMEM),
         scratch_shapes=[
             pltpu.VMEM((LOCAL_LINES + 16, 128), f32),
             pltpu.VMEM((LINES, 128), f32),
         ],
-    )(meta, flat)
-
-
-def unframe_kernel(meta, mine_ref, other_ref, out_ref, framed):
+    )(params)
+
+
+def finish_kernel(
+    meta, mine_ref, other_ref, param_ref, first_ref, second_ref, grad_out, param_out, first_out, second_out, framed
+):
     shift, odd, first_col, other_col = meta[0], meta[1], meta[2], meta[3]
-    for j in range(3):
-        framed[pl.ds(first_col + j, FRAME, stride=6), :] = mine_ref[:, 128 * j : 128 * (j + 1)]
-        framed[pl.ds(other_col + j, FRAME, stride=6), :] = other_ref[:, 128 * j : 128 * (j + 1)]
-    low = lax.broadcasted_iota(jnp.int32, (LOCAL_LINES, 128), 1) < 64
-    here = framed[pl.ds(shift, LOCAL_LINES), :]
-    after = framed[pl.ds(shift + 1, LOCAL_LINES), :]
+    step = pl.program_id(0)
+
+    @pl.when(step == 0)
+    def _():
+        framed[LINES : LINES + 16, :] = jnp.zeros((16, 128), f32)
+        for j in range(3):
+            at = slice(128 * j, 128 * (j + 1))
+            framed[pl.ds(first_col + j, FRAME, stride=6), :] = mine_ref[:, at]
+            framed[pl.ds(other_col + j, FRAME, stride=6), :] = other_ref[:, at]
+
+    low = lax.broadcasted_iota(jnp.int32, (BLOCK_LINES, 128), 1) < 64
+    here = framed[pl.ds(shift + BLOCK_LINES * step, BLOCK_LINES), :]
+    after = framed[pl.ds(shift + BLOCK_LINES * step + 1, BLOCK_LINES), :]
     moved = jnp.where(low, swap_half(here), swap_half(after))
-    out_ref[...] = jnp.where(odd == 1, moved, here)
-
-
-def take_frame(mine, other, meta):
-    lines = pl.pallas_call(
-        unframe_kernel,
-        out_shape=jax.ShapeDtypeStruct((LOCAL_LINES, 128), f32),
-        in_specs=[
-            pl.BlockSpec(memory_space=pltpu.SMEM),
-            pl.BlockSpec(memory_space=pltpu.VMEM),
-            pl.BlockSpec(memory_space=pltpu.VMEM),
-        ],
-        out_specs=pl.BlockSpec(memory_space=pltpu.VMEM),
-        scratch_shapes=[pltpu.VMEM((LINES + 8, 128), f32)],
-    )(meta, mine, other)
-    return lines.reshape(LOCAL_LINES * 128)[:LOCAL]
+    grad = jnp.where(odd == 1, moved, here).reshape(BLOCK_LINES * 128)
+    grad_out[...] = grad
+    new_param, new_first, new_second = adamw(param_ref[...], first_ref[...], second_ref[...], grad)
+    param_out[...] = new_param
+    first_out[...] = new_first
+    second_out[...] = new_second
+
+
+def finish(mine, other, meta, params, first_moment, second_moment):
+    vmem_spec = pl.BlockSpec(memory_space=pltpu.VMEM)
+    block_spec = pl.BlockSpec((BLOCK_LINES * 128,), lambda i: (i,))
+    return pl.pallas_call(
+        finish_kernel,
+        grid=(4,),
+        out_shape=[jax.ShapeDtypeStruct((LOCAL,), f32)] * 4,
+        in_specs=[pl.BlockSpec(memory_space=pltpu.SMEM), vmem_spec, vmem_spec] + [block_spec] * 3,
+        out_specs=[block_spec] * 4,
+        scratch_shapes=[pltpu.VMEM((LINES + 16, 128), f32)],
+    )(meta, mine, other, params, first_moment, second_moment)
 
 
 def dot_nn(left_side, right_side):
@@ -358,7 +371,7 @@
             sem_tail.at[side, shard],
         )
 
-    for quad in range(4):
+    def start_copies(quad, mains, ends):
         for t in range(4):
 
             @pl.when(meta[6 + quad] == t)
@@ -366,22 +379,28 @@
                 for side in range(2):
                     for j in range(4):
                         shard = 4 * quad + meta[10 + 4 * side + j]
-                        tail_copy(frames[16 * side + 4 * t + j], shard, side).start()
-                        main_copy(frames[16 * side + 4 * t + j], shard, side).start()
-
-    for shard in range(16):
-        for side in range(2):
-            tail_copy(frames[0], shard, side).wait()
+                        if mains:
+                            main_copy(frames[16 * side + 4 * t + j], shard, side).start()
+                        if ends:
+                            tail_copy(frames[16 * side + 4 * t + j], shard, side).start()
+
+    start_copies(3, False, True)
+    for quad in range(4):
+        start_copies(quad, True, quad < 3)
 
     def arrive(first, last):
         for shard in range(first, last):
             for side in range(2):
                 main_copy(frames[0], shard, side).wait()
             if shard > 0:
+                for side in range(2):
+                    tail_copy(frames[0], shard - 1, side).wait()
                 at = STEP_ROWS * shard
                 joined = weights[at : at + 16, :].astype(f32) + tails[shard - 1].astype(f32)
                 weights[at : at + 16, :] = joined.astype(bf16)
 
+    for side in range(2):
+        tail_copy(frames[0], 15, side).wait()
     arrive(0, 4)
 
     def spread_triple(i, carry):
@@ -611,7 +630,7 @@
                 grads[pl.ds(at, rows_used), 128 * j : 128 * (j + 1)] = stage[j, 0:rows_used, :].astype(bf16)
             return carry
 
-        lax.fori_loop(0, chunks, step, 0)
+        lax.fori_loop(0, chunks, step, 0, unroll=True)
 
     def plain(first, right_first, chunks, row):
         def step(i, carry):
@@ -620,7 +639,7 @@
             grads[pl.ds(pl.multiple_of(row + 256 * i, 16), 256), :] = block.astype(bf16)
             return carry
 
-        lax.fori_loop(0, chunks, step, 0)
+        lax.fori_loop(0, chunks, step, 0, unroll=True)
 
     def last_rows(first, right_first):
         block = inner_rows(left[:, first : first + 128], right[:, right_first : right_first + HALF])
@@ -719,7 +738,7 @@
     device = lax.axis_index("rep") * n + lax.axis_index("shard")
     meta = lax.dynamic_slice(jnp.asarray(device_table(n)), (device, 0), (1, 18)).reshape(18)
 
-    own = make_frame(params, meta)
+    own = make_frame(params)
     mine, other = [], []
     up = [(s, (s + 4) % n) for s in range(n)]
     down = [(s, (s - 4) % n) for s in range(n)]
@@ -755,8 +774,9 @@
             total = total + passed.astype(f32)
         if t > 0:
             passed = lax.ppermute(total.astype(bf16), "shard", down)
-    weight_grad = take_frame(total, lax.ppermute(total, "rep", swap), meta)
-    new_params, new_first, new_second = adamw(params, first_moment, second_moment, weight_grad)
+    weight_grad, new_params, new_first, new_second = finish(
+        total, lax.ppermute(total, "rep", swap), meta, params, first_moment, second_moment
+    )
     return (block_out, input_grad, weight_grad, new_params, new_first, new_second)
 
 

time: 198 us -> 188 us (0.949)
  other arithmetic: 11.4 us -> 5.56 us
  Pallas kernels: 53.2 us -> 49.3 us
  local copies, waits for them, and re-layouts: 7.3 us -> 3.59 us
  waiting for transfers between devices: 78.2 us -> 80.2 us
    sub x1 -> x0, other arithmetic: 5.85 us -> none  [adamw(): param_now - learn_rate * (first_new / fix_one / (jnp.sqrt(second_new / fi...]
    pallas_call x4, Pallas kernels: 23.2 us -> 18.4 us  [quad_grads(): pl.pallas_call(functools.partial(grad_kernel, slot), out_shape=[frames, f...]
    pallas_call x1, Pallas kernels: 3.79 us -> 7.43 us  [finish(): pl.pallas_call(finish_kernel, grid=(4,), out_shape=[jax.ShapeDtypeStruct(...]
    reshape x1 -> x0, local copies, waits for them, and re-layouts: 2.8 us -> none  [make_frame(): jnp.pad(params, (0, LOCAL_LINES * 128 - LOCAL)).reshape(LOCAL_LINES, 128)]
    pallas_call x1, Pallas kernels: 22.9 us -> 20.1 us  [run_layer(): pl.pallas_call(layer_kernel, out_shape=[thin, thin, jax.ShapeDtypeStruct(...]
    ppermute x4, waiting for transfers between devices: 19.5 us -> 21.9 us  [on_device_planes(): from_far = lax.ppermute(high, both, far)]
  transfers between devices with their start and end apart: 46 -> 46, of which waited for: 18 -> 19; matrix products, arithmetic and copies ran while one was open for 3% -> 3% of each run, Pallas kernels for 9% -> 7%
where the time goes in v4:
time: 188 us; the launch traced here: 187 us
  waiting for transfers between devices  80.2 us (43%)
  Pallas kernels  49.3 us (26%)
  starting transfers between devices  46.8 us (25%)
  other arithmetic  5.56 us (3%)
  local copies, waits for them, and re-layouts  3.59 us (2%)
    ppermute x3, waiting for transfers between devices, on_device_planes(): zero = own if t == 0 else lax.ppermute(zero, 'shard', up)  28.4 us
    ppermute x4, waiting for transfers between devices, on_device_planes(): from_far = lax.ppermute(high, both, far)  21.9 us
    pallas_call x1, Pallas kernels, run_layer(): pl.pallas_call(layer_kernel, out_shape=[thin, thin, jax.ShapeDtypeStruct(...  20.1 us
    pallas_call x4, Pallas kernels, quad_grads(): pl.pallas_call(functools.partial(grad_kernel, slot), out_shape=[frames, f...  18.4 us
    ppermute x3, starting transfers between devices, on_device_planes(): passed = lax.ppermute(total.astype(bf16), 'shard', down)  10.9 us
    ppermute x4, waiting for transfers between devices, on_device_planes(): three = lax.ppermute(one, both, far)  8.6 us
    pallas_call x1, Pallas kernels, finish(): pl.pallas_call(finish_kernel, grid=(4,), out_shape=[jax.ShapeDtypeStruct(...  7.43 us
    ppermute x4, starting transfers between devices, on_device_planes(): one = lax.ppermute(zero, both, near)  6.03 us
  transfers between devices with their start and end apart: 46, of which 19 were waited for; matrix products, arithmetic and copies ran while one was open for 3% of the time, Pallas kernels for 7%

profile of v4, /device:TPU:0, one launch (start us, length us, event | category | flops | bytes accessed | tf_op | source)
XLA Modules:
  0.0 187.1 jit_solution(4781836531441832907)
XLA Ops:
  0.6 3.3 %shard_map.118.refs_0_ = bf16[592,384]{1,0:T(8,128)(2,1)} custom-call(f32[442944]{0:T(1024)} %param_ref.1), custom_call_target="tpu_custom_call" | custom-call | tf_op jit(solution)/shard_map/pallas_call | solution.py:281
  4.0 3.0 %collective-permute-start.3 = (bf16[592,384]{1,0:T(8,128)(2,1)}, bf16[592,384]{1,0:T(8,128)(2,1)S(1)}, u32[]{:S(2)}, u32[]{:S(2)}) collective-permute-start(bf16[592,384]{1,0:T(8,128)(2,1)} %shard_map.118.refs_0_), channel_id=1, source_target_pairs={{0,4},{1,5},{2,6},{3,7},{4,8},{5,9},{6,10},{7,11},{8,12},{9,13},{1... | collective-permute-start | bytes 1363976 | tf_op jit(solution)/shard_map/ppermute | solution.py:747
  10.0 9.6 %collective-permute-done.3.refs_4_ = bf16[592,384]{1,0:T(8,128)(2,1)S(1)} collective-permute-done((bf16[592,384]{1,0:T(8,128)(2,1)}, bf16[592,384]{1,0:T(8,128)(2,1)S(1)}, u32[]{:S(2)}, u32[]{:S(2)}) %collective-permute-start.3) | collective-permute-done | bytes 454688 | tf_op jit(solution)/shard_map/ppermute | solution.py:747
  23.3 9.8 %collective-permute-done.7.refs_8_ = bf16[592,384]{1,0:T(8,128)(2,1)S(1)} collective-permute-done((bf16[592,384]{1,0:T(8,128)(2,1)S(1)}, bf16[592,384]{1,0:T(8,128)(2,1)S(1)}, u32[]{:S(2)}, u32[]{:S(2)}) %collective-permute-start.7) | collective-permute-done | bytes 454688 | tf_op jit(solution)/shard_map/ppermute | solution.py:747
  38.9 9.0 %collective-permute-done.11.refs_12_ = bf16[592,384]{1,0:T(8,128)(2,1)S(1)} collective-permute-done((bf16[592,384]{1,0:T(8,128)(2,1)S(1)}, bf16[592,384]{1,0:T(8,128)(2,1)S(1)}, u32[]{:S(2)}, u32[]{:S(2)}) %collective-permute-start.11) | collective-permute-done | bytes 454688 | tf_op jit(solution)/shard_map/ppermute | solution.py:747
  54.7 4.5 %collective-permute-done.12.refs_13_ = bf16[592,384]{1,0:T(8,128)(2,1)S(1)} collective-permute-done((bf16[592,384]{1,0:T(8,128)(2,1)S(1)}, bf16[592,384]{1,0:T(8,128)(2,1)S(1)}, u32[]{:S(2)}, u32[]{:S(2)}) %collective-permute-start.12) | collective-permute-done | bytes 454688 | tf_op jit(solution)/shard_map/ppermute | solution.py:748
  63.0 3.4 %collective-permute-done.10.refs_11_ = bf16[592,384]{1,0:T(8,128)(2,1)} collective-permute-done((bf16[592,384]{1,0:T(8,128)(2,1)S(1)}, bf16[592,384]{1,0:T(8,128)(2,1)}, u32[]{:S(2)}, u32[]{:S(2)}) %collective-permute-start.10) | collective-permute-done | bytes 454688 | tf_op jit(solution)/shard_map/ppermute | solution.py:750
  68.1 3.2 %collective-permute-done.14.refs_15_ = bf16[592,384]{1,0:T(8,128)(2,1)} collective-permute-done((bf16[592,384]{1,0:T(8,128)(2,1)S(1)}, bf16[592,384]{1,0:T(8,128)(2,1)}, u32[]{:S(2)}, u32[]{:S(2)}) %collective-permute-start.14) | collective-permute-done | bytes 454688 | tf_op jit(solution)/shard_map/ppermute | solution.py:750
  73.9 20.1 %shard_map.119 = (bf16[128,768]{1,0:T(8,128)(2,1)}, bf16[128,768]{1,0:T(8,128)(2,1)}, bf16[128,8064]{1,0:T(8,128)(2,1)}, bf16[128,3456]{1,0:T(8,128)(2,1)}, f32[16,768]{1,0:T(8,128)}) custom-call(s32[18]{0:T(128)} %dynamic-slice_bitcast_fusion.meta, s32[1]{0:T(128)S(6)} %copy.13.length_ref, bf16[128,768]{1,0:T(8,128)(2,1)} %tokens_ref.9, ...), custom_call_target="tpu_custom_call" | custom-call | tf_op jit(solution)/shard_map/pallas_call | solution.py:546
  94.7 3.6 %collective-permute-done.31.tokens_other = bf16[128,768]{1,0:T(8,128)(2,1)S(1)} collective-permute-done((bf16[128,768]{1,0:T(8,128)(2,1)S(1)}, bf16[128,768]{1,0:T(8,128)(2,1)S(1)}, u32[]{:S(2)}, u32[]{:S(2)}) %collective-permute-start.31) | collective-permute-done | bytes 196640 | tf_op jit(solution)/shard_map/ppermute | solution.py:759
  100.1 4.9 %shard_map.123 = (bf16[2,592,384]{2,1,0:T(8,128)(2,1)}, bf16[2,592,384]{2,1,0:T(8,128)(2,1)}) custom-call(s32[18]{0:T(128)} %dynamic-slice_bitcast_fusion.meta, bf16[128,768]{1,0:T(8,128)(2,1)} %tokens_ref.9, bf16[128,768]{1,0:T(8,128)(2,1)} %copy-done.3, bf16[128,8064]{1,0:T(8,128)(2,1)} %get-tuple-element.25.left_ref, bf16[128,8064]{1,0:T(8,128)(2,1)} %copy-done, ...), custom_call_target="tpu_custom_call" | custom-call | flops 1000 | bytes 1000 | tf_op jit(solution)/shard_map/pallas_call | solution.py:695
  106.7 4.5 %shard_map.122 = (bf16[2,592,384]{2,1,0:T(8,128)(2,1)}, bf16[2,592,384]{2,1,0:T(8,128)(2,1)}) custom-call(s32[18]{0:T(128)} %dynamic-slice_bitcast_fusion.meta, bf16[128,768]{1,0:T(8,128)(2,1)} %tokens_ref.9, bf16[128,768]{1,0:T(8,128)(2,1)} %copy-done.3, bf16[128,8064]{1,0:T(8,128)(2,1)} %get-tuple-element.25.left_ref, bf16[128,8064]{1,0:T(8,128)(2,1)} %copy-done, ...), custom_call_target="tpu_custom_call" | custom-call | flops 1000 | bytes 1000 | tf_op jit(solution)/shard_map/pallas_call | solution.py:695
  111.7 6.9 %collective-permute-done.40 = bf16[2,592,384]{2,1,0:T(8,128)(2,1)S(1)} collective-permute-done((bf16[2,592,384]{2,1,0:T(8,128)(2,1)}, bf16[2,592,384]{2,1,0:T(8,128)(2,1)S(1)}, u32[]{:S(2)}, u32[]{:S(2)}) %collective-permute-start.40) | collective-permute-done | bytes 909344 | tf_op jit(solution)/shard_map/ppermute | solution.py:769
  120.3 4.3 %shard_map.121 = (bf16[2,592,384]{2,1,0:T(8,128)(2,1)}, bf16[2,592,384]{2,1,0:T(8,128)(2,1)}) custom-call(s32[18]{0:T(128)} %dynamic-slice_bitcast_fusion.meta, bf16[128,768]{1,0:T(8,128)(2,1)} %tokens_ref.9, bf16[128,768]{1,0:T(8,128)(2,1)} %copy-done.3, bf16[128,8064]{1,0:T(8,128)(2,1)} %get-tuple-element.25.left_ref, bf16[128,8064]{1,0:T(8,128)(2,1)} %copy-done, ...), custom_call_target="tpu_custom_call" | custom-call | flops 1000 | bytes 1000 | tf_op jit(solution)/shard_map/pallas_call | solution.py:695
  126.2 7.1 %collective-permute-done.38 = bf16[2,592,384]{2,1,0:T(8,128)(2,1)} collective-permute-done((bf16[2,592,384]{2,1,0:T(8,128)(2,1)}, bf16[2,592,384]{2,1,0:T(8,128)(2,1)}, u32[]{:S(2)}, u32[]{:S(2)}) %collective-permute-start.38) | collective-permute-done | bytes 909344 | tf_op jit(solution)/shard_map/ppermute | solution.py:769
  138.1 2.8 %collective-permute-start.42 = (bf16[592,384]{1,0:T(8,128)(2,1)S(1)}, bf16[592,384]{1,0:T(8,128)(2,1)}, u32[]{:S(2)}, u32[]{:S(2)}) collective-permute-start(bf16[592,384]{1,0:T(8,128)(2,1)S(1)} %fusion), channel_id=1, source_target_pairs={{0,12},{1,13},{2,14},{3,15},{4,0},{5,1},{6,2},{7,3},{8,4},{9,5},{1... | collective-permute-start | bytes 1363976 | tf_op jit(solution)/shard_map/ppermute | solution.py:776
  140.8 4.8 %shard_map.120 = (bf16[2,592,384]{2,1,0:T(8,128)(2,1)}, bf16[2,592,384]{2,1,0:T(8,128)(2,1)}) custom-call(s32[18]{0:T(128)} %dynamic-slice_bitcast_fusion.meta, bf16[128,768]{1,0:T(8,128)(2,1)} %tokens_ref.9, bf16[128,768]{1,0:T(8,128)(2,1)} %copy-done.3, bf16[128,8064]{1,0:T(8,128)(2,1)} %get-tuple-element.25.left_ref, bf16[128,8064]{1,0:T(8,128)(2,1)} %copy-done, ...), custom_call_target="tpu_custom_call" | custom-call | flops 1000 | bytes 1000 | tf_op jit(solution)/shard_map/pallas_call | solution.py:695
  151.3 4.4 %collective-permute-start.43 = (bf16[592,384]{1,0:T(8,128)(2,1)S(1)}, bf16[592,384]{1,0:T(8,128)(2,1)S(1)}, u32[]{:S(2)}, u32[]{:S(2)}) collective-permute-start(bf16[592,384]{1,0:T(8,128)(2,1)S(1)} %fusion.2), channel_id=1, source_target_pairs={{0,12},{1,13},{2,14},{3,15},{4,0},{5,1},{6,2},{7,3},{8,4},{9,5},{1... | collective-permute-start | bytes 1363976 | tf_op jit(solution)/shard_map/ppermute | solution.py:776
  155.7 7.3 %collective-permute-done.34 = bf16[2,592,384]{2,1,0:T(8,128)(2,1)S(1)} collective-permute-done((bf16[2,592,384]{2,1,0:T(8,128)(2,1)}, bf16[2,592,384]{2,1,0:T(8,128)(2,1)S(1)}, u32[]{:S(2)}, u32[]{:S(2)}) %collective-permute-start.34) | collective-permute-done | bytes 909344 | tf_op jit(solution)/shard_map/ppermute | solution.py:769
  164.6 3.7 %collective-permute-start.44 = (bf16[592,384]{1,0:T(8,128)(2,1)S(1)}, bf16[592,384]{1,0:T(8,128)(2,1)S(1)}, u32[]{:S(2)}, u32[]{:S(2)}) collective-permute-start(bf16[592,384]{1,0:T(8,128)(2,1)S(1)} %fusion.4), channel_id=1, source_target_pairs={{0,12},{1,13},{2,14},{3,15},{4,0},{5,1},{6,2},{7,3},{8,4},{9,5},{1... | collective-permute-start | bytes 1363976 | tf_op jit(solution)/shard_map/ppermute | solution.py:776
  168.3 3.4 %collective-permute-done.35 = bf16[592,384]{1,0:T(8,128)(2,1)S(1)} collective-permute-done((bf16[592,384]{1,0:T(8,128)(2,1)S(1)}, bf16[592,384]{1,0:T(8,128)(2,1)S(1)}, u32[]{:S(2)}, u32[]{:S(2)}) %collective-permute-start.35) | collective-permute-done | bytes 454688 | tf_op jit(solution)/shard_map/ppermute | solution.py:771
  171.7 4.3 %collective-permute-done.44 = bf16[592,384]{1,0:T(8,128)(2,1)S(1)} collective-permute-done((bf16[592,384]{1,0:T(8,128)(2,1)S(1)}, bf16[592,384]{1,0:T(8,128)(2,1)S(1)}, u32[]{:S(2)}, u32[]{:S(2)}) %collective-permute-start.44) | collective-permute-done | bytes 454688 | tf_op jit(solution)/shard_map/ppermute | solution.py:776
  176.3 2.4 %collective-permute-done.45.other_ref = f32[592,384]{1,0:T(8,128)S(1)} collective-permute-done((f32[592,384]{1,0:T(8,128)S(1)}, f32[592,384]{1,0:T(8,128)S(1)}, u32[]{:S(2)}, u32[]{:S(2)}) %collective-permute-start.45) | collective-permute-done | bytes 909344 | tf_op jit(solution)/shard_map/ppermute | solution.py:778
  179.7 7.4 %shard_map.124 = (f32[442944]{0:T(1024)}, f32[442944]{0:T(1024)}, f32[442944]{0:T(1024)}, f32[442944]{0:T(1024)}) custom-call(s32[18]{0:T(128)} %dynamic-slice_bitcast_fusion.meta, f32[592,384]{1,0:T(8,128)} %copy-done.2, f32[592,384]{1,0:T(8,128)} %copy-done.8, f32[442944]{0:T(1024)} %param_ref.1, f32[442944]{0:T(1024)} %first_ref.1, f32[442944]{0:T(1024)} %second_ref.1), custom_call_target="tpu_custom_call" | custom-call | tf_op jit(solution)/shard_map/pallas_call | solution.py:322
  (152 shorter events, 47.7 us)
Async XLA Ops:
  4.0 15.7 %collective-permute-start.3 = (bf16[592,384]{1,0:T(8,128)(2,1)}, bf16[592,384]{1,0:T(8,128)(2,1)S(1)}, u32[]{:S(2)}, u32[]{:S(2)}) collective-permute-start(bf16[592,384]{1,0:T(8,128)(2,1)} %shard_map.118.refs_0_), channel_id=1, source_target_pairs={{0,4},{1,5},{2,6},{3,7},{4,8},{5,9},{6,10},{7,11},{8,12},{9,13},{1... | collective-permute-start | bytes 1363976 | tf_op jit(solution)/shard_map/ppermute | solution.py:747
  7.0 14.2 %collective-permute-start = (bf16[592,384]{1,0:T(8,128)(2,1)}, bf16[592,384]{1,0:T(8,128)(2,1)S(1)}, u32[]{:S(2)}, u32[]{:S(2)}) collective-permute-start(bf16[592,384]{1,0:T(8,128)(2,1)} %shard_map.118.refs_0_), channel_id=1, source_target_pairs={{0,1},{16,18},{1,0},{17,19},{2,3},{18,16},{3,2},{19,17},{4,5},{20,... | collective-permute-start | bytes 1363976 | tf_op jit(solution)/shard_map/ppermute | solution.py:748
  8.5 14.2 %collective-permute-start.1 = (bf16[592,384]{1,0:T(8,128)(2,1)}, bf16[592,384]{1,0:T(8,128)(2,1)S(1)}, u32[]{:S(2)}, u32[]{:S(2)}) collective-permute-start(bf16[592,384]{1,0:T(8,128)(2,1)} %shard_map.118.refs_0_), channel_id=1, source_target_pairs={{0,2},{16,17},{1,3},{17,16},{2,0},{18,19},{3,1},{19,18},{4,6},{20,... | collective-permute-start | bytes 1363976 | tf_op jit(solution)/shard_map/ppermute | solution.py:749
  10.0 12.7 %collective-permute-start.15 = (bf16[592,384]{1,0:T(8,128)(2,1)}, bf16[592,384]{1,0:T(8,128)(2,1)S(1)}, u32[]{:S(2)}, u32[]{:S(2)}) collective-permute-start(bf16[592,384]{1,0:T(8,128)(2,1)} %shard_map.118.refs_0_), channel_id=1, source_target_pairs={{0,16},{16,0},{1,17},{17,1},{2,18},{18,2},{3,19},{19,3},{4,20},{20... | collective-permute-start | bytes 1363976 | tf_op jit(solution)/shard_map/ppermute | solution.py:753
  19.6 13.4 %collective-permute-start.7 = (bf16[592,384]{1,0:T(8,128)(2,1)S(1)}, bf16[592,384]{1,0:T(8,128)(2,1)S(1)}, u32[]{:S(2)}, u32[]{:S(2)}) collective-permute-start(bf16[592,384]{1,0:T(8,128)(2,1)S(1)} %collective-permute-done.3.refs_4_), channel_id=1, source_target_pairs={{0,4},{1,5},{2,6},{3,7},{4,8},{5,9},{6,10},{7,11},{8,12},{9,13},{1... | collective-permute-start | bytes 1363976 | tf_op jit(solution)/shard_map/ppermute | solution.py:747
  19.6 13.4 %collective-permute-start.4 = (bf16[592,384]{1,0:T(8,128)(2,1)S(1)}, bf16[592,384]{1,0:T(8,128)(2,1)S(1)}, u32[]{:S(2)}, u32[]{:S(2)}) collective-permute-start(bf16[592,384]{1,0:T(8,128)(2,1)S(1)} %collective-permute-done.3.refs_4_), channel_id=1, source_target_pairs={{0,1},{16,18},{1,0},{17,19},{2,3},{18,16},{3,2},{19,17},{4,5},{20,... | collective-permute-start | bytes 1363976 | tf_op jit(solution)/shard_map/ppermute | solution.py:748
  21.1 12.4 %collective-permute-start.5 = (bf16[592,384]{1,0:T(8,128)(2,1)S(1)}, bf16[592,384]{1,0:T(8,128)(2,1)S(1)}, u32[]{:S(2)}, u32[]{:S(2)}) collective-permute-start(bf16[592,384]{1,0:T(8,128)(2,1)S(1)} %collective-permute-done.3.refs_4_), channel_id=1, source_target_pairs={{0,2},{16,17},{1,3},{17,16},{2,0},{18,19},{3,1},{19,18},{4,6},{20,... | collective-permute-start | bytes 1363976 | tf_op jit(solution)/shard_map/ppermute | solution.py:749
  22.7 13.4 %collective-permute-start.2 = (bf16[592,384]{1,0:T(8,128)(2,1)S(1)}, bf16[592,384]{1,0:T(8,128)(2,1)S(1)}, u32[]{:S(2)}, u32[]{:S(2)}) collective-permute-start(bf16[592,384]{1,0:T(8,128)(2,1)S(1)} %collective-permute-done.refs_1_), channel_id=1, source_target_pairs={{0,2},{16,17},{1,3},{17,16},{2,0},{18,19},{3,1},{19,18},{4,6},{20,... | collective-permute-start | bytes 1363976 | tf_op jit(solution)/shard_map/ppermute | solution.py:750
  33.6 14.3 %collective-permute-start.11 = (bf16[592,384]{1,0:T(8,128)(2,1)S(1)}, bf16[592,384]{1,0:T(8,128)(2,1)S(1)}, u32[]{:S(2)}, u32[]{:S(2)}) collective-permute-start(bf16[592,384]{1,0:T(8,128)(2,1)S(1)} %collective-permute-done.7.refs_8_), channel_id=1, source_target_pairs={{0,4},{1,5},{2,6},{3,7},{4,8},{5,9},{6,10},{7,11},{8,12},{9,13},{1... | collective-permute-start | bytes 1363976 | tf_op jit(solution)/shard_map/ppermute | solution.py:747
  34.3 13.6 %collective-permute-start.8 = (bf16[592,384]{1,0:T(8,128)(2,1)S(1)}, bf16[592,384]{1,0:T(8,128)(2,1)S(1)}, u32[]{:S(2)}, u32[]{:S(2)}) collective-permute-start(bf16[592,384]{1,0:T(8,128)(2,1)S(1)} %collective-permute-done.7.refs_8_), channel_id=1, source_target_pairs={{0,1},{16,18},{1,0},{17,19},{2,3},{18,16},{3,2},{19,17},{4,5},{20,... | collective-permute-start | bytes 1363976 | tf_op jit(solution)/shard_map/ppermute | solution.py:748
  36.1 12.3 %collective-permute-start.9 = (bf16[592,384]{1,0:T(8,128)(2,1)S(1)}, bf16[592,384]{1,0:T(8,128)(2,1)S(1)}, u32[]{:S(2)}, u32[]{:S(2)}) collective-permute-start(bf16[592,384]{1,0:T(8,128)(2,1)S(1)} %collective-permute-done.7.refs_8_), channel_id=1, source_target_pairs={{0,2},{16,17},{1,3},{17,16},{2,0},{18,19},{3,1},{19,18},{4,6},{20,... | collective-permute-start | bytes 1363976 | tf_op jit(solution)/shard_map/ppermute | solution.py:749
  38.2 13.5 %collective-permute-start.6 = (bf16[592,384]{1,0:T(8,128)(2,1)S(1)}, bf16[592,384]{1,0:T(8,128)(2,1)S(1)}, u32[]{:S(2)}, u32[]{:S(2)}) collective-permute-start(bf16[592,384]{1,0:T(8,128)(2,1)S(1)} %collective-permute-done.4.refs_5_), channel_id=1, source_target_pairs={{0,2},{16,17},{1,3},{17,16},{2,0},{18,19},{3,1},{19,18},{4,6},{20,... | collective-permute-start | bytes 1363976 | tf_op jit(solution)/shard_map/ppermute | solution.py:750
  53.3 13.1 %collective-permute-start.10 = (bf16[592,384]{1,0:T(8,128)(2,1)S(1)}, bf16[592,384]{1,0:T(8,128)(2,1)}, u32[]{:S(2)}, u32[]{:S(2)}) collective-permute-start(bf16[592,384]{1,0:T(8,128)(2,1)S(1)} %collective-permute-done.8.refs_9_), channel_id=1, source_target_pairs={{0,2},{16,17},{1,3},{17,16},{2,0},{18,19},{3,1},{19,18},{4,6},{20,... | collective-permute-start | bytes 1363976 | tf_op jit(solution)/shard_map/ppermute | solution.py:750
  53.9 13.5 %collective-permute-start.27 = (bf16[592,384]{1,0:T(8,128)(2,1)S(1)}, bf16[592,384]{1,0:T(8,128)(2,1)S(1)}, u32[]{:S(2)}, u32[]{:S(2)}) collective-permute-start(bf16[592,384]{1,0:T(8,128)(2,1)S(1)} %collective-permute-done.11.refs_12_), channel_id=1, source_target_pairs={{0,16},{16,0},{1,17},{17,1},{2,18},{18,2},{3,19},{19,3},{4,20},{20... | collective-permute-start | bytes 1363976 | tf_op jit(solution)/shard_map/ppermute | solution.py:753
  54.6 12.9 %collective-permute-start.24 = (bf16[592,384]{1,0:T(8,128)(2,1)S(1)}, bf16[592,384]{1,0:T(8,128)(2,1)S(1)}, u32[]{:S(2)}, u32[]{:S(2)}) collective-permute-start(bf16[592,384]{1,0:T(8,128)(2,1)S(1)} %collective-permute-done.8.refs_9_), channel_id=1, source_target_pairs={{0,16},{16,0},{1,17},{17,1},{2,18},{18,2},{3,19},{19,3},{4,20},{20... | collective-permute-start | bytes 1363976 | tf_op jit(solution)/shard_map/ppermute | solution.py:753
  105.0 13.6 %collective-permute-start.40 = (bf16[2,592,384]{2,1,0:T(8,128)(2,1)}, bf16[2,592,384]{2,1,0:T(8,128)(2,1)S(1)}, u32[]{:S(2)}, u32[]{:S(2)}) collective-permute-start(bf16[2,592,384]{2,1,0:T(8,128)(2,1)} %get-tuple-element.35), channel_id=1, source_target_pairs={{0,2},{16,17},{1,3},{17,16},{2,0},{18,19},{3,1},{19,18},{4,6},{20,... | collective-permute-start | bytes 2727944 | tf_op jit(solution)/shard_map/ppermute | solution.py:769
  111.2 22.1 %collective-permute-start.38 = (bf16[2,592,384]{2,1,0:T(8,128)(2,1)}, bf16[2,592,384]{2,1,0:T(8,128)(2,1)}, u32[]{:S(2)}, u32[]{:S(2)}) collective-permute-start(bf16[2,592,384]{2,1,0:T(8,128)(2,1)} %get-tuple-element.33), channel_id=1, source_target_pairs={{0,2},{16,17},{1,3},{17,16},{2,0},{18,19},{3,1},{19,18},{4,6},{20,... | collective-permute-start | bytes 2727944 | tf_op jit(solution)/shard_map/ppermute | solution.py:769
  118.7 18.2 %collective-permute-start.41 = (bf16[592,384]{1,0:T(8,128)(2,1)S(1)}, bf16[592,384]{1,0:T(8,128)(2,1)}, u32[]{:S(2)}, u32[]{:S(2)}) collective-permute-start(bf16[592,384]{1,0:T(8,128)(2,1)S(1)} %fusion.9), channel_id=1, source_target_pairs={{0,1},{16,18},{1,0},{17,19},{2,3},{18,16},{3,2},{19,17},{4,5},{20,... | collective-permute-start | bytes 1363976 | tf_op jit(solution)/shard_map/ppermute | solution.py:771
  124.5 23.3 %collective-permute-start.36 = (bf16[2,592,384]{2,1,0:T(8,128)(2,1)}, bf16[2,592,384]{2,1,0:T(8,128)(2,1)S(1)}, u32[]{:S(2)}, u32[]{:S(2)}) collective-permute-start(bf16[2,592,384]{2,1,0:T(8,128)(2,1)} %get-tuple-element.31), channel_id=1, source_target_pairs={{0,2},{16,17},{1,3},{17,16},{2,0},{18,19},{3,1},{19,18},{4,6},{20,... | collective-permute-start | bytes 2727944 | tf_op jit(solution)/shard_map/ppermute | solution.py:769
  135.3 14.2 %collective-permute-start.39 = (bf16[592,384]{1,0:T(8,128)(2,1)}, bf16[592,384]{1,0:T(8,128)(2,1)}, u32[]{:S(2)}, u32[]{:S(2)}) collective-permute-start(bf16[592,384]{1,0:T(8,128)(2,1)} %fusion.8), channel_id=1, source_target_pairs={{0,1},{16,18},{1,0},{17,19},{2,3},{18,16},{3,2},{19,17},{4,5},{20,... | collective-permute-start | bytes 1363976 | tf_op jit(solution)/shard_map/ppermute | solution.py:771
  138.1 11.7 %collective-permute-start.42 = (bf16[592,384]{1,0:T(8,128)(2,1)S(1)}, bf16[592,384]{1,0:T(8,128)(2,1)}, u32[]{:S(2)}, u32[]{:S(2)}) collective-permute-start(bf16[592,384]{1,0:T(8,128)(2,1)S(1)} %fusion), channel_id=1, source_target_pairs={{0,12},{1,13},{2,14},{3,15},{4,0},{5,1},{6,2},{7,3},{8,4},{9,5},{1... | collective-permute-start | bytes 1363976 | tf_op jit(solution)/shard_map/ppermute | solution.py:776
  145.6 17.5 %collective-permute-start.34 = (bf16[2,592,384]{2,1,0:T(8,128)(2,1)}, bf16[2,592,384]{2,1,0:T(8,128)(2,1)S(1)}, u32[]{:S(2)}, u32[]{:S(2)}) collective-permute-start(bf16[2,592,384]{2,1,0:T(8,128)(2,1)} %get-tuple-element.29), channel_id=1, source_target_pairs={{0,2},{16,17},{1,3},{17,16},{2,0},{18,19},{3,1},{19,18},{4,6},{20,... | collective-permute-start | bytes 2727944 | tf_op jit(solution)/shard_map/ppermute | solution.py:769
  147.9 16.4 %collective-permute-start.37 = (bf16[592,384]{1,0:T(8,128)(2,1)S(1)}, bf16[592,384]{1,0:T(8,128)(2,1)S(1)}, u32[]{:S(2)}, u32[]{:S(2)}) collective-permute-start(bf16[592,384]{1,0:T(8,128)(2,1)S(1)} %fusion.7), channel_id=1, source_target_pairs={{0,1},{16,18},{1,0},{17,19},{2,3},{18,16},{3,2},{19,17},{4,5},{20,... | collective-permute-start | bytes 1363976 | tf_op jit(solution)/shard_map/ppermute | solution.py:771
  151.3 13.0 %collective-permute-start.43 = (bf16[592,384]{1,0:T(8,128)(2,1)S(1)}, bf16[592,384]{1,0:T(8,128)(2,1)S(1)}, u32[]{:S(2)}, u32[]{:S(2)}) collective-permute-start(bf16[592,384]{1,0:T(8,128)(2,1)S(1)} %fusion.2), channel_id=1, source_target_pairs={{0,12},{1,13},{2,14},{3,15},{4,0},{5,1},{6,2},{7,3},{8,4},{9,5},{1... | collective-permute-start | bytes 1363976 | tf_op jit(solution)/shard_map/ppermute | solution.py:776
  (56 other events, 660.9 us)

commit v5 on v4

--- a/solution.py
+++ b/solution.py
@@ -3,7 +3,6 @@
 
 import jax
 import jax.numpy as jnp
-import numpy as np
 from jax import lax
 from jax.experimental import pallas as pl
 from jax.experimental.pallas import tpu as pltpu
@@ -245,36 +244,44 @@
 RED_ROW = 6144
 BIAS_ROW = 9216
 LEFT = 4608
-BLOCK_LINES = 872
+FRONT = 72
+BLOCKS = 2
+BLOCK_LINES = 1736
 RIGHT = 9 * HALF
-VMEM_CAP = 64 * 1024 * 1000
+MIB = 1024 * 1024
 
 f32 = jnp.float32
 bf16 = jnp.bfloat16
 
 
+def place():
+    here, core = lax.axis_index("shard"), lax.axis_index("rep")
+    plane, spot = here // 4, here % 4
+    flip = [0, core + 1, 2 - core, 3]
+    back = [0, 2 - core, core + 1, 3]
+    listed = [(9 * here) // 2, here % 2, 3 * core, 3 - 3 * core, HALF * core, HALF - HALF * core]
+    listed += [(plane + 4 - t) % 4 for t in range(4)]
+    return listed + [spot ^ k for k in flip] + [spot ^ k for k in back]
+
+
 def swap_half(block):
     return pltpu.roll(block, 64, 1)
 
 
-def frame_kernel(flat_ref, out_ref, lines, framed):
-    here_at, core = lax.axis_index("shard"), lax.axis_index("rep")
-    shift, odd, first_col = (9 * here_at) // 2, here_at % 2, 3 * core
-    lines[0:8, :] = jnp.zeros((8, 128), f32)
-    lines[LOCAL_LINES : LOCAL_LINES + 16, :] = jnp.zeros((16, 128), f32)
-    lines[8:3464, :] = flat_ref[pl.ds(0, 442368)].reshape(3456, 128)
-    lines[3464:3468, :] = flat_ref[pl.ds(442368, 512)].reshape(4, 128)
-    lines[3468:3469, 0:64] = flat_ref[pl.ds(442880, 64)].reshape(1, 64)
-    framed[0:96, :] = jnp.zeros((96, 128), f32)
-    framed[LINES - 96 : LINES, :] = jnp.zeros((96, 128), f32)
-    low = lax.broadcasted_iota(jnp.int32, (LOCAL_LINES, 128), 1) < 64
-    here = lines[8 : 8 + LOCAL_LINES, :]
-    before = lines[7 : 7 + LOCAL_LINES, :]
-    moved = jnp.where(low, swap_half(before), swap_half(here))
-    framed[pl.ds(shift, LOCAL_LINES), :] = jnp.where(odd == 1, moved, here)
+def frame_kernel(flat_ref, out_ref, lines):
+    shift, odd, first_col = place()[:3]
+    lines[0:FRONT, :] = jnp.zeros((FRONT, 128), f32)
+    lines[FRONT : FRONT + 3456, :] = flat_ref[pl.ds(0, 442368)].reshape(3456, 128)
+    lines[FRONT + 3456 : FRONT + LINES, :] = jnp.zeros((LINES - 3456, 128), f32)
+    lines[FRONT + 3456 : FRONT + 3460, :] = flat_ref[pl.ds(442368, 512)].reshape(4, 128)
+    lines[FRONT + 3460 : FRONT + 3461, 0:64] = flat_ref[pl.ds(442880, 64)].reshape(1, 64)
+    low = lax.broadcasted_iota(jnp.int32, (FRAME, 128), 1) < 64
     for j in range(3):
-        column = framed[pl.ds(first_col + j, FRAME, stride=6), :]
-        out_ref[:, 128 * j : 128 * (j + 1)] = column.astype(bf16)
+        at = FRONT + first_col + j - shift
+        here = lines[pl.ds(at, FRAME, stride=6), :]
+        before = lines[pl.ds(at - 1, FRAME, stride=6), :]
+        moved = jnp.where(low, swap_half(before), swap_half(here))
+        out_ref[:, 128 * j : 128 * (j + 1)] = jnp.where(odd == 1, moved, here).astype(bf16)
 
 
 def make_frame(params):
@@ -283,22 +290,20 @@
         out_shape=jax.ShapeDtypeStruct((FRAME, HALF), bf16),
         in_specs=[pl.BlockSpec(memory_space=pltpu.VMEM)],
         out_specs=pl.BlockSpec(memory_space=pltpu.VMEM),
-        scratch_shapes=[
-            pltpu.VMEM((LOCAL_LINES + 16, 128), f32),
-            pltpu.VMEM((LINES, 128), f32),
-        ],
+        scratch_shapes=[pltpu.VMEM((FRONT + LINES, 128), f32)],
+        compiler_params=pltpu.CompilerParams(vmem_limit_bytes=12 * MIB),
     )(params)
 
 
 def finish_kernel(
-    meta, mine_ref, other_ref, param_ref, first_ref, second_ref, grad_out, param_out, first_out, second_out, framed
+    mine_ref, other_ref, param_ref, first_ref, second_ref, grad_out, param_out, first_out, second_out, framed
 ):
-    shift, odd, first_col, other_col = meta[0], meta[1], meta[2], meta[3]
+    shift, odd, first_col, other_col = place()[:4]
     step = pl.program_id(0)
 
     @pl.when(step == 0)
     def _():
-        framed[LINES : LINES + 16, :] = jnp.zeros((16, 128), f32)
+        framed[LINES : LINES + 48, :] = jnp.zeros((48, 128), f32)
         for j in range(3):
             at = slice(128 * j, 128 * (j + 1))
             framed[pl.ds(first_col + j, FRAME, stride=6), :] = mine_ref[:, at]
@@ -316,17 +321,18 @@
     second_out[...] = new_second
 
 
-def finish(mine, other, meta, params, first_moment, second_moment):
+def finish(mine, other, params, first_moment, second_moment):
     vmem_spec = pl.BlockSpec(memory_space=pltpu.VMEM)
     block_spec = pl.BlockSpec((BLOCK_LINES * 128,), lambda i: (i,))
     return pl.pallas_call(
         finish_kernel,
-        grid=(4,),
+        grid=(BLOCKS,),
         out_shape=[jax.ShapeDtypeStruct((LOCAL,), f32)] * 4,
-        in_specs=[pl.BlockSpec(memory_space=pltpu.SMEM), vmem_spec, vmem_spec] + [block_spec] * 3,
+        in_specs=[vmem_spec, vmem_spec] + [block_spec] * 3,
         out_specs=[block_spec] * 4,
-        scratch_shapes=[pltpu.VMEM((LINES + 16, 128), f32)],
-    )(meta, mine, other, params, first_moment, second_moment)
+        scratch_shapes=[pltpu.VMEM((LINES + 48, 128), f32)],
+        compiler_params=pltpu.CompilerParams(vmem_limit_bytes=30 * MIB),
+    )(mine, other, params, first_moment, second_moment)
 
 
 def dot_nn(left_side, right_side):
@@ -337,7 +343,7 @@
     return jnp.mean(block, axis=-1, keepdims=True)
 
 
-def layer_kernel(meta, length_ref, tokens_ref, cot_ref, *refs):
+def layer_kernel(length_ref, tokens_ref, cot_ref, *refs):
     frames = refs[:32]
     block_ref, input_ref, left_ref, right_ref, sums_ref = refs[32:37]
     (
@@ -354,6 +360,7 @@
         sem_tail,
     ) = refs[37:]
     bias_grads = sums_ref
+    meta = place()
     length = length_ref[0]
     cols = (pl.multiple_of(meta[4], 128), pl.multiple_of(meta[5], 128))
 
@@ -371,22 +378,21 @@
             sem_tail.at[side, shard],
         )
 
-    def start_copies(quad, mains, ends):
+    def each_frame(t):
+        for side in range(2):
+            for j in range(4):
+                yield frames[16 * side + 4 * t + j], 4 * meta[6 + t] + meta[10 + 4 * side + j], side
+
+    for t in range(4):
+        for frame, shard, side in each_frame(t):
+            tail_copy(frame, shard, side).start()
+    for now in (True, False):
         for t in range(4):
 
-            @pl.when(meta[6 + quad] == t)
+            @pl.when((meta[6 + t] == 0) == now)
             def _():
-                for side in range(2):
-                    for j in range(4):
-                        shard = 4 * quad + meta[10 + 4 * side + j]
-                        if mains:
-                            main_copy(frames[16 * side + 4 * t + j], shard, side).start()
-                        if ends:
-                            tail_copy(frames[16 * side + 4 * t + j], shard, side).start()
-
-    start_copies(3, False, True)
-    for quad in range(4):
-        start_copies(quad, True, quad < 3)
+                for frame, shard, side in each_frame(t):
+                    main_copy(frame, shard, side).start()
 
     def arrive(first, last):
         for shard in range(first, last):
@@ -538,7 +544,7 @@
         left_ref[:, 4608 + HALF * k : 4608 + HALF * (k + 1)] = rights[k, :, pl.ds(cols[1], HALF)]
 
 
-def run_layer(meta, lengths, tokens, cotangent, frames):
+def run_layer(lengths, tokens, cotangent, frames):
     any_spec = pl.BlockSpec(memory_space=pl.ANY)
     vmem_spec = pl.BlockSpec(memory_space=pltpu.VMEM)
     rows = tokens.shape[0]
@@ -552,7 +558,7 @@
             jax.ShapeDtypeStruct((rows, RIGHT), bf16),
             jax.ShapeDtypeStruct((16, ROW), f32),
         ],
-        in_specs=[pl.BlockSpec(memory_space=pltpu.SMEM)] * 2 + [vmem_spec] * 2 + [any_spec] * 32,
+        in_specs=[pl.BlockSpec(memory_space=pltpu.SMEM)] + [vmem_spec] * 2 + [any_spec] * 32,
         out_specs=[vmem_spec] * 5,
         scratch_shapes=[
             pltpu.VMEM((ROWS, ROW), bf16),
@@ -567,14 +573,13 @@
             pltpu.SemaphoreType.DMA((2, 16)),
             pltpu.SemaphoreType.DMA((2, 16)),
         ],
-        compiler_params=pltpu.CompilerParams(vmem_limit_bytes=VMEM_CAP),
-    )(meta, lengths, tokens, cotangent, *frames)
+        compiler_params=pltpu.CompilerParams(vmem_limit_bytes=42 * MIB),
+    )(lengths, tokens, cotangent, *frames)
     return out
 
 
 def grad_kernel(
     slot,
-    meta,
     tokens_ref,
     tokens_other,
     left_ref,
@@ -591,6 +596,7 @@
     sem_in,
     sem_out,
 ):
+    meta = place()
     quad = meta[6 + slot]
 
     def load(pieces):
@@ -630,7 +636,7 @@
                 grads[pl.ds(at, rows_used), 128 * j : 128 * (j + 1)] = stage[j, 0:rows_used, :].astype(bf16)
             return carry
 
-        lax.fori_loop(0, chunks, step, 0, unroll=True)
+        lax.fori_loop(0, chunks, step, 0, unroll=min(chunks, 3))
 
     def plain(first, right_first, chunks, row):
         def step(i, carry):
@@ -639,7 +645,7 @@
             grads[pl.ds(pl.multiple_of(row + 256 * i, 16), 256), :] = block.astype(bf16)
             return carry
 
-        lax.fori_loop(0, chunks, step, 0, unroll=True)
+        lax.fori_loop(0, chunks, step, 0, unroll=min(chunks, 3))
 
     def last_rows(first, right_first):
         block = inner_rows(left[:, first : first + 128], right[:, right_first : right_first + HALF])
@@ -688,14 +694,15 @@
         copy.wait()
 
 
-def quad_grads(slot, meta, operands):
+def quad_grads(slot, operands):
     any_spec = pl.BlockSpec(memory_space=pl.ANY)
+    hbm_spec = pl.BlockSpec(memory_space=pltpu.HBM)
     vmem_spec = pl.BlockSpec(memory_space=pltpu.VMEM)
     frames = jax.ShapeDtypeStruct((2, FRAME, HALF), bf16)
     return pl.pallas_call(
         functools.partial(grad_kernel, slot),
         out_shape=[frames, frames],
-        in_specs=[pl.BlockSpec(memory_space=pltpu.SMEM)] + [any_spec] * 5 + [vmem_spec] * 2,
+        in_specs=[any_spec] * 2 + [hbm_spec, any_spec, hbm_spec] + [vmem_spec] * 2,
         out_specs=[any_spec] * 2,
         scratch_shapes=[
             pltpu.VMEM((256, 2304), bf16),
@@ -705,8 +712,9 @@
             pltpu.SemaphoreType.DMA((8,)),
             pltpu.SemaphoreType.DMA((4,)),
         ],
+        compiler_params=pltpu.CompilerParams(vmem_limit_bytes=14 * MIB),
         cost_estimate=pl.CostEstimate(flops=1000, bytes_accessed=1000, transcendentals=0),
-    )(meta, *operands)
+    )(*operands)
 
 
 def plane_moves(n):
@@ -717,27 +725,11 @@
     return near, far
 
 
-def device_table(n):
-    rows = []
-    for core in range(2):
-        for here in range(n):
-            plane, spot = divmod(here, 4)
-            spots = ((0, 1, 2, 3), (0, 2, 1, 3))
-            row = [(9 * here) // 2, here % 2, 3 * core, 3 - 3 * core, HALF * core, HALF - HALF * core]
-            row += [(plane - t) % 4 for t in range(4)]
-            row += [spot ^ k for k in spots[core]] + [spot ^ k for k in spots[1 - core]]
-            rows.append(row)
-    return np.array(rows, np.int32)
-
-
 def on_device_planes(hidden_states, cotangent, lengths, params, first_moment, second_moment):
     n = 16
     both = ("rep", "shard")
     near, far = plane_moves(n)
     swap = [(0, 1), (1, 0)]
-    device = lax.axis_index("rep") * n + lax.axis_index("shard")
-    meta = lax.dynamic_slice(jnp.asarray(device_table(n)), (device, 0), (1, 18)).reshape(18)
-
     own = make_frame(params)
     mine, other = [], []
     up = [(s, (s + 4) % n) for s in range(n)]
@@ -752,7 +744,7 @@
         mine += group
         other += [lax.ppermute(piece, "rep", swap) for piece in group]
 
-    block_out, input_grad, left, right, sums = run_layer(meta, lengths, hidden_states, cotangent, mine + other)
+    block_out, input_grad, left, right, sums = run_layer(lengths, hidden_states, cotangent, mine + other)
 
     operands = (
         hidden_states,
@@ -765,7 +757,7 @@
     )
     passed = None
     for t in (3, 2, 1, 0):
-        low, high = quad_grads(t, meta, operands)
+        low, high = quad_grads(t, operands)
         from_far = lax.ppermute(high, both, far)
         away = (low[1].astype(f32) + from_far[1].astype(f32)).astype(bf16)
         from_near = lax.ppermute(away, both, near)
@@ -775,7 +767,7 @@
         if t > 0:
             passed = lax.ppermute(total.astype(bf16), "shard", down)
     weight_grad, new_params, new_first, new_second = finish(
-        total, lax.ppermute(total, "rep", swap), meta, params, first_moment, second_moment
+        total, lax.ppermute(total, "rep", swap), params, first_moment, second_moment
     )
     return (block_out, input_grad, weight_grad, new_params, new_first, new_second)
 

time: 188 us -> 180 us (0.957)
  Pallas kernels: 49.3 us -> 33.8 us
  waiting for transfers between devices: 80.2 us -> 92.5 us
  other arithmetic: 5.56 us -> 1.36 us
    ppermute x4, waiting for transfers between devices: 21.9 us -> 32 us  [on_device_planes(): from_far = lax.ppermute(high, both, far)]
    pallas_call x4, Pallas kernels: 18.4 us -> 10.2 us  [quad_grads(): pl.pallas_call(functools.partial(grad_kernel, slot), out_shape=[frames, f...]
    pallas_call x1, Pallas kernels: 7.43 us -> 4.27 us  [finish(): pl.pallas_call(finish_kernel, grid=(BLOCKS,), out_shape=[jax.ShapeDtypeSt...]
    unnamed x68 -> x28, local copies, waits for them, and re-layouts: 2.41 us -> 5.32 us
    pallas_call x1, Pallas kernels: 3.32 us -> 0.46 us  [make_frame(): pl.pallas_call(frame_kernel, out_shape=jax.ShapeDtypeStruct((FRAME, HALF)...]
    convert_element_type x3, other arithmetic: 2.97 us -> 0.68 us  [on_device_planes(): passed = lax.ppermute(total.astype(bf16), 'shard', down)]
    convert_element_type x4, other arithmetic: 2.38 us -> 0.48 us  [on_device_planes(): away = (low[1].astype(f32) + from_far[1].astype(f32)).astype(bf16)]
  transfers between devices with their start and end apart: 46 -> 46, of which waited for: 19 -> 20; matrix products, arithmetic and copies ran while one was open for 3% -> 1% of each run, Pallas kernels for 7% -> 4%
where the time goes in v5:
time: 180 us
  waiting for transfers between devices  92.5 us (51%)
  starting transfers between devices  45.7 us (25%)
  Pallas kernels  33.8 us (19%)
  local copies, waits for them, and re-layouts  5.32 us (3%)
    ppermute x4, waiting for transfers between devices, on_device_planes(): from_far = lax.ppermute(high, both, far)  32 us
    ppermute x3, waiting for transfers between devices, on_device_planes(): zero = own if t == 0 else lax.ppermute(zero, 'shard', up)  28.4 us
    pallas_call x1, Pallas kernels, run_layer(): pl.pallas_call(layer_kernel, out_shape=[thin, thin, jax.ShapeDtypeStruct(...  18.9 us
    pallas_call x4, Pallas kernels, quad_grads(): pl.pallas_call(functools.partial(grad_kernel, slot), out_shape=[frames, f...  10.2 us
    ppermute x3, starting transfers between devices, on_device_planes(): passed = lax.ppermute(total.astype(bf16), 'shard', down)  10 us
    ppermute x4, waiting for transfers between devices, on_device_planes(): three = lax.ppermute(one, both, far)  8.94 us
    ppermute x4, starting transfers between devices, on_device_planes(): from_near = lax.ppermute(away, both, near)  6.25 us
    ppermute x4, starting transfers between devices, on_device_planes(): one = lax.ppermute(zero, both, near)  5.97 us
  transfers between devices with their start and end apart: 46, of which 20 were waited for; matrix products, arithmetic and copies ran while one was open for 1% of the time, Pallas kernels for 4%

profile of v5, /device:TPU:0, one launch (start us, length us, event | category | flops | bytes accessed | tf_op | source)
XLA Modules:
  0.0 180.2 jit_solution(15888054957723656070)
XLA Ops:
  2.6 3.1 %collective-permute-start.3 = (bf16[592,384]{1,0:T(8,128)(2,1)S(1)}, bf16[592,384]{1,0:T(8,128)(2,1)S(1)}, u32[]{:S(2)}, u32[]{:S(2)}) collective-permute-start(bf16[592,384]{1,0:T(8,128)(2,1)S(1)} %shard_map.109.refs_0_), channel_id=1, source_target_pairs={{0,4},{1,5},{2,6},{3,7},{4,8},{5,9},{6,10},{7,11},{8,12},{9,13},{1... | collective-permute-start | bytes 1363976 | tf_op jit(solution)/shard_map/ppermute | solution.py:739
  8.7 9.4 %collective-permute-done.3.refs_4_ = bf16[592,384]{1,0:T(8,128)(2,1)S(1)} collective-permute-done((bf16[592,384]{1,0:T(8,128)(2,1)S(1)}, bf16[592,384]{1,0:T(8,128)(2,1)S(1)}, u32[]{:S(2)}, u32[]{:S(2)}) %collective-permute-start.3) | collective-permute-done | bytes 454688 | tf_op jit(solution)/shard_map/ppermute | solution.py:739
  21.7 9.8 %collective-permute-done.7.refs_8_ = bf16[592,384]{1,0:T(8,128)(2,1)S(1)} collective-permute-done((bf16[592,384]{1,0:T(8,128)(2,1)S(1)}, bf16[592,384]{1,0:T(8,128)(2,1)S(1)}, u32[]{:S(2)}, u32[]{:S(2)}) %collective-permute-start.7) | collective-permute-done | bytes 454688 | tf_op jit(solution)/shard_map/ppermute | solution.py:739
  37.2 9.1 %collective-permute-done.11.refs_12_ = bf16[592,384]{1,0:T(8,128)(2,1)S(1)} collective-permute-done((bf16[592,384]{1,0:T(8,128)(2,1)S(1)}, bf16[592,384]{1,0:T(8,128)(2,1)S(1)}, u32[]{:S(2)}, u32[]{:S(2)}) %collective-permute-start.11) | collective-permute-done | bytes 454688 | tf_op jit(solution)/shard_map/ppermute | solution.py:739
  52.9 4.6 %collective-permute-done.12.refs_13_ = bf16[592,384]{1,0:T(8,128)(2,1)S(1)} collective-permute-done((bf16[592,384]{1,0:T(8,128)(2,1)S(1)}, bf16[592,384]{1,0:T(8,128)(2,1)S(1)}, u32[]{:S(2)}, u32[]{:S(2)}) %collective-permute-start.12) | collective-permute-done | bytes 454688 | tf_op jit(solution)/shard_map/ppermute | solution.py:740
  57.5 2.4 %collective-permute-done.13.refs_14_ = bf16[592,384]{1,0:T(8,128)(2,1)S(1)} collective-permute-done((bf16[592,384]{1,0:T(8,128)(2,1)S(1)}, bf16[592,384]{1,0:T(8,128)(2,1)S(1)}, u32[]{:S(2)}, u32[]{:S(2)}) %collective-permute-start.13) | collective-permute-done | bytes 454688 | tf_op jit(solution)/shard_map/ppermute | solution.py:741
  61.5 3.3 %collective-permute-done.10.refs_11_ = bf16[592,384]{1,0:T(8,128)(2,1)S(1)} collective-permute-done((bf16[592,384]{1,0:T(8,128)(2,1)S(1)}, bf16[592,384]{1,0:T(8,128)(2,1)S(1)}, u32[]{:S(2)}, u32[]{:S(2)}) %collective-permute-start.10) | collective-permute-done | bytes 454688 | tf_op jit(solution)/shard_map/ppermute | solution.py:742
  66.2 3.4 %collective-permute-done.14.refs_15_ = bf16[592,384]{1,0:T(8,128)(2,1)S(1)} collective-permute-done((bf16[592,384]{1,0:T(8,128)(2,1)S(1)}, bf16[592,384]{1,0:T(8,128)(2,1)S(1)}, u32[]{:S(2)}, u32[]{:S(2)}) %collective-permute-start.14) | collective-permute-done | bytes 454688 | tf_op jit(solution)/shard_map/ppermute | solution.py:742
  72.7 18.9 %shard_map.110 = (bf16[128,768]{1,0:T(8,128)(2,1)}, bf16[128,768]{1,0:T(8,128)(2,1)}, bf16[128,8064]{1,0:T(8,128)(2,1)}, bf16[128,3456]{1,0:T(8,128)(2,1)}, f32[16,768]{1,0:T(8,128)S(1)}) custom-call(s32[1]{0:T(128)S(6)} %copy.12.length_ref, bf16[128,768]{1,0:T(8,128)(2,1)S(1)} %copy-done.4, bf16[128,768]{1,0:T(8,128)(2,1)S(1)} %copy-done.7, ...), custom_call_target="tpu_custom_call" | custom-call | tf_op jit(solution)/shard_map/pallas_call | solution.py:552
  92.4 3.5 %collective-permute-done.31.tokens_other = bf16[128,768]{1,0:T(8,128)(2,1)S(1)} collective-permute-done((bf16[128,768]{1,0:T(8,128)(2,1)S(1)}, bf16[128,768]{1,0:T(8,128)(2,1)S(1)}, u32[]{:S(2)}, u32[]{:S(2)}) %collective-permute-start.31) | collective-permute-done | bytes 196640 | tf_op jit(solution)/shard_map/ppermute | solution.py:751
  99.1 2.6 %shard_map.114 = (bf16[2,592,384]{2,1,0:T(8,128)(2,1)S(1)}, bf16[2,592,384]{2,1,0:T(8,128)(2,1)S(1)}) custom-call(bf16[128,768]{1,0:T(8,128)(2,1)S(1)} %copy-done.4, bf16[128,768]{1,0:T(8,128)(2,1)S(1)} %collective-permute-done.31.tokens_other, bf16[128,8064]{1,0:T(8,128)(2,1)S(1)} %copy-done, bf16[128,8064]{1,0:T(8,128)(2,1)S(1)} %collective-permute-done.32.left_other, ...), custom_call_target="tpu_custom_call" | custom-call | flops 1000 | bytes 1000 | tf_op jit(solution)/shard_map/pallas_call | solution.py:702
  106.2 8.9 %collective-permute-done.40 = bf16[2,592,384]{2,1,0:T(8,128)(2,1)S(1)} collective-permute-done((bf16[2,592,384]{2,1,0:T(8,128)(2,1)S(1)}, bf16[2,592,384]{2,1,0:T(8,128)(2,1)S(1)}, u32[]{:S(2)}, u32[]{:S(2)}) %collective-permute-start.40) | collective-permute-done | bytes 909344 | tf_op jit(solution)/shard_map/ppermute | solution.py:761
  116.8 2.5 %shard_map.112 = (bf16[2,592,384]{2,1,0:T(8,128)(2,1)S(1)}, bf16[2,592,384]{2,1,0:T(8,128)(2,1)S(1)}) custom-call(bf16[128,768]{1,0:T(8,128)(2,1)S(1)} %copy-done.4, bf16[128,768]{1,0:T(8,128)(2,1)S(1)} %collective-permute-done.31.tokens_other, bf16[128,8064]{1,0:T(8,128)(2,1)S(1)} %copy-done, bf16[128,8064]{1,0:T(8,128)(2,1)S(1)} %collective-permute-done.32.left_other, ...), custom_call_target="tpu_custom_call" | custom-call | flops 1000 | bytes 1000 | tf_op jit(solution)/shard_map/pallas_call | solution.py:702
  121.0 8.7 %collective-permute-done.38 = bf16[2,592,384]{2,1,0:T(8,128)(2,1)S(1)} collective-permute-done((bf16[2,592,384]{2,1,0:T(8,128)(2,1)S(1)}, bf16[2,592,384]{2,1,0:T(8,128)(2,1)S(1)}, u32[]{:S(2)}, u32[]{:S(2)}) %collective-permute-start.38) | collective-permute-done | bytes 909344 | tf_op jit(solution)/shard_map/ppermute | solution.py:761
  131.6 3.3 %collective-permute-start.42 = (bf16[592,384]{1,0:T(8,128)(2,1)S(1)}, bf16[592,384]{1,0:T(8,128)(2,1)S(1)}, u32[]{:S(2)}, u32[]{:S(2)}) collective-permute-start(bf16[592,384]{1,0:T(8,128)(2,1)S(1)} %fusion), channel_id=1, source_target_pairs={{0,12},{1,13},{2,14},{3,15},{4,0},{5,1},{6,2},{7,3},{8,4},{9,5},{1... | collective-permute-start | bytes 1363976 | tf_op jit(solution)/shard_map/ppermute | solution.py:768
  135.0 2.7 %shard_map.111 = (bf16[2,592,384]{2,1,0:T(8,128)(2,1)S(1)}, bf16[2,592,384]{2,1,0:T(8,128)(2,1)S(1)}) custom-call(bf16[128,768]{1,0:T(8,128)(2,1)S(1)} %copy-done.4, bf16[128,768]{1,0:T(8,128)(2,1)S(1)} %collective-permute-done.31.tokens_other, bf16[128,8064]{1,0:T(8,128)(2,1)S(1)} %copy-done, bf16[128,8064]{1,0:T(8,128)(2,1)S(1)} %collective-permute-done.32.left_other, ...), custom_call_target="tpu_custom_call" | custom-call | flops 1000 | bytes 1000 | tf_op jit(solution)/shard_map/pallas_call | solution.py:702
  139.3 5.0 %collective-permute-done.36 = bf16[2,592,384]{2,1,0:T(8,128)(2,1)S(1)} collective-permute-done((bf16[2,592,384]{2,1,0:T(8,128)(2,1)S(1)}, bf16[2,592,384]{2,1,0:T(8,128)(2,1)S(1)}, u32[]{:S(2)}, u32[]{:S(2)}) %collective-permute-start.36) | collective-permute-done | bytes 909344 | tf_op jit(solution)/shard_map/ppermute | solution.py:761
  146.3 3.3 %collective-permute-start.43 = (bf16[592,384]{1,0:T(8,128)(2,1)S(1)}, bf16[592,384]{1,0:T(8,128)(2,1)S(1)}, u32[]{:S(2)}, u32[]{:S(2)}) collective-permute-start(bf16[592,384]{1,0:T(8,128)(2,1)S(1)} %fusion.2), channel_id=1, source_target_pairs={{0,12},{1,13},{2,14},{3,15},{4,0},{5,1},{6,2},{7,3},{8,4},{9,5},{1... | collective-permute-start | bytes 1363976 | tf_op jit(solution)/shard_map/ppermute | solution.py:768
  149.6 9.3 %collective-permute-done.34 = bf16[2,592,384]{2,1,0:T(8,128)(2,1)S(1)} collective-permute-done((bf16[2,592,384]{2,1,0:T(8,128)(2,1)S(1)}, bf16[2,592,384]{2,1,0:T(8,128)(2,1)S(1)}, u32[]{:S(2)}, u32[]{:S(2)}) %collective-permute-start.34) | collective-permute-done | bytes 909344 | tf_op jit(solution)/shard_map/ppermute | solution.py:761
  160.9 3.3 %collective-permute-start.44 = (bf16[592,384]{1,0:T(8,128)(2,1)S(1)}, bf16[592,384]{1,0:T(8,128)(2,1)S(1)}, u32[]{:S(2)}, u32[]{:S(2)}) collective-permute-start(bf16[592,384]{1,0:T(8,128)(2,1)S(1)} %fusion.4), channel_id=1, source_target_pairs={{0,12},{1,13},{2,14},{3,15},{4,0},{5,1},{6,2},{7,3},{8,4},{9,5},{1... | collective-permute-start | bytes 1363976 | tf_op jit(solution)/shard_map/ppermute | solution.py:768
  164.3 3.3 %collective-permute-done.35 = bf16[592,384]{1,0:T(8,128)(2,1)S(1)} collective-permute-done((bf16[592,384]{1,0:T(8,128)(2,1)S(1)}, bf16[592,384]{1,0:T(8,128)(2,1)S(1)}, u32[]{:S(2)}, u32[]{:S(2)}) %collective-permute-start.35) | collective-permute-done | bytes 454688 | tf_op jit(solution)/shard_map/ppermute | solution.py:763
  167.6 5.6 %collective-permute-done.44 = bf16[592,384]{1,0:T(8,128)(2,1)S(1)} collective-permute-done((bf16[592,384]{1,0:T(8,128)(2,1)S(1)}, bf16[592,384]{1,0:T(8,128)(2,1)S(1)}, u32[]{:S(2)}, u32[]{:S(2)}) %collective-permute-start.44) | collective-permute-done | bytes 454688 | tf_op jit(solution)/shard_map/ppermute | solution.py:768
  173.5 2.4 %collective-permute-done.45.other_ref = f32[592,384]{1,0:T(8,128)S(1)} collective-permute-done((f32[592,384]{1,0:T(8,128)S(1)}, f32[592,384]{1,0:T(8,128)S(1)}, u32[]{:S(2)}, u32[]{:S(2)}) %collective-permute-start.45) | collective-permute-done | bytes 909344 | tf_op jit(solution)/shard_map/ppermute | solution.py:770
  175.9 4.3 %shard_map.115 = (f32[442944]{0:T(1024)}, f32[442944]{0:T(1024)}, f32[442944]{0:T(1024)}, f32[442944]{0:T(1024)}) custom-call(f32[592,384]{1,0:T(8,128)S(1)} %fusion.5.mine_ref, f32[592,384]{1,0:T(8,128)S(1)} %collective-permute-done.45.other_ref, f32[442944]{0:T(1024)S(1)} %copy-done.3, f32[442944]{0:T(1024)S(1)} %copy-done.5, f32[442944]{0:T(1024)S(1)} %copy-done.6), custom_call_target="tpu_custom_call" | custom-call | tf_op jit(solution)/shard_map/pallas_call | solution.py:327
  (111 shorter events, 45.6 us)
Async XLA Ops:
  2.6 15.5 %collective-permute-start.3 = (bf16[592,384]{1,0:T(8,128)(2,1)S(1)}, bf16[592,384]{1,0:T(8,128)(2,1)S(1)}, u32[]{:S(2)}, u32[]{:S(2)}) collective-permute-start(bf16[592,384]{1,0:T(8,128)(2,1)S(1)} %shard_map.109.refs_0_), channel_id=1, source_target_pairs={{0,4},{1,5},{2,6},{3,7},{4,8},{5,9},{6,10},{7,11},{8,12},{9,13},{1... | collective-permute-start | bytes 1363976 | tf_op jit(solution)/shard_map/ppermute | solution.py:739
  5.7 14.0 %collective-permute-start = (bf16[592,384]{1,0:T(8,128)(2,1)S(1)}, bf16[592,384]{1,0:T(8,128)(2,1)S(1)}, u32[]{:S(2)}, u32[]{:S(2)}) collective-permute-start(bf16[592,384]{1,0:T(8,128)(2,1)S(1)} %shard_map.109.refs_0_), channel_id=1, source_target_pairs={{0,1},{16,18},{1,0},{17,19},{2,3},{18,16},{3,2},{19,17},{4,5},{20,... | collective-permute-start | bytes 1363976 | tf_op jit(solution)/shard_map/ppermute | solution.py:740
  7.2 14.0 %collective-permute-start.1 = (bf16[592,384]{1,0:T(8,128)(2,1)S(1)}, bf16[592,384]{1,0:T(8,128)(2,1)S(1)}, u32[]{:S(2)}, u32[]{:S(2)}) collective-permute-start(bf16[592,384]{1,0:T(8,128)(2,1)S(1)} %shard_map.109.refs_0_), channel_id=1, source_target_pairs={{0,2},{16,17},{1,3},{17,16},{2,0},{18,19},{3,1},{19,18},{4,6},{20,... | collective-permute-start | bytes 1363976 | tf_op jit(solution)/shard_map/ppermute | solution.py:741
  8.7 12.5 %collective-permute-start.15 = (bf16[592,384]{1,0:T(8,128)(2,1)S(1)}, bf16[592,384]{1,0:T(8,128)(2,1)S(1)}, u32[]{:S(2)}, u32[]{:S(2)}) collective-permute-start(bf16[592,384]{1,0:T(8,128)(2,1)S(1)} %shard_map.109.refs_0_), channel_id=1, source_target_pairs={{0,16},{16,0},{1,17},{17,1},{2,18},{18,2},{3,19},{19,3},{4,20},{20... | collective-permute-start | bytes 1363976 | tf_op jit(solution)/shard_map/ppermute | solution.py:745
  18.1 13.4 %collective-permute-start.7 = (bf16[592,384]{1,0:T(8,128)(2,1)S(1)}, bf16[592,384]{1,0:T(8,128)(2,1)S(1)}, u32[]{:S(2)}, u32[]{:S(2)}) collective-permute-start(bf16[592,384]{1,0:T(8,128)(2,1)S(1)} %collective-permute-done.3.refs_4_), channel_id=1, source_target_pairs={{0,4},{1,5},{2,6},{3,7},{4,8},{5,9},{6,10},{7,11},{8,12},{9,13},{1... | collective-permute-start | bytes 1363976 | tf_op jit(solution)/shard_map/ppermute | solution.py:739
  18.1 13.4 %collective-permute-start.4 = (bf16[592,384]{1,0:T(8,128)(2,1)S(1)}, bf16[592,384]{1,0:T(8,128)(2,1)S(1)}, u32[]{:S(2)}, u32[]{:S(2)}) collective-permute-start(bf16[592,384]{1,0:T(8,128)(2,1)S(1)} %collective-permute-done.3.refs_4_), channel_id=1, source_target_pairs={{0,1},{16,18},{1,0},{17,19},{2,3},{18,16},{3,2},{19,17},{4,5},{20,... | collective-permute-start | bytes 1363976 | tf_op jit(solution)/shard_map/ppermute | solution.py:740
  19.6 12.4 %collective-permute-start.5 = (bf16[592,384]{1,0:T(8,128)(2,1)S(1)}, bf16[592,384]{1,0:T(8,128)(2,1)S(1)}, u32[]{:S(2)}, u32[]{:S(2)}) collective-permute-start(bf16[592,384]{1,0:T(8,128)(2,1)S(1)} %collective-permute-done.3.refs_4_), channel_id=1, source_target_pairs={{0,2},{16,17},{1,3},{17,16},{2,0},{18,19},{3,1},{19,18},{4,6},{20,... | collective-permute-start | bytes 1363976 | tf_op jit(solution)/shard_map/ppermute | solution.py:741
  21.1 13.5 %collective-permute-start.2 = (bf16[592,384]{1,0:T(8,128)(2,1)S(1)}, bf16[592,384]{1,0:T(8,128)(2,1)S(1)}, u32[]{:S(2)}, u32[]{:S(2)}) collective-permute-start(bf16[592,384]{1,0:T(8,128)(2,1)S(1)} %collective-permute-done.refs_1_), channel_id=1, source_target_pairs={{0,2},{16,17},{1,3},{17,16},{2,0},{18,19},{3,1},{19,18},{4,6},{20,... | collective-permute-start | bytes 1363976 | tf_op jit(solution)/shard_map/ppermute | solution.py:742
  32.0 14.3 %collective-permute-start.11 = (bf16[592,384]{1,0:T(8,128)(2,1)S(1)}, bf16[592,384]{1,0:T(8,128)(2,1)S(1)}, u32[]{:S(2)}, u32[]{:S(2)}) collective-permute-start(bf16[592,384]{1,0:T(8,128)(2,1)S(1)} %collective-permute-done.7.refs_8_), channel_id=1, source_target_pairs={{0,4},{1,5},{2,6},{3,7},{4,8},{5,9},{6,10},{7,11},{8,12},{9,13},{1... | collective-permute-start | bytes 1363976 | tf_op jit(solution)/shard_map/ppermute | solution.py:739
  32.7 13.6 %collective-permute-start.8 = (bf16[592,384]{1,0:T(8,128)(2,1)S(1)}, bf16[592,384]{1,0:T(8,128)(2,1)S(1)}, u32[]{:S(2)}, u32[]{:S(2)}) collective-permute-start(bf16[592,384]{1,0:T(8,128)(2,1)S(1)} %collective-permute-done.7.refs_8_), channel_id=1, source_target_pairs={{0,1},{16,18},{1,0},{17,19},{2,3},{18,16},{3,2},{19,17},{4,5},{20,... | collective-permute-start | bytes 1363976 | tf_op jit(solution)/shard_map/ppermute | solution.py:740
  34.6 12.3 %collective-permute-start.9 = (bf16[592,384]{1,0:T(8,128)(2,1)S(1)}, bf16[592,384]{1,0:T(8,128)(2,1)S(1)}, u32[]{:S(2)}, u32[]{:S(2)}) collective-permute-start(bf16[592,384]{1,0:T(8,128)(2,1)S(1)} %collective-permute-done.7.refs_8_), channel_id=1, source_target_pairs={{0,2},{16,17},{1,3},{17,16},{2,0},{18,19},{3,1},{19,18},{4,6},{20,... | collective-permute-start | bytes 1363976 | tf_op jit(solution)/shard_map/ppermute | solution.py:741
  36.6 13.6 %collective-permute-start.6 = (bf16[592,384]{1,0:T(8,128)(2,1)S(1)}, bf16[592,384]{1,0:T(8,128)(2,1)S(1)}, u32[]{:S(2)}, u32[]{:S(2)}) collective-permute-start(bf16[592,384]{1,0:T(8,128)(2,1)S(1)} %collective-permute-done.4.refs_5_), channel_id=1, source_target_pairs={{0,2},{16,17},{1,3},{17,16},{2,0},{18,19},{3,1},{19,18},{4,6},{20,... | collective-permute-start | bytes 1363976 | tf_op jit(solution)/shard_map/ppermute | solution.py:742
  51.9 12.9 %collective-permute-start.10 = (bf16[592,384]{1,0:T(8,128)(2,1)S(1)}, bf16[592,384]{1,0:T(8,128)(2,1)S(1)}, u32[]{:S(2)}, u32[]{:S(2)}) collective-permute-start(bf16[592,384]{1,0:T(8,128)(2,1)S(1)} %collective-permute-done.8.refs_9_), channel_id=1, source_target_pairs={{0,2},{16,17},{1,3},{17,16},{2,0},{18,19},{3,1},{19,18},{4,6},{20,... | collective-permute-start | bytes 1363976 | tf_op jit(solution)/shard_map/ppermute | solution.py:742
  52.3 13.3 %collective-permute-start.27 = (bf16[592,384]{1,0:T(8,128)(2,1)S(1)}, bf16[592,384]{1,0:T(8,128)(2,1)S(1)}, u32[]{:S(2)}, u32[]{:S(2)}) collective-permute-start(bf16[592,384]{1,0:T(8,128)(2,1)S(1)} %collective-permute-done.11.refs_12_), channel_id=1, source_target_pairs={{0,16},{16,0},{1,17},{17,1},{2,18},{18,2},{3,19},{19,3},{4,20},{20... | collective-permute-start | bytes 1363976 | tf_op jit(solution)/shard_map/ppermute | solution.py:745
  52.8 12.9 %collective-permute-start.24 = (bf16[592,384]{1,0:T(8,128)(2,1)S(1)}, bf16[592,384]{1,0:T(8,128)(2,1)S(1)}, u32[]{:S(2)}, u32[]{:S(2)}) collective-permute-start(bf16[592,384]{1,0:T(8,128)(2,1)S(1)} %collective-permute-done.8.refs_9_), channel_id=1, source_target_pairs={{0,16},{16,0},{1,17},{17,1},{2,18},{18,2},{3,19},{19,3},{4,20},{20... | collective-permute-start | bytes 1363976 | tf_op jit(solution)/shard_map/ppermute | solution.py:745
  101.7 13.4 %collective-permute-start.40 = (bf16[2,592,384]{2,1,0:T(8,128)(2,1)S(1)}, bf16[2,592,384]{2,1,0:T(8,128)(2,1)S(1)}, u32[]{:S(2)}, u32[]{:S(2)}) collective-permute-start(bf16[2,592,384]{2,1,0:T(8,128)(2,1)S(1)} %get-tuple-element.35), channel_id=1, source_target_pairs={{0,2},{16,17},{1,3},{17,16},{2,0},{18,19},{3,1},{19,18},{4,6},{20,... | collective-permute-start | bytes 2727944 | tf_op jit(solution)/shard_map/ppermute | solution.py:761
  105.7 24.0 %collective-permute-start.38 = (bf16[2,592,384]{2,1,0:T(8,128)(2,1)S(1)}, bf16[2,592,384]{2,1,0:T(8,128)(2,1)S(1)}, u32[]{:S(2)}, u32[]{:S(2)}) collective-permute-start(bf16[2,592,384]{2,1,0:T(8,128)(2,1)S(1)} %get-tuple-element.33), channel_id=1, source_target_pairs={{0,2},{16,17},{1,3},{17,16},{2,0},{18,19},{3,1},{19,18},{4,6},{20,... | collective-permute-start | bytes 2727944 | tf_op jit(solution)/shard_map/ppermute | solution.py:761
  115.3 16.2 %collective-permute-start.41 = (bf16[592,384]{1,0:T(8,128)(2,1)S(1)}, bf16[592,384]{1,0:T(8,128)(2,1)S(1)}, u32[]{:S(2)}, u32[]{:S(2)}) collective-permute-start(bf16[592,384]{1,0:T(8,128)(2,1)S(1)} %fusion.9), channel_id=1, source_target_pairs={{0,1},{16,18},{1,0},{17,19},{2,3},{18,16},{3,2},{19,17},{4,5},{20,... | collective-permute-start | bytes 1363976 | tf_op jit(solution)/shard_map/ppermute | solution.py:763
  119.3 25.0 %collective-permute-start.36 = (bf16[2,592,384]{2,1,0:T(8,128)(2,1)S(1)}, bf16[2,592,384]{2,1,0:T(8,128)(2,1)S(1)}, u32[]{:S(2)}, u32[]{:S(2)}) collective-permute-start(bf16[2,592,384]{2,1,0:T(8,128)(2,1)S(1)} %get-tuple-element.31), channel_id=1, source_target_pairs={{0,2},{16,17},{1,3},{17,16},{2,0},{18,19},{3,1},{19,18},{4,6},{20,... | collective-permute-start | bytes 2727944 | tf_op jit(solution)/shard_map/ppermute | solution.py:761
  129.9 16.2 %collective-permute-start.39 = (bf16[592,384]{1,0:T(8,128)(2,1)S(1)}, bf16[592,384]{1,0:T(8,128)(2,1)S(1)}, u32[]{:S(2)}, u32[]{:S(2)}) collective-permute-start(bf16[592,384]{1,0:T(8,128)(2,1)S(1)} %fusion.8), channel_id=1, source_target_pairs={{0,1},{16,18},{1,0},{17,19},{2,3},{18,16},{3,2},{19,17},{4,5},{20,... | collective-permute-start | bytes 1363976 | tf_op jit(solution)/shard_map/ppermute | solution.py:763
  131.6 14.4 %collective-permute-start.42 = (bf16[592,384]{1,0:T(8,128)(2,1)S(1)}, bf16[592,384]{1,0:T(8,128)(2,1)S(1)}, u32[]{:S(2)}, u32[]{:S(2)}) collective-permute-start(bf16[592,384]{1,0:T(8,128)(2,1)S(1)} %fusion), channel_id=1, source_target_pairs={{0,12},{1,13},{2,14},{3,15},{4,0},{5,1},{6,2},{7,3},{8,4},{9,5},{1... | collective-permute-start | bytes 1363976 | tf_op jit(solution)/shard_map/ppermute | solution.py:768
  137.7 21.3 %collective-permute-start.34 = (bf16[2,592,384]{2,1,0:T(8,128)(2,1)S(1)}, bf16[2,592,384]{2,1,0:T(8,128)(2,1)S(1)}, u32[]{:S(2)}, u32[]{:S(2)}) collective-permute-start(bf16[2,592,384]{2,1,0:T(8,128)(2,1)S(1)} %get-tuple-element.29), channel_id=1, source_target_pairs={{0,2},{16,17},{1,3},{17,16},{2,0},{18,19},{3,1},{19,18},{4,6},{20,... | collective-permute-start | bytes 2727944 | tf_op jit(solution)/shard_map/ppermute | solution.py:761
  144.5 16.2 %collective-permute-start.37 = (bf16[592,384]{1,0:T(8,128)(2,1)S(1)}, bf16[592,384]{1,0:T(8,128)(2,1)S(1)}, u32[]{:S(2)}, u32[]{:S(2)}) collective-permute-start(bf16[592,384]{1,0:T(8,128)(2,1)S(1)} %fusion.7), channel_id=1, source_target_pairs={{0,1},{16,18},{1,0},{17,19},{2,3},{18,16},{3,2},{19,17},{4,5},{20,... | collective-permute-start | bytes 1363976 | tf_op jit(solution)/shard_map/ppermute | solution.py:763
  146.3 14.4 %collective-permute-start.43 = (bf16[592,384]{1,0:T(8,128)(2,1)S(1)}, bf16[592,384]{1,0:T(8,128)(2,1)S(1)}, u32[]{:S(2)}, u32[]{:S(2)}) collective-permute-start(bf16[592,384]{1,0:T(8,128)(2,1)S(1)} %fusion.2), channel_id=1, source_target_pairs={{0,12},{1,13},{2,14},{3,15},{4,0},{5,1},{6,2},{7,3},{8,4},{9,5},{1... | collective-permute-start | bytes 1363976 | tf_op jit(solution)/shard_map/ppermute | solution.py:768
  (36 other events, 354.8 us)

commit v6 on v5

--- a/solution.py
+++ b/solution.py
@@ -554,8 +554,8 @@
         out_shape=[
             thin,
             thin,
-            jax.ShapeDtypeStruct((rows, LEFT + RIGHT), bf16),
-            jax.ShapeDtypeStruct((rows, RIGHT), bf16),
+            pltpu.VMEM((rows, LEFT + RIGHT), bf16),
+            pltpu.VMEM((rows, RIGHT), bf16),
             jax.ShapeDtypeStruct((16, ROW), f32),
         ],
         in_specs=[pl.BlockSpec(memory_space=pltpu.SMEM)] + [vmem_spec] * 2 + [any_spec] * 32,
@@ -696,13 +696,12 @@
 
 def quad_grads(slot, operands):
     any_spec = pl.BlockSpec(memory_space=pl.ANY)
-    hbm_spec = pl.BlockSpec(memory_space=pltpu.HBM)
     vmem_spec = pl.BlockSpec(memory_space=pltpu.VMEM)
     frames = jax.ShapeDtypeStruct((2, FRAME, HALF), bf16)
     return pl.pallas_call(
         functools.partial(grad_kernel, slot),
         out_shape=[frames, frames],
-        in_specs=[any_spec] * 2 + [hbm_spec, any_spec, hbm_spec] + [vmem_spec] * 2,
+        in_specs=[any_spec] * 5 + [vmem_spec] * 2,
         out_specs=[any_spec] * 2,
         scratch_shapes=[
             pltpu.VMEM((256, 2304), bf16),
@@ -758,14 +757,19 @@
     passed = None
     for t in (3, 2, 1, 0):
         low, high = quad_grads(t, operands)
+        if t == 0:
+            high = lax.optimization_barrier((high, away))[0]
         from_far = lax.ppermute(high, both, far)
+        if passed is not None:
+            from_far = lax.optimization_barrier((from_far, leaving))[0]
         away = (low[1].astype(f32) + from_far[1].astype(f32)).astype(bf16)
         from_near = lax.ppermute(away, both, near)
         total = low[0].astype(f32) + from_far[0].astype(f32) + from_near.astype(f32)
         if passed is not None:
             total = total + passed.astype(f32)
         if t > 0:
-            passed = lax.ppermute(total.astype(bf16), "shard", down)
+            leaving = total.astype(bf16)
+            passed = lax.ppermute(leaving, "shard", down)
     weight_grad, new_params, new_first, new_second = finish(
         total, lax.ppermute(total, "rep", swap), params, first_moment, second_moment
     )

time: 180 us -> 176 us (0.978)
  local copies, waits for them, and re-layouts: 5.32 us -> 2.71 us
    ppermute x4, waiting for transfers between devices: 32 us -> 10 us  [on_device_planes(): from_far = lax.ppermute(high, both, far)]
    ppermute x4, waiting for transfers between devices: 3.33 us -> 22.6 us  [on_device_planes(): from_near = lax.ppermute(away, both, near)]
    unnamed x28 -> x36, local copies, waits for them, and re-layouts: 5.32 us -> 2.71 us
    ppermute x3, waiting for transfers between devices: 5.58 us -> 7.76 us  [on_device_planes(): passed = lax.ppermute(leaving, 'shard', down)]
  transfers between devices with their start and end apart: 46 -> 46, of which waited for: 20 -> 23; matrix products, arithmetic and copies ran while one was open for 1% -> 1% of each run, Pallas kernels for 4% -> 4%
where the time goes in v6:
time: 176 us
  waiting for transfers between devices  91.7 us (52%)
  starting transfers between devices  46 us (26%)
  Pallas kernels  32.7 us (19%)
  local copies, waits for them, and re-layouts  2.71 us (2%)
    ppermute x3, waiting for transfers between devices, on_device_planes(): zero = own if t == 0 else lax.ppermute(zero, 'shard', up)  28.4 us
    ppermute x4, waiting for transfers between devices, on_device_planes(): from_near = lax.ppermute(away, both, near)  22.6 us
    pallas_call x1, Pallas kernels, run_layer(): pl.pallas_call(layer_kernel, out_shape=[thin, thin, pltpu.VMEM((rows, LEF...  17.8 us
    ppermute x3, starting transfers between devices, on_device_planes(): passed = lax.ppermute(leaving, 'shard', down)  11.4 us
    pallas_call x4, Pallas kernels, quad_grads(): pl.pallas_call(functools.partial(grad_kernel, slot), out_shape=[frames, f...  10.2 us
    ppermute x4, waiting for transfers between devices, on_device_planes(): from_far = lax.ppermute(high, both, far)  10 us
    ppermute x4, waiting for transfers between devices, on_device_planes(): three = lax.ppermute(one, both, far)  8.92 us
    ppermute x3, waiting for transfers between devices, on_device_planes(): passed = lax.ppermute(leaving, 'shard', down)  7.76 us
  transfers between devices with their start and end apart: 46, of which 23 were waited for; matrix products, arithmetic and copies ran while one was open for 1% of the time, Pallas kernels for 4%

profile of v6, /device:TPU:0, one launch (start us, length us, event | category | flops | bytes accessed | tf_op | source)
XLA Modules:
  0.0 176.1 jit_solution(14245719187611950140)
XLA Ops:
  2.6 3.1 %collective-permute-start.3 = (bf16[592,384]{1,0:T(8,128)(2,1)S(1)}, bf16[592,384]{1,0:T(8,128)(2,1)S(1)}, u32[]{:S(2)}, u32[]{:S(2)}) collective-permute-start(bf16[592,384]{1,0:T(8,128)(2,1)S(1)} %shard_map.109.refs_0_), channel_id=1, source_target_pairs={{0,4},{1,5},{2,6},{3,7},{4,8},{5,9},{6,10},{7,11},{8,12},{9,13},{1... | collective-permute-start | bytes 1363976 | tf_op jit(solution)/shard_map/ppermute | solution.py:738
  8.7 9.4 %collective-permute-done.3.refs_4_ = bf16[592,384]{1,0:T(8,128)(2,1)S(1)} collective-permute-done((bf16[592,384]{1,0:T(8,128)(2,1)S(1)}, bf16[592,384]{1,0:T(8,128)(2,1)S(1)}, u32[]{:S(2)}, u32[]{:S(2)}) %collective-permute-start.3) | collective-permute-done | bytes 454688 | tf_op jit(solution)/shard_map/ppermute | solution.py:738
  21.7 9.8 %collective-permute-done.7.refs_8_ = bf16[592,384]{1,0:T(8,128)(2,1)S(1)} collective-permute-done((bf16[592,384]{1,0:T(8,128)(2,1)S(1)}, bf16[592,384]{1,0:T(8,128)(2,1)S(1)}, u32[]{:S(2)}, u32[]{:S(2)}) %collective-permute-start.7) | collective-permute-done | bytes 454688 | tf_op jit(solution)/shard_map/ppermute | solution.py:738
  37.2 9.1 %collective-permute-done.11.refs_12_ = bf16[592,384]{1,0:T(8,128)(2,1)S(1)} collective-permute-done((bf16[592,384]{1,0:T(8,128)(2,1)S(1)}, bf16[592,384]{1,0:T(8,128)(2,1)S(1)}, u32[]{:S(2)}, u32[]{:S(2)}) %collective-permute-start.11) | collective-permute-done | bytes 454688 | tf_op jit(solution)/shard_map/ppermute | solution.py:738
  52.9 4.6 %collective-permute-done.12.refs_13_ = bf16[592,384]{1,0:T(8,128)(2,1)S(1)} collective-permute-done((bf16[592,384]{1,0:T(8,128)(2,1)S(1)}, bf16[592,384]{1,0:T(8,128)(2,1)S(1)}, u32[]{:S(2)}, u32[]{:S(2)}) %collective-permute-start.12) | collective-permute-done | bytes 454688 | tf_op jit(solution)/shard_map/ppermute | solution.py:739
  57.6 2.4 %collective-permute-done.13.refs_14_ = bf16[592,384]{1,0:T(8,128)(2,1)S(1)} collective-permute-done((bf16[592,384]{1,0:T(8,128)(2,1)S(1)}, bf16[592,384]{1,0:T(8,128)(2,1)S(1)}, u32[]{:S(2)}, u32[]{:S(2)}) %collective-permute-start.13) | collective-permute-done | bytes 454688 | tf_op jit(solution)/shard_map/ppermute | solution.py:740
  61.5 3.3 %collective-permute-done.10.refs_11_ = bf16[592,384]{1,0:T(8,128)(2,1)S(1)} collective-permute-done((bf16[592,384]{1,0:T(8,128)(2,1)S(1)}, bf16[592,384]{1,0:T(8,128)(2,1)S(1)}, u32[]{:S(2)}, u32[]{:S(2)}) %collective-permute-start.10) | collective-permute-done | bytes 454688 | tf_op jit(solution)/shard_map/ppermute | solution.py:741
  66.3 3.4 %collective-permute-done.14.refs_15_ = bf16[592,384]{1,0:T(8,128)(2,1)S(1)} collective-permute-done((bf16[592,384]{1,0:T(8,128)(2,1)S(1)}, bf16[592,384]{1,0:T(8,128)(2,1)S(1)}, u32[]{:S(2)}, u32[]{:S(2)}) %collective-permute-start.14) | collective-permute-done | bytes 454688 | tf_op jit(solution)/shard_map/ppermute | solution.py:741
  72.9 17.8 %shard_map.110 = (bf16[128,768]{1,0:T(8,128)(2,1)}, bf16[128,768]{1,0:T(8,128)(2,1)}, bf16[128,8064]{1,0:T(8,128)(2,1)S(1)}, bf16[128,3456]{1,0:T(8,128)(2,1)S(1)}, f32[16,768]{1,0:T(8,128)S(1)}) custom-call(s32[1]{0:T(128)S(6)} %copy.12.length_ref, bf16[128,768]{1,0:T(8,128)(2,1)S(1)} %copy-done.2, bf16[128,768]{1,0:T(8,128)(2,1)S(1)} %copy-done.5, ...), custom_call_target="tpu_custom_call" | custom-call | tf_op jit(solution)/shard_map/pallas_call | solution.py:552
  91.4 3.8 %collective-permute-done.31.tokens_other = bf16[128,768]{1,0:T(8,128)(2,1)S(1)} collective-permute-done((bf16[128,768]{1,0:T(8,128)(2,1)S(1)}, bf16[128,768]{1,0:T(8,128)(2,1)S(1)}, u32[]{:S(2)}, u32[]{:S(2)}) %collective-permute-start.31) | collective-permute-done | bytes 196640 | tf_op jit(solution)/shard_map/ppermute | solution.py:750
  95.3 2.6 %shard_map.114 = (bf16[2,592,384]{2,1,0:T(8,128)(2,1)S(1)}, bf16[2,592,384]{2,1,0:T(8,128)(2,1)S(1)}) custom-call(bf16[128,768]{1,0:T(8,128)(2,1)S(1)} %copy-done.2, bf16[128,768]{1,0:T(8,128)(2,1)S(1)} %collective-permute-done.31.tokens_other, bf16[128,8064]{1,0:T(8,128)(2,1)S(1)} %get-tuple-element.29.left_ref, ...), custom_call_target="tpu_custom_call" | custom-call | flops 1000 | bytes 1000 | tf_op jit(solution)/shard_map/pallas_call | solution.py:701
  99.6 2.3 %shard_map.113 = (bf16[2,592,384]{2,1,0:T(8,128)(2,1)S(1)}, bf16[2,592,384]{2,1,0:T(8,128)(2,1)S(1)}) custom-call(bf16[128,768]{1,0:T(8,128)(2,1)S(1)} %copy-done.2, bf16[128,768]{1,0:T(8,128)(2,1)S(1)} %collective-permute-done.31.tokens_other, bf16[128,8064]{1,0:T(8,128)(2,1)S(1)} %get-tuple-element.29.left_ref, ...), custom_call_target="tpu_custom_call" | custom-call | flops 1000 | bytes 1000 | tf_op jit(solution)/shard_map/pallas_call | solution.py:701
  102.4 8.9 %collective-permute-done.36 = bf16[2,592,384]{2,1,0:T(8,128)(2,1)S(1)} collective-permute-done((bf16[2,592,384]{2,1,0:T(8,128)(2,1)S(1)}, bf16[2,592,384]{2,1,0:T(8,128)(2,1)S(1)}, u32[]{:S(2)}, u32[]{:S(2)}) %collective-permute-start.36) | collective-permute-done | bytes 909344 | tf_op jit(solution)/shard_map/ppermute | solution.py:762
  113.0 2.5 %shard_map.112 = (bf16[2,592,384]{2,1,0:T(8,128)(2,1)S(1)}, bf16[2,592,384]{2,1,0:T(8,128)(2,1)S(1)}) custom-call(bf16[128,768]{1,0:T(8,128)(2,1)S(1)} %copy-done.2, bf16[128,768]{1,0:T(8,128)(2,1)S(1)} %collective-permute-done.31.tokens_other, bf16[128,8064]{1,0:T(8,128)(2,1)S(1)} %get-tuple-element.29.left_ref, ...), custom_call_target="tpu_custom_call" | custom-call | flops 1000 | bytes 1000 | tf_op jit(solution)/shard_map/pallas_call | solution.py:701
  117.1 7.7 %collective-permute-done.37 = bf16[592,384]{1,0:T(8,128)(2,1)S(1)} collective-permute-done((bf16[592,384]{1,0:T(8,128)(2,1)S(1)}, bf16[592,384]{1,0:T(8,128)(2,1)S(1)}, u32[]{:S(2)}, u32[]{:S(2)}) %collective-permute-start.37) | collective-permute-done | bytes 454688 | tf_op jit(solution)/shard_map/ppermute | solution.py:766
  127.6 3.6 %collective-permute-start.39 = (bf16[592,384]{1,0:T(8,128)(2,1)S(1)}, bf16[592,384]{1,0:T(8,128)(2,1)S(1)}, u32[]{:S(2)}, u32[]{:S(2)}) collective-permute-start(bf16[592,384]{1,0:T(8,128)(2,1)S(1)} %fusion.5), channel_id=1, source_target_pairs={{0,12},{1,13},{2,14},{3,15},{4,0},{5,1},{6,2},{7,3},{8,4},{9,5},{1... | collective-permute-start | bytes 1363976 | tf_op jit(solution)/shard_map/ppermute | solution.py:772
  131.2 2.7 %shard_map.111 = (bf16[2,592,384]{2,1,0:T(8,128)(2,1)S(1)}, bf16[2,592,384]{2,1,0:T(8,128)(2,1)S(1)}) custom-call(bf16[128,768]{1,0:T(8,128)(2,1)S(1)} %copy-done.2, bf16[128,768]{1,0:T(8,128)(2,1)S(1)} %collective-permute-done.31.tokens_other, bf16[128,8064]{1,0:T(8,128)(2,1)S(1)} %get-tuple-element.29.left_ref, ...), custom_call_target="tpu_custom_call" | custom-call | flops 1000 | bytes 1000 | tf_op jit(solution)/shard_map/pallas_call | solution.py:701
  133.9 5.6 %collective-permute-done.38 = bf16[592,384]{1,0:T(8,128)(2,1)S(1)} collective-permute-done((bf16[592,384]{1,0:T(8,128)(2,1)S(1)}, bf16[592,384]{1,0:T(8,128)(2,1)S(1)}, u32[]{:S(2)}, u32[]{:S(2)}) %collective-permute-start.38) | collective-permute-done | bytes 454688 | tf_op jit(solution)/shard_map/ppermute | solution.py:766
  143.8 3.5 %collective-permute-start.42 = (bf16[592,384]{1,0:T(8,128)(2,1)S(1)}, bf16[592,384]{1,0:T(8,128)(2,1)S(1)}, u32[]{:S(2)}, u32[]{:S(2)}) collective-permute-start(bf16[592,384]{1,0:T(8,128)(2,1)S(1)} %fusion.4), channel_id=1, source_target_pairs={{0,12},{1,13},{2,14},{3,15},{4,0},{5,1},{6,2},{7,3},{8,4},{9,5},{1... | collective-permute-start | bytes 1363976 | tf_op jit(solution)/shard_map/ppermute | solution.py:772
  147.3 8.4 %collective-permute-done.41 = bf16[592,384]{1,0:T(8,128)(2,1)S(1)} collective-permute-done((bf16[592,384]{1,0:T(8,128)(2,1)S(1)}, bf16[592,384]{1,0:T(8,128)(2,1)S(1)}, u32[]{:S(2)}, u32[]{:S(2)}) %collective-permute-start.41) | collective-permute-done | bytes 454688 | tf_op jit(solution)/shard_map/ppermute | solution.py:766
  156.1 4.3 %collective-permute-start.44 = (bf16[592,384]{1,0:T(8,128)(2,1)S(1)}, bf16[592,384]{1,0:T(8,128)(2,1)S(1)}, u32[]{:S(2)}, u32[]{:S(2)}) collective-permute-start(bf16[592,384]{1,0:T(8,128)(2,1)S(1)} %fusion.2), channel_id=1, source_target_pairs={{0,12},{1,13},{2,14},{3,15},{4,0},{5,1},{6,2},{7,3},{8,4},{9,5},{1... | collective-permute-start | bytes 1363976 | tf_op jit(solution)/shard_map/ppermute | solution.py:772
  161.2 6.9 %collective-permute-done.44 = bf16[592,384]{1,0:T(8,128)(2,1)S(1)} collective-permute-done((bf16[592,384]{1,0:T(8,128)(2,1)S(1)}, bf16[592,384]{1,0:T(8,128)(2,1)S(1)}, u32[]{:S(2)}, u32[]{:S(2)}) %collective-permute-start.44) | collective-permute-done | bytes 454688 | tf_op jit(solution)/shard_map/ppermute | solution.py:772
  169.4 2.4 %collective-permute-done.45.other_ref = f32[592,384]{1,0:T(8,128)S(1)} collective-permute-done((f32[592,384]{1,0:T(8,128)S(1)}, f32[592,384]{1,0:T(8,128)S(1)}, u32[]{:S(2)}, u32[]{:S(2)}) %collective-permute-start.45) | collective-permute-done | bytes 909344 | tf_op jit(solution)/shard_map/ppermute | solution.py:774
  171.8 4.3 %shard_map.115 = (f32[442944]{0:T(1024)}, f32[442944]{0:T(1024)}, f32[442944]{0:T(1024)}, f32[442944]{0:T(1024)}) custom-call(f32[592,384]{1,0:T(8,128)S(1)} %fusion.mine_ref, f32[592,384]{1,0:T(8,128)S(1)} %collective-permute-done.45.other_ref, f32[442944]{0:T(1024)S(1)} %copy-done.1, f32[442944]{0:T(1024)S(1)} %copy-done.3, f32[442944]{0:T(1024)S(1)} %copy-done.4), custom_call_target="tpu_custom_call" | custom-call | tf_op jit(solution)/shard_map/pallas_call | solution.py:327
  (119 shorter events, 42.0 us)
Async XLA Ops:
  2.6 15.5 %collective-permute-start.3 = (bf16[592,384]{1,0:T(8,128)(2,1)S(1)}, bf16[592,384]{1,0:T(8,128)(2,1)S(1)}, u32[]{:S(2)}, u32[]{:S(2)}) collective-permute-start(bf16[592,384]{1,0:T(8,128)(2,1)S(1)} %shard_map.109.refs_0_), channel_id=1, source_target_pairs={{0,4},{1,5},{2,6},{3,7},{4,8},{5,9},{6,10},{7,11},{8,12},{9,13},{1... | collective-permute-start | bytes 1363976 | tf_op jit(solution)/shard_map/ppermute | solution.py:738
  5.7 14.0 %collective-permute-start = (bf16[592,384]{1,0:T(8,128)(2,1)S(1)}, bf16[592,384]{1,0:T(8,128)(2,1)S(1)}, u32[]{:S(2)}, u32[]{:S(2)}) collective-permute-start(bf16[592,384]{1,0:T(8,128)(2,1)S(1)} %shard_map.109.refs_0_), channel_id=1, source_target_pairs={{0,1},{16,18},{1,0},{17,19},{2,3},{18,16},{3,2},{19,17},{4,5},{20,... | collective-permute-start | bytes 1363976 | tf_op jit(solution)/shard_map/ppermute | solution.py:739
  7.2 14.0 %collective-permute-start.1 = (bf16[592,384]{1,0:T(8,128)(2,1)S(1)}, bf16[592,384]{1,0:T(8,128)(2,1)S(1)}, u32[]{:S(2)}, u32[]{:S(2)}) collective-permute-start(bf16[592,384]{1,0:T(8,128)(2,1)S(1)} %shard_map.109.refs_0_), channel_id=1, source_target_pairs={{0,2},{16,17},{1,3},{17,16},{2,0},{18,19},{3,1},{19,18},{4,6},{20,... | collective-permute-start | bytes 1363976 | tf_op jit(solution)/shard_map/ppermute | solution.py:740
  8.7 12.5 %collective-permute-start.15 = (bf16[592,384]{1,0:T(8,128)(2,1)S(1)}, bf16[592,384]{1,0:T(8,128)(2,1)S(1)}, u32[]{:S(2)}, u32[]{:S(2)}) collective-permute-start(bf16[592,384]{1,0:T(8,128)(2,1)S(1)} %shard_map.109.refs_0_), channel_id=1, source_target_pairs={{0,16},{16,0},{1,17},{17,1},{2,18},{18,2},{3,19},{19,3},{4,20},{20... | collective-permute-start | bytes 1363976 | tf_op jit(solution)/shard_map/ppermute | solution.py:744
  18.1 13.4 %collective-permute-start.7 = (bf16[592,384]{1,0:T(8,128)(2,1)S(1)}, bf16[592,384]{1,0:T(8,128)(2,1)S(1)}, u32[]{:S(2)}, u32[]{:S(2)}) collective-permute-start(bf16[592,384]{1,0:T(8,128)(2,1)S(1)} %collective-permute-done.3.refs_4_), channel_id=1, source_target_pairs={{0,4},{1,5},{2,6},{3,7},{4,8},{5,9},{6,10},{7,11},{8,12},{9,13},{1... | collective-permute-start | bytes 1363976 | tf_op jit(solution)/shard_map/ppermute | solution.py:738
  18.1 13.4 %collective-permute-start.4 = (bf16[592,384]{1,0:T(8,128)(2,1)S(1)}, bf16[592,384]{1,0:T(8,128)(2,1)S(1)}, u32[]{:S(2)}, u32[]{:S(2)}) collective-permute-start(bf16[592,384]{1,0:T(8,128)(2,1)S(1)} %collective-permute-done.3.refs_4_), channel_id=1, source_target_pairs={{0,1},{16,18},{1,0},{17,19},{2,3},{18,16},{3,2},{19,17},{4,5},{20,... | collective-permute-start | bytes 1363976 | tf_op jit(solution)/shard_map/ppermute | solution.py:739
  19.6 12.4 %collective-permute-start.5 = (bf16[592,384]{1,0:T(8,128)(2,1)S(1)}, bf16[592,384]{1,0:T(8,128)(2,1)S(1)}, u32[]{:S(2)}, u32[]{:S(2)}) collective-permute-start(bf16[592,384]{1,0:T(8,128)(2,1)S(1)} %collective-permute-done.3.refs_4_), channel_id=1, source_target_pairs={{0,2},{16,17},{1,3},{17,16},{2,0},{18,19},{3,1},{19,18},{4,6},{20,... | collective-permute-start | bytes 1363976 | tf_op jit(solution)/shard_map/ppermute | solution.py:740
  21.1 13.5 %collective-permute-start.2 = (bf16[592,384]{1,0:T(8,128)(2,1)S(1)}, bf16[592,384]{1,0:T(8,128)(2,1)S(1)}, u32[]{:S(2)}, u32[]{:S(2)}) collective-permute-start(bf16[592,384]{1,0:T(8,128)(2,1)S(1)} %collective-permute-done.refs_1_), channel_id=1, source_target_pairs={{0,2},{16,17},{1,3},{17,16},{2,0},{18,19},{3,1},{19,18},{4,6},{20,... | collective-permute-start | bytes 1363976 | tf_op jit(solution)/shard_map/ppermute | solution.py:741
  32.0 14.3 %collective-permute-start.11 = (bf16[592,384]{1,0:T(8,128)(2,1)S(1)}, bf16[592,384]{1,0:T(8,128)(2,1)S(1)}, u32[]{:S(2)}, u32[]{:S(2)}) collective-permute-start(bf16[592,384]{1,0:T(8,128)(2,1)S(1)} %collective-permute-done.7.refs_8_), channel_id=1, source_target_pairs={{0,4},{1,5},{2,6},{3,7},{4,8},{5,9},{6,10},{7,11},{8,12},{9,13},{1... | collective-permute-start | bytes 1363976 | tf_op jit(solution)/shard_map/ppermute | solution.py:738
  32.7 13.6 %collective-permute-start.8 = (bf16[592,384]{1,0:T(8,128)(2,1)S(1)}, bf16[592,384]{1,0:T(8,128)(2,1)S(1)}, u32[]{:S(2)}, u32[]{:S(2)}) collective-permute-start(bf16[592,384]{1,0:T(8,128)(2,1)S(1)} %collective-permute-done.7.refs_8_), channel_id=1, source_target_pairs={{0,1},{16,18},{1,0},{17,19},{2,3},{18,16},{3,2},{19,17},{4,5},{20,... | collective-permute-start | bytes 1363976 | tf_op jit(solution)/shard_map/ppermute | solution.py:739
  34.6 12.3 %collective-permute-start.9 = (bf16[592,384]{1,0:T(8,128)(2,1)S(1)}, bf16[592,384]{1,0:T(8,128)(2,1)S(1)}, u32[]{:S(2)}, u32[]{:S(2)}) collective-permute-start(bf16[592,384]{1,0:T(8,128)(2,1)S(1)} %collective-permute-done.7.refs_8_), channel_id=1, source_target_pairs={{0,2},{16,17},{1,3},{17,16},{2,0},{18,19},{3,1},{19,18},{4,6},{20,... | collective-permute-start | bytes 1363976 | tf_op jit(solution)/shard_map/ppermute | solution.py:740
  36.6 13.6 %collective-permute-start.6 = (bf16[592,384]{1,0:T(8,128)(2,1)S(1)}, bf16[592,384]{1,0:T(8,128)(2,1)S(1)}, u32[]{:S(2)}, u32[]{:S(2)}) collective-permute-start(bf16[592,384]{1,0:T(8,128)(2,1)S(1)} %collective-permute-done.4.refs_5_), channel_id=1, source_target_pairs={{0,2},{16,17},{1,3},{17,16},{2,0},{18,19},{3,1},{19,18},{4,6},{20,... | collective-permute-start | bytes 1363976 | tf_op jit(solution)/shard_map/ppermute | solution.py:741
  51.9 12.9 %collective-permute-start.10 = (bf16[592,384]{1,0:T(8,128)(2,1)S(1)}, bf16[592,384]{1,0:T(8,128)(2,1)S(1)}, u32[]{:S(2)}, u32[]{:S(2)}) collective-permute-start(bf16[592,384]{1,0:T(8,128)(2,1)S(1)} %collective-permute-done.8.refs_9_), channel_id=1, source_target_pairs={{0,2},{16,17},{1,3},{17,16},{2,0},{18,19},{3,1},{19,18},{4,6},{20,... | collective-permute-start | bytes 1363976 | tf_op jit(solution)/shard_map/ppermute | solution.py:741
  52.3 13.3 %collective-permute-start.27 = (bf16[592,384]{1,0:T(8,128)(2,1)S(1)}, bf16[592,384]{1,0:T(8,128)(2,1)S(1)}, u32[]{:S(2)}, u32[]{:S(2)}) collective-permute-start(bf16[592,384]{1,0:T(8,128)(2,1)S(1)} %collective-permute-done.11.refs_12_), channel_id=1, source_target_pairs={{0,16},{16,0},{1,17},{17,1},{2,18},{18,2},{3,19},{19,3},{4,20},{20... | collective-permute-start | bytes 1363976 | tf_op jit(solution)/shard_map/ppermute | solution.py:744
  52.8 12.9 %collective-permute-start.24 = (bf16[592,384]{1,0:T(8,128)(2,1)S(1)}, bf16[592,384]{1,0:T(8,128)(2,1)S(1)}, u32[]{:S(2)}, u32[]{:S(2)}) collective-permute-start(bf16[592,384]{1,0:T(8,128)(2,1)S(1)} %collective-permute-done.8.refs_9_), channel_id=1, source_target_pairs={{0,16},{16,0},{1,17},{17,1},{2,18},{18,2},{3,19},{19,3},{4,20},{20... | collective-permute-start | bytes 1363976 | tf_op jit(solution)/shard_map/ppermute | solution.py:744
  97.9 13.4 %collective-permute-start.36 = (bf16[2,592,384]{2,1,0:T(8,128)(2,1)S(1)}, bf16[2,592,384]{2,1,0:T(8,128)(2,1)S(1)}, u32[]{:S(2)}, u32[]{:S(2)}) collective-permute-start(bf16[2,592,384]{2,1,0:T(8,128)(2,1)S(1)} %get-tuple-element.39), channel_id=1, source_target_pairs={{0,2},{16,17},{1,3},{17,16},{2,0},{18,19},{3,1},{19,18},{4,6},{20,... | collective-permute-start | bytes 2727944 | tf_op jit(solution)/shard_map/ppermute | solution.py:762
  101.9 24.0 %collective-permute-start.35 = (bf16[2,592,384]{2,1,0:T(8,128)(2,1)S(1)}, bf16[2,592,384]{2,1,0:T(8,128)(2,1)S(1)}, u32[]{:S(2)}, u32[]{:S(2)}) collective-permute-start(bf16[2,592,384]{2,1,0:T(8,128)(2,1)S(1)} %get-tuple-element.37), channel_id=1, source_target_pairs={{0,2},{16,17},{1,3},{17,16},{2,0},{18,19},{3,1},{19,18},{4,6},{20,... | collective-permute-start | bytes 2727944 | tf_op jit(solution)/shard_map/ppermute | solution.py:762
  111.4 13.4 %collective-permute-start.37 = (bf16[592,384]{1,0:T(8,128)(2,1)S(1)}, bf16[592,384]{1,0:T(8,128)(2,1)S(1)}, u32[]{:S(2)}, u32[]{:S(2)}) collective-permute-start(bf16[592,384]{1,0:T(8,128)(2,1)S(1)} %fusion.6), channel_id=1, source_target_pairs={{0,1},{16,18},{1,0},{17,19},{2,3},{18,16},{3,2},{19,17},{4,5},{20,... | collective-permute-start | bytes 1363976 | tf_op jit(solution)/shard_map/ppermute | solution.py:766
  115.5 25.0 %collective-permute-start.34 = (bf16[2,592,384]{2,1,0:T(8,128)(2,1)S(1)}, bf16[2,592,384]{2,1,0:T(8,128)(2,1)S(1)}, u32[]{:S(2)}, u32[]{:S(2)}) collective-permute-start(bf16[2,592,384]{2,1,0:T(8,128)(2,1)S(1)} %get-tuple-element.35), channel_id=1, source_target_pairs={{0,2},{16,17},{1,3},{17,16},{2,0},{18,19},{3,1},{19,18},{4,6},{20,... | collective-permute-start | bytes 2727944 | tf_op jit(solution)/shard_map/ppermute | solution.py:762
  126.0 13.4 %collective-permute-start.38 = (bf16[592,384]{1,0:T(8,128)(2,1)S(1)}, bf16[592,384]{1,0:T(8,128)(2,1)S(1)}, u32[]{:S(2)}, u32[]{:S(2)}) collective-permute-start(bf16[592,384]{1,0:T(8,128)(2,1)S(1)} %fusion.7), channel_id=1, source_target_pairs={{0,1},{16,18},{1,0},{17,19},{2,3},{18,16},{3,2},{19,17},{4,5},{20,... | collective-permute-start | bytes 1363976 | tf_op jit(solution)/shard_map/ppermute | solution.py:766
  127.6 12.5 %collective-permute-start.39 = (bf16[592,384]{1,0:T(8,128)(2,1)S(1)}, bf16[592,384]{1,0:T(8,128)(2,1)S(1)}, u32[]{:S(2)}, u32[]{:S(2)}) collective-permute-start(bf16[592,384]{1,0:T(8,128)(2,1)S(1)} %fusion.5), channel_id=1, source_target_pairs={{0,12},{1,13},{2,14},{3,15},{4,0},{5,1},{6,2},{7,3},{8,4},{9,5},{1... | collective-permute-start | bytes 1363976 | tf_op jit(solution)/shard_map/ppermute | solution.py:772
  140.6 19.8 %collective-permute-start.40 = (bf16[2,592,384]{2,1,0:T(8,128)(2,1)S(1)}, bf16[2,592,384]{2,1,0:T(8,128)(2,1)S(1)}, u32[]{:S(2)}, u32[]{:S(2)}) collective-permute-start(bf16[2,592,384]{2,1,0:T(8,128)(2,1)S(1)} %get-tuple-element.42), channel_id=1, source_target_pairs={{0,2},{16,17},{1,3},{17,16},{2,0},{18,19},{3,1},{19,18},{4,6},{20,... | collective-permute-start | bytes 2727944 | tf_op jit(solution)/shard_map/ppermute | solution.py:762
  142.3 13.4 %collective-permute-start.41 = (bf16[592,384]{1,0:T(8,128)(2,1)S(1)}, bf16[592,384]{1,0:T(8,128)(2,1)S(1)}, u32[]{:S(2)}, u32[]{:S(2)}) collective-permute-start(bf16[592,384]{1,0:T(8,128)(2,1)S(1)} %fusion.8), channel_id=1, source_target_pairs={{0,1},{16,18},{1,0},{17,19},{2,3},{18,16},{3,2},{19,17},{4,5},{20,... | collective-permute-start | bytes 1363976 | tf_op jit(solution)/shard_map/ppermute | solution.py:766
  143.8 12.1 %collective-permute-start.42 = (bf16[592,384]{1,0:T(8,128)(2,1)S(1)}, bf16[592,384]{1,0:T(8,128)(2,1)S(1)}, u32[]{:S(2)}, u32[]{:S(2)}) collective-permute-start(bf16[592,384]{1,0:T(8,128)(2,1)S(1)} %fusion.4), channel_id=1, source_target_pairs={{0,12},{1,13},{2,14},{3,15},{4,0},{5,1},{6,2},{7,3},{8,4},{9,5},{1... | collective-permute-start | bytes 1363976 | tf_op jit(solution)/shard_map/ppermute | solution.py:772
  (40 other events, 454.0 us)

commit v7 on v6

--- a/solution.py
+++ b/solution.py
@@ -573,7 +573,7 @@
             pltpu.SemaphoreType.DMA((2, 16)),
             pltpu.SemaphoreType.DMA((2, 16)),
         ],
-        compiler_params=pltpu.CompilerParams(vmem_limit_bytes=42 * MIB),
+        compiler_params=pltpu.CompilerParams(vmem_limit_bytes=35 * MIB),
     )(lengths, tokens, cotangent, *frames)
     return out
 

time: 176 us -> 176 us (level)
  no operation moved by 1% of the time
where the time goes in v7:
time: 176 us; the launch traced here: 175 us
  waiting for transfers between devices  92.1 us (52%)
  starting transfers between devices  45.6 us (26%)
  Pallas kernels  33.4 us (19%)
    ppermute x3, waiting for transfers between devices, on_device_planes(): zero = own if t == 0 else lax.ppermute(zero, 'shard', up)  28.4 us
    ppermute x4, waiting for transfers between devices, on_device_planes(): from_near = lax.ppermute(away, both, near)  23.1 us
    pallas_call x1, Pallas kernels, run_layer(): pl.pallas_call(layer_kernel, out_shape=[thin, thin, pltpu.VMEM((rows, LEF...  18.4 us
    ppermute x3, starting transfers between devices, on_device_planes(): passed = lax.ppermute(leaving, 'shard', down)  10.7 us
    pallas_call x4, Pallas kernels, quad_grads(): pl.pallas_call(functools.partial(grad_kernel, slot), out_shape=[frames, f...  10.2 us
    ppermute x4, waiting for transfers between devices, on_device_planes(): from_far = lax.ppermute(high, both, far)  10.1 us
    ppermute x4, waiting for transfers between devices, on_device_planes(): three = lax.ppermute(one, both, far)  8.95 us
    ppermute x3, waiting for transfers between devices, on_device_planes(): passed = lax.ppermute(leaving, 'shard', down)  7.72 us
  transfers between devices with their start and end apart: 46, of which 23 were waited for; matrix products, arithmetic and copies ran while one was open for 1% of the time, Pallas kernels for 4%

profile of v7, /device:TPU:0, one launch (start us, length us, event | category | flops | bytes accessed | tf_op | source)
XLA Modules:
  0.0 175.4 jit_solution(17383674415042842180)
XLA Ops:
  2.6 3.1 %collective-permute-start.3 = (bf16[592,384]{1,0:T(8,128)(2,1)S(1)}, bf16[592,384]{1,0:T(8,128)(2,1)S(1)}, u32[]{:S(2)}, u32[]{:S(2)}) collective-permute-start(bf16[592,384]{1,0:T(8,128)(2,1)S(1)} %shard_map.109.refs_0_), channel_id=1, source_target_pairs={{0,4},{1,5},{2,6},{3,7},{4,8},{5,9},{6,10},{7,11},{8,12},{9,13},{1... | collective-permute-start | bytes 1363976 | tf_op jit(solution)/shard_map/ppermute | solution.py:738
  8.7 9.4 %collective-permute-done.3.refs_4_ = bf16[592,384]{1,0:T(8,128)(2,1)S(1)} collective-permute-done((bf16[592,384]{1,0:T(8,128)(2,1)S(1)}, bf16[592,384]{1,0:T(8,128)(2,1)S(1)}, u32[]{:S(2)}, u32[]{:S(2)}) %collective-permute-start.3) | collective-permute-done | bytes 454688 | tf_op jit(solution)/shard_map/ppermute | solution.py:738
  21.7 9.8 %collective-permute-done.7.refs_8_ = bf16[592,384]{1,0:T(8,128)(2,1)S(1)} collective-permute-done((bf16[592,384]{1,0:T(8,128)(2,1)S(1)}, bf16[592,384]{1,0:T(8,128)(2,1)S(1)}, u32[]{:S(2)}, u32[]{:S(2)}) %collective-permute-start.7) | collective-permute-done | bytes 454688 | tf_op jit(solution)/shard_map/ppermute | solution.py:738
  37.2 9.1 %collective-permute-done.11.refs_12_ = bf16[592,384]{1,0:T(8,128)(2,1)S(1)} collective-permute-done((bf16[592,384]{1,0:T(8,128)(2,1)S(1)}, bf16[592,384]{1,0:T(8,128)(2,1)S(1)}, u32[]{:S(2)}, u32[]{:S(2)}) %collective-permute-start.11) | collective-permute-done | bytes 454688 | tf_op jit(solution)/shard_map/ppermute | solution.py:738
  52.9 4.6 %collective-permute-done.12.refs_13_ = bf16[592,384]{1,0:T(8,128)(2,1)S(1)} collective-permute-done((bf16[592,384]{1,0:T(8,128)(2,1)S(1)}, bf16[592,384]{1,0:T(8,128)(2,1)S(1)}, u32[]{:S(2)}, u32[]{:S(2)}) %collective-permute-start.12) | collective-permute-done | bytes 454688 | tf_op jit(solution)/shard_map/ppermute | solution.py:739
  57.5 2.4 %collective-permute-done.13.refs_14_ = bf16[592,384]{1,0:T(8,128)(2,1)S(1)} collective-permute-done((bf16[592,384]{1,0:T(8,128)(2,1)S(1)}, bf16[592,384]{1,0:T(8,128)(2,1)S(1)}, u32[]{:S(2)}, u32[]{:S(2)}) %collective-permute-start.13) | collective-permute-done | bytes 454688 | tf_op jit(solution)/shard_map/ppermute | solution.py:740
  61.5 3.3 %collective-permute-done.10.refs_11_ = bf16[592,384]{1,0:T(8,128)(2,1)S(1)} collective-permute-done((bf16[592,384]{1,0:T(8,128)(2,1)S(1)}, bf16[592,384]{1,0:T(8,128)(2,1)S(1)}, u32[]{:S(2)}, u32[]{:S(2)}) %collective-permute-start.10) | collective-permute-done | bytes 454688 | tf_op jit(solution)/shard_map/ppermute | solution.py:741
  66.2 3.4 %collective-permute-done.14.refs_15_ = bf16[592,384]{1,0:T(8,128)(2,1)S(1)} collective-permute-done((bf16[592,384]{1,0:T(8,128)(2,1)S(1)}, bf16[592,384]{1,0:T(8,128)(2,1)S(1)}, u32[]{:S(2)}, u32[]{:S(2)}) %collective-permute-start.14) | collective-permute-done | bytes 454688 | tf_op jit(solution)/shard_map/ppermute | solution.py:741
  71.7 18.4 %shard_map.110 = (bf16[128,768]{1,0:T(8,128)(2,1)}, bf16[128,768]{1,0:T(8,128)(2,1)}, bf16[128,8064]{1,0:T(8,128)(2,1)S(1)}, bf16[128,3456]{1,0:T(8,128)(2,1)S(1)}, f32[16,768]{1,0:T(8,128)S(1)}) custom-call(s32[1]{0:T(128)S(6)} %copy.12.length_ref, bf16[128,768]{1,0:T(8,128)(2,1)S(1)} %copy-done.2, bf16[128,768]{1,0:T(8,128)(2,1)S(1)} %copy-done.5, ...), custom_call_target="tpu_custom_call" | custom-call | tf_op jit(solution)/shard_map/pallas_call | solution.py:552
  91.1 3.5 %collective-permute-done.31.tokens_other = bf16[128,768]{1,0:T(8,128)(2,1)S(1)} collective-permute-done((bf16[128,768]{1,0:T(8,128)(2,1)S(1)}, bf16[128,768]{1,0:T(8,128)(2,1)S(1)}, u32[]{:S(2)}, u32[]{:S(2)}) %collective-permute-start.31) | collective-permute-done | bytes 196640 | tf_op jit(solution)/shard_map/ppermute | solution.py:750
  94.7 2.6 %shard_map.114 = (bf16[2,592,384]{2,1,0:T(8,128)(2,1)S(1)}, bf16[2,592,384]{2,1,0:T(8,128)(2,1)S(1)}) custom-call(bf16[128,768]{1,0:T(8,128)(2,1)S(1)} %copy-done.2, bf16[128,768]{1,0:T(8,128)(2,1)S(1)} %collective-permute-done.31.tokens_other, bf16[128,8064]{1,0:T(8,128)(2,1)S(1)} %get-tuple-element.29.left_ref, ...), custom_call_target="tpu_custom_call" | custom-call | flops 1000 | bytes 1000 | tf_op jit(solution)/shard_map/pallas_call | solution.py:701
  99.0 2.3 %shard_map.113 = (bf16[2,592,384]{2,1,0:T(8,128)(2,1)S(1)}, bf16[2,592,384]{2,1,0:T(8,128)(2,1)S(1)}) custom-call(bf16[128,768]{1,0:T(8,128)(2,1)S(1)} %copy-done.2, bf16[128,768]{1,0:T(8,128)(2,1)S(1)} %collective-permute-done.31.tokens_other, bf16[128,8064]{1,0:T(8,128)(2,1)S(1)} %get-tuple-element.29.left_ref, ...), custom_call_target="tpu_custom_call" | custom-call | flops 1000 | bytes 1000 | tf_op jit(solution)/shard_map/pallas_call | solution.py:701
  101.8 8.9 %collective-permute-done.36 = bf16[2,592,384]{2,1,0:T(8,128)(2,1)S(1)} collective-permute-done((bf16[2,592,384]{2,1,0:T(8,128)(2,1)S(1)}, bf16[2,592,384]{2,1,0:T(8,128)(2,1)S(1)}, u32[]{:S(2)}, u32[]{:S(2)}) %collective-permute-start.36) | collective-permute-done | bytes 909344 | tf_op jit(solution)/shard_map/ppermute | solution.py:762
  112.4 2.5 %shard_map.112 = (bf16[2,592,384]{2,1,0:T(8,128)(2,1)S(1)}, bf16[2,592,384]{2,1,0:T(8,128)(2,1)S(1)}) custom-call(bf16[128,768]{1,0:T(8,128)(2,1)S(1)} %copy-done.2, bf16[128,768]{1,0:T(8,128)(2,1)S(1)} %collective-permute-done.31.tokens_other, bf16[128,8064]{1,0:T(8,128)(2,1)S(1)} %get-tuple-element.29.left_ref, ...), custom_call_target="tpu_custom_call" | custom-call | flops 1000 | bytes 1000 | tf_op jit(solution)/shard_map/pallas_call | solution.py:701
  116.6 7.7 %collective-permute-done.37 = bf16[592,384]{1,0:T(8,128)(2,1)S(1)} collective-permute-done((bf16[592,384]{1,0:T(8,128)(2,1)S(1)}, bf16[592,384]{1,0:T(8,128)(2,1)S(1)}, u32[]{:S(2)}, u32[]{:S(2)}) %collective-permute-start.37) | collective-permute-done | bytes 454688 | tf_op jit(solution)/shard_map/ppermute | solution.py:766
  127.0 3.2 %collective-permute-start.39 = (bf16[592,384]{1,0:T(8,128)(2,1)S(1)}, bf16[592,384]{1,0:T(8,128)(2,1)S(1)}, u32[]{:S(2)}, u32[]{:S(2)}) collective-permute-start(bf16[592,384]{1,0:T(8,128)(2,1)S(1)} %fusion.5), channel_id=1, source_target_pairs={{0,12},{1,13},{2,14},{3,15},{4,0},{5,1},{6,2},{7,3},{8,4},{9,5},{1... | collective-permute-start | bytes 1363976 | tf_op jit(solution)/shard_map/ppermute | solution.py:772
  130.2 2.7 %shard_map.111 = (bf16[2,592,384]{2,1,0:T(8,128)(2,1)S(1)}, bf16[2,592,384]{2,1,0:T(8,128)(2,1)S(1)}) custom-call(bf16[128,768]{1,0:T(8,128)(2,1)S(1)} %copy-done.2, bf16[128,768]{1,0:T(8,128)(2,1)S(1)} %collective-permute-done.31.tokens_other, bf16[128,8064]{1,0:T(8,128)(2,1)S(1)} %get-tuple-element.29.left_ref, ...), custom_call_target="tpu_custom_call" | custom-call | flops 1000 | bytes 1000 | tf_op jit(solution)/shard_map/pallas_call | solution.py:701
  133.0 5.9 %collective-permute-done.38 = bf16[592,384]{1,0:T(8,128)(2,1)S(1)} collective-permute-done((bf16[592,384]{1,0:T(8,128)(2,1)S(1)}, bf16[592,384]{1,0:T(8,128)(2,1)S(1)}, u32[]{:S(2)}, u32[]{:S(2)}) %collective-permute-start.38) | collective-permute-done | bytes 454688 | tf_op jit(solution)/shard_map/ppermute | solution.py:766
  143.2 3.2 %collective-permute-start.42 = (bf16[592,384]{1,0:T(8,128)(2,1)S(1)}, bf16[592,384]{1,0:T(8,128)(2,1)S(1)}, u32[]{:S(2)}, u32[]{:S(2)}) collective-permute-start(bf16[592,384]{1,0:T(8,128)(2,1)S(1)} %fusion.4), channel_id=1, source_target_pairs={{0,12},{1,13},{2,14},{3,15},{4,0},{5,1},{6,2},{7,3},{8,4},{9,5},{1... | collective-permute-start | bytes 1363976 | tf_op jit(solution)/shard_map/ppermute | solution.py:772
  146.4 8.7 %collective-permute-done.41 = bf16[592,384]{1,0:T(8,128)(2,1)S(1)} collective-permute-done((bf16[592,384]{1,0:T(8,128)(2,1)S(1)}, bf16[592,384]{1,0:T(8,128)(2,1)S(1)}, u32[]{:S(2)}, u32[]{:S(2)}) %collective-permute-start.41) | collective-permute-done | bytes 454688 | tf_op jit(solution)/shard_map/ppermute | solution.py:766
  155.4 4.3 %collective-permute-start.44 = (bf16[592,384]{1,0:T(8,128)(2,1)S(1)}, bf16[592,384]{1,0:T(8,128)(2,1)S(1)}, u32[]{:S(2)}, u32[]{:S(2)}) collective-permute-start(bf16[592,384]{1,0:T(8,128)(2,1)S(1)} %fusion.2), channel_id=1, source_target_pairs={{0,12},{1,13},{2,14},{3,15},{4,0},{5,1},{6,2},{7,3},{8,4},{9,5},{1... | collective-permute-start | bytes 1363976 | tf_op jit(solution)/shard_map/ppermute | solution.py:772
  160.5 7.2 %collective-permute-done.44 = bf16[592,384]{1,0:T(8,128)(2,1)S(1)} collective-permute-done((bf16[592,384]{1,0:T(8,128)(2,1)S(1)}, bf16[592,384]{1,0:T(8,128)(2,1)S(1)}, u32[]{:S(2)}, u32[]{:S(2)}) %collective-permute-start.44) | collective-permute-done | bytes 454688 | tf_op jit(solution)/shard_map/ppermute | solution.py:772
  168.7 2.4 %collective-permute-done.45.other_ref = f32[592,384]{1,0:T(8,128)S(1)} collective-permute-done((f32[592,384]{1,0:T(8,128)S(1)}, f32[592,384]{1,0:T(8,128)S(1)}, u32[]{:S(2)}, u32[]{:S(2)}) %collective-permute-start.45) | collective-permute-done | bytes 909344 | tf_op jit(solution)/shard_map/ppermute | solution.py:774
  171.1 4.3 %shard_map.115 = (f32[442944]{0:T(1024)}, f32[442944]{0:T(1024)}, f32[442944]{0:T(1024)}, f32[442944]{0:T(1024)}) custom-call(f32[592,384]{1,0:T(8,128)S(1)} %fusion.mine_ref, f32[592,384]{1,0:T(8,128)S(1)} %collective-permute-done.45.other_ref, f32[442944]{0:T(1024)S(1)} %copy-done.1, f32[442944]{0:T(1024)S(1)} %copy-done.3, f32[442944]{0:T(1024)S(1)} %copy-done.4), custom_call_target="tpu_custom_call" | custom-call | tf_op jit(solution)/shard_map/pallas_call | solution.py:327
  (95 shorter events, 40.8 us)
Async XLA Ops:
  2.6 15.5 %collective-permute-start.3 = (bf16[592,384]{1,0:T(8,128)(2,1)S(1)}, bf16[592,384]{1,0:T(8,128)(2,1)S(1)}, u32[]{:S(2)}, u32[]{:S(2)}) collective-permute-start(bf16[592,384]{1,0:T(8,128)(2,1)S(1)} %shard_map.109.refs_0_), channel_id=1, source_target_pairs={{0,4},{1,5},{2,6},{3,7},{4,8},{5,9},{6,10},{7,11},{8,12},{9,13},{1... | collective-permute-start | bytes 1363976 | tf_op jit(solution)/shard_map/ppermute | solution.py:738
  5.7 14.0 %collective-permute-start = (bf16[592,384]{1,0:T(8,128)(2,1)S(1)}, bf16[592,384]{1,0:T(8,128)(2,1)S(1)}, u32[]{:S(2)}, u32[]{:S(2)}) collective-permute-start(bf16[592,384]{1,0:T(8,128)(2,1)S(1)} %shard_map.109.refs_0_), channel_id=1, source_target_pairs={{0,1},{16,18},{1,0},{17,19},{2,3},{18,16},{3,2},{19,17},{4,5},{20,... | collective-permute-start | bytes 1363976 | tf_op jit(solution)/shard_map/ppermute | solution.py:739
  7.2 14.0 %collective-permute-start.1 = (bf16[592,384]{1,0:T(8,128)(2,1)S(1)}, bf16[592,384]{1,0:T(8,128)(2,1)S(1)}, u32[]{:S(2)}, u32[]{:S(2)}) collective-permute-start(bf16[592,384]{1,0:T(8,128)(2,1)S(1)} %shard_map.109.refs_0_), channel_id=1, source_target_pairs={{0,2},{16,17},{1,3},{17,16},{2,0},{18,19},{3,1},{19,18},{4,6},{20,... | collective-permute-start | bytes 1363976 | tf_op jit(solution)/shard_map/ppermute | solution.py:740
  8.7 12.5 %collective-permute-start.15 = (bf16[592,384]{1,0:T(8,128)(2,1)S(1)}, bf16[592,384]{1,0:T(8,128)(2,1)S(1)}, u32[]{:S(2)}, u32[]{:S(2)}) collective-permute-start(bf16[592,384]{1,0:T(8,128)(2,1)S(1)} %shard_map.109.refs_0_), channel_id=1, source_target_pairs={{0,16},{16,0},{1,17},{17,1},{2,18},{18,2},{3,19},{19,3},{4,20},{20... | collective-permute-start | bytes 1363976 | tf_op jit(solution)/shard_map/ppermute | solution.py:744
  18.1 13.4 %collective-permute-start.7 = (bf16[592,384]{1,0:T(8,128)(2,1)S(1)}, bf16[592,384]{1,0:T(8,128)(2,1)S(1)}, u32[]{:S(2)}, u32[]{:S(2)}) collective-permute-start(bf16[592,384]{1,0:T(8,128)(2,1)S(1)} %collective-permute-done.3.refs_4_), channel_id=1, source_target_pairs={{0,4},{1,5},{2,6},{3,7},{4,8},{5,9},{6,10},{7,11},{8,12},{9,13},{1... | collective-permute-start | bytes 1363976 | tf_op jit(solution)/shard_map/ppermute | solution.py:738
  18.1 13.4 %collective-permute-start.4 = (bf16[592,384]{1,0:T(8,128)(2,1)S(1)}, bf16[592,384]{1,0:T(8,128)(2,1)S(1)}, u32[]{:S(2)}, u32[]{:S(2)}) collective-permute-start(bf16[592,384]{1,0:T(8,128)(2,1)S(1)} %collective-permute-done.3.refs_4_), channel_id=1, source_target_pairs={{0,1},{16,18},{1,0},{17,19},{2,3},{18,16},{3,2},{19,17},{4,5},{20,... | collective-permute-start | bytes 1363976 | tf_op jit(solution)/shard_map/ppermute | solution.py:739
  19.6 12.4 %collective-permute-start.5 = (bf16[592,384]{1,0:T(8,128)(2,1)S(1)}, bf16[592,384]{1,0:T(8,128)(2,1)S(1)}, u32[]{:S(2)}, u32[]{:S(2)}) collective-permute-start(bf16[592,384]{1,0:T(8,128)(2,1)S(1)} %collective-permute-done.3.refs_4_), channel_id=1, source_target_pairs={{0,2},{16,17},{1,3},{17,16},{2,0},{18,19},{3,1},{19,18},{4,6},{20,... | collective-permute-start | bytes 1363976 | tf_op jit(solution)/shard_map/ppermute | solution.py:740
  21.1 13.5 %collective-permute-start.2 = (bf16[592,384]{1,0:T(8,128)(2,1)S(1)}, bf16[592,384]{1,0:T(8,128)(2,1)S(1)}, u32[]{:S(2)}, u32[]{:S(2)}) collective-permute-start(bf16[592,384]{1,0:T(8,128)(2,1)S(1)} %collective-permute-done.refs_1_), channel_id=1, source_target_pairs={{0,2},{16,17},{1,3},{17,16},{2,0},{18,19},{3,1},{19,18},{4,6},{20,... | collective-permute-start | bytes 1363976 | tf_op jit(solution)/shard_map/ppermute | solution.py:741
  32.0 14.3 %collective-permute-start.11 = (bf16[592,384]{1,0:T(8,128)(2,1)S(1)}, bf16[592,384]{1,0:T(8,128)(2,1)S(1)}, u32[]{:S(2)}, u32[]{:S(2)}) collective-permute-start(bf16[592,384]{1,0:T(8,128)(2,1)S(1)} %collective-permute-done.7.refs_8_), channel_id=1, source_target_pairs={{0,4},{1,5},{2,6},{3,7},{4,8},{5,9},{6,10},{7,11},{8,12},{9,13},{1... | collective-permute-start | bytes 1363976 | tf_op jit(solution)/shard_map/ppermute | solution.py:738
  32.7 13.6 %collective-permute-start.8 = (bf16[592,384]{1,0:T(8,128)(2,1)S(1)}, bf16[592,384]{1,0:T(8,128)(2,1)S(1)}, u32[]{:S(2)}, u32[]{:S(2)}) collective-permute-start(bf16[592,384]{1,0:T(8,128)(2,1)S(1)} %collective-permute-done.7.refs_8_), channel_id=1, source_target_pairs={{0,1},{16,18},{1,0},{17,19},{2,3},{18,16},{3,2},{19,17},{4,5},{20,... | collective-permute-start | bytes 1363976 | tf_op jit(solution)/shard_map/ppermute | solution.py:739
  34.6 12.3 %collective-permute-start.9 = (bf16[592,384]{1,0:T(8,128)(2,1)S(1)}, bf16[592,384]{1,0:T(8,128)(2,1)S(1)}, u32[]{:S(2)}, u32[]{:S(2)}) collective-permute-start(bf16[592,384]{1,0:T(8,128)(2,1)S(1)} %collective-permute-done.7.refs_8_), channel_id=1, source_target_pairs={{0,2},{16,17},{1,3},{17,16},{2,0},{18,19},{3,1},{19,18},{4,6},{20,... | collective-permute-start | bytes 1363976 | tf_op jit(solution)/shard_map/ppermute | solution.py:740
  36.6 13.6 %collective-permute-start.6 = (bf16[592,384]{1,0:T(8,128)(2,1)S(1)}, bf16[592,384]{1,0:T(8,128)(2,1)S(1)}, u32[]{:S(2)}, u32[]{:S(2)}) collective-permute-start(bf16[592,384]{1,0:T(8,128)(2,1)S(1)} %collective-permute-done.4.refs_5_), channel_id=1, source_target_pairs={{0,2},{16,17},{1,3},{17,16},{2,0},{18,19},{3,1},{19,18},{4,6},{20,... | collective-permute-start | bytes 1363976 | tf_op jit(solution)/shard_map/ppermute | solution.py:741
  51.9 12.9 %collective-permute-start.10 = (bf16[592,384]{1,0:T(8,128)(2,1)S(1)}, bf16[592,384]{1,0:T(8,128)(2,1)S(1)}, u32[]{:S(2)}, u32[]{:S(2)}) collective-permute-start(bf16[592,384]{1,0:T(8,128)(2,1)S(1)} %collective-permute-done.8.refs_9_), channel_id=1, source_target_pairs={{0,2},{16,17},{1,3},{17,16},{2,0},{18,19},{3,1},{19,18},{4,6},{20,... | collective-permute-start | bytes 1363976 | tf_op jit(solution)/shard_map/ppermute | solution.py:741
  52.3 13.3 %collective-permute-start.27 = (bf16[592,384]{1,0:T(8,128)(2,1)S(1)}, bf16[592,384]{1,0:T(8,128)(2,1)S(1)}, u32[]{:S(2)}, u32[]{:S(2)}) collective-permute-start(bf16[592,384]{1,0:T(8,128)(2,1)S(1)} %collective-permute-done.11.refs_12_), channel_id=1, source_target_pairs={{0,16},{16,0},{1,17},{17,1},{2,18},{18,2},{3,19},{19,3},{4,20},{20... | collective-permute-start | bytes 1363976 | tf_op jit(solution)/shard_map/ppermute | solution.py:744
  52.8 12.8 %collective-permute-start.24 = (bf16[592,384]{1,0:T(8,128)(2,1)S(1)}, bf16[592,384]{1,0:T(8,128)(2,1)S(1)}, u32[]{:S(2)}, u32[]{:S(2)}) collective-permute-start(bf16[592,384]{1,0:T(8,128)(2,1)S(1)} %collective-permute-done.8.refs_9_), channel_id=1, source_target_pairs={{0,16},{16,0},{1,17},{17,1},{2,18},{18,2},{3,19},{19,3},{4,20},{20... | collective-permute-start | bytes 1363976 | tf_op jit(solution)/shard_map/ppermute | solution.py:744
  97.3 13.4 %collective-permute-start.36 = (bf16[2,592,384]{2,1,0:T(8,128)(2,1)S(1)}, bf16[2,592,384]{2,1,0:T(8,128)(2,1)S(1)}, u32[]{:S(2)}, u32[]{:S(2)}) collective-permute-start(bf16[2,592,384]{2,1,0:T(8,128)(2,1)S(1)} %get-tuple-element.39), channel_id=1, source_target_pairs={{0,2},{16,17},{1,3},{17,16},{2,0},{18,19},{3,1},{19,18},{4,6},{20,... | collective-permute-start | bytes 2727944 | tf_op jit(solution)/shard_map/ppermute | solution.py:762
  101.3 24.0 %collective-permute-start.35 = (bf16[2,592,384]{2,1,0:T(8,128)(2,1)S(1)}, bf16[2,592,384]{2,1,0:T(8,128)(2,1)S(1)}, u32[]{:S(2)}, u32[]{:S(2)}) collective-permute-start(bf16[2,592,384]{2,1,0:T(8,128)(2,1)S(1)} %get-tuple-element.37), channel_id=1, source_target_pairs={{0,2},{16,17},{1,3},{17,16},{2,0},{18,19},{3,1},{19,18},{4,6},{20,... | collective-permute-start | bytes 2727944 | tf_op jit(solution)/shard_map/ppermute | solution.py:762
  110.8 13.4 %collective-permute-start.37 = (bf16[592,384]{1,0:T(8,128)(2,1)S(1)}, bf16[592,384]{1,0:T(8,128)(2,1)S(1)}, u32[]{:S(2)}, u32[]{:S(2)}) collective-permute-start(bf16[592,384]{1,0:T(8,128)(2,1)S(1)} %fusion.6), channel_id=1, source_target_pairs={{0,1},{16,18},{1,0},{17,19},{2,3},{18,16},{3,2},{19,17},{4,5},{20,... | collective-permute-start | bytes 1363976 | tf_op jit(solution)/shard_map/ppermute | solution.py:766
  114.9 25.0 %collective-permute-start.34 = (bf16[2,592,384]{2,1,0:T(8,128)(2,1)S(1)}, bf16[2,592,384]{2,1,0:T(8,128)(2,1)S(1)}, u32[]{:S(2)}, u32[]{:S(2)}) collective-permute-start(bf16[2,592,384]{2,1,0:T(8,128)(2,1)S(1)} %get-tuple-element.35), channel_id=1, source_target_pairs={{0,2},{16,17},{1,3},{17,16},{2,0},{18,19},{3,1},{19,18},{4,6},{20,... | collective-permute-start | bytes 2727944 | tf_op jit(solution)/shard_map/ppermute | solution.py:762
  125.5 13.4 %collective-permute-start.38 = (bf16[592,384]{1,0:T(8,128)(2,1)S(1)}, bf16[592,384]{1,0:T(8,128)(2,1)S(1)}, u32[]{:S(2)}, u32[]{:S(2)}) collective-permute-start(bf16[592,384]{1,0:T(8,128)(2,1)S(1)} %fusion.7), channel_id=1, source_target_pairs={{0,1},{16,18},{1,0},{17,19},{2,3},{18,16},{3,2},{19,17},{4,5},{20,... | collective-permute-start | bytes 1363976 | tf_op jit(solution)/shard_map/ppermute | solution.py:766
  127.0 12.4 %collective-permute-start.39 = (bf16[592,384]{1,0:T(8,128)(2,1)S(1)}, bf16[592,384]{1,0:T(8,128)(2,1)S(1)}, u32[]{:S(2)}, u32[]{:S(2)}) collective-permute-start(bf16[592,384]{1,0:T(8,128)(2,1)S(1)} %fusion.5), channel_id=1, source_target_pairs={{0,12},{1,13},{2,14},{3,15},{4,0},{5,1},{6,2},{7,3},{8,4},{9,5},{1... | collective-permute-start | bytes 1363976 | tf_op jit(solution)/shard_map/ppermute | solution.py:772
  140.1 19.7 %collective-permute-start.40 = (bf16[2,592,384]{2,1,0:T(8,128)(2,1)S(1)}, bf16[2,592,384]{2,1,0:T(8,128)(2,1)S(1)}, u32[]{:S(2)}, u32[]{:S(2)}) collective-permute-start(bf16[2,592,384]{2,1,0:T(8,128)(2,1)S(1)} %get-tuple-element.42), channel_id=1, source_target_pairs={{0,2},{16,17},{1,3},{17,16},{2,0},{18,19},{3,1},{19,18},{4,6},{20,... | collective-permute-start | bytes 2727944 | tf_op jit(solution)/shard_map/ppermute | solution.py:762
  141.7 13.4 %collective-permute-start.41 = (bf16[592,384]{1,0:T(8,128)(2,1)S(1)}, bf16[592,384]{1,0:T(8,128)(2,1)S(1)}, u32[]{:S(2)}, u32[]{:S(2)}) collective-permute-start(bf16[592,384]{1,0:T(8,128)(2,1)S(1)} %fusion.8), channel_id=1, source_target_pairs={{0,1},{16,18},{1,0},{17,19},{2,3},{18,16},{3,2},{19,17},{4,5},{20,... | collective-permute-start | bytes 1363976 | tf_op jit(solution)/shard_map/ppermute | solution.py:766
  155.4 12.2 %collective-permute-start.44 = (bf16[592,384]{1,0:T(8,128)(2,1)S(1)}, bf16[592,384]{1,0:T(8,128)(2,1)S(1)}, u32[]{:S(2)}, u32[]{:S(2)}) collective-permute-start(bf16[592,384]{1,0:T(8,128)(2,1)S(1)} %fusion.2), channel_id=1, source_target_pairs={{0,12},{1,13},{2,14},{3,15},{4,0},{5,1},{6,2},{7,3},{8,4},{9,5},{1... | collective-permute-start | bytes 1363976 | tf_op jit(solution)/shard_map/ppermute | solution.py:772
  (28 other events, 326.4 us)
